TPU v7x, 512 devices: a whole 4x4x16 slice. The times are simulated.
512 devices in a mesh: hid: 32 (over z, core), out: 8 (over y, x_lo), rep: 2 (over x_hi).
Axes of the slice: x: 4 (x_hi: 2, x_lo: 2; x = x_hi * 2 + x_lo), y: 4, z: 16, core: 2. Of those that a mesh axis runs over, the one named last changes fastest.
Arguments:
- x_act: bfloat16 [2, 512, 28672], P('rep', None, 'hid'), may hold values from -6 to 6
- out_grad: bfloat16 [2, 512, 4096], P('rep', None, 'out'), may hold values from -6 to 6
- weight_codes: int32 [4096, 28672], P(('out', 'rep'), 'hid'), may hold values from -127 to 127
- group_exps: int32 [4096, 224], P(('out', 'rep'), 'hid'), may hold values from -13 to -11
- local_factor: bfloat16 [896, 896], P(('out', 'rep')), may hold values from -0.1875 to 0.1875
- first_moment: bfloat16 [4096, 28672], P(('out', 'rep'), 'hid'), may hold values from -6 to 6
- second_moment: bfloat16 [4096, 28672], P(('out', 'rep'), 'hid'), may hold values from 1 to 8
Outputs:
- input_grad: bfloat16 [2, 512, 28672], P('rep', 'out', 'hid')
- weight_step: bfloat16 [4096, 28672], P(('out', 'rep'), 'hid')
- new_first: bfloat16 [4096, 28672], P(('out', 'rep'), 'hid')
- new_second: bfloat16 [4096, 28672], P(('out', 'rep'), 'hid')
All inputs are finite; a program needn't handle non-finite values.
Results may differ from a plain program's by a relative error of at most 0.0049.
Values may be sent and summed in bfloat16 or wider, within the bound.
No kernel may reach another device: no remote copies, remote signals or barrier semaphores. Data moves between devices by JAX's collectives and lax.ppermute only.
A program may use at most 64 MiB of HBM per device.

v0:
```python
import math

import jax
import jax.numpy as jnp
from jax import lax
from jax.sharding import PartitionSpec as P

GROUP = 128


def partner_2(block, axis, distance):
    count = lax.axis_size(axis)
    route = []
    for low in range(count):
        high = low | 1 << distance
        if high != low and high < count:
            route += [(low, high), (high, low)]
    return lax.ppermute(block, axis, route)


def mix_blocks(values):
    dev_count = lax.axis_size("hid")
    my_index = lax.axis_index("hid")
    current = values
    for section_index in range(dev_count.bit_length() - 1):
        partner = partner_2(current, "hid", section_index)
        upper = my_index // 2**section_index % 2
        current = jnp.where(upper == 1, partner - current, current + partner)
    return current / math.sqrt(dev_count)


def shards(x_act, out_grad, weight_codes, group_exps, local_factor, first_moment, second_moment):
    width_all = x_act.shape[2]
    factor = lax.all_gather(local_factor, ("out", "rep"), axis=0, tiled=True)
    tokens = x_act[0]
    grads_out = out_grad[0]
    pre_mix = jnp.dot(tokens, factor, preferred_element_type=jnp.float32)
    x_rot = mix_blocks(pre_mix).astype(jnp.bfloat16)
    code_rows = weight_codes.shape[0]
    scales = jnp.exp2(group_exps.astype(jnp.float32))
    w_deq = (
        weight_codes.astype(jnp.float32).reshape(code_rows, width_all // GROUP, GROUP)
        * scales[:, :, None]
    )
    w_deq = w_deq.reshape(code_rows, width_all).astype(jnp.bfloat16)
    columns = grads_out
    partial_rot = jnp.dot(
        columns,
        lax.all_gather(w_deq, "rep", axis=0, tiled=True),
        preferred_element_type=jnp.float32,
    )
    grad_rot = lax.psum_scatter(partial_rot, "out", scatter_dimension=0, tiled=True).astype(
        jnp.bfloat16
    )
    back_pre = lax.dot_general(
        grad_rot, factor, (((1,), (1,)), ((), ())), preferred_element_type=jnp.float32
    )
    input_grad = mix_blocks(back_pre).astype(jnp.bfloat16)[None]
    columns = grads_out
    weight_grad = lax.psum_scatter(
        lax.dot_general(
            columns, x_rot, (((0,), (0,)), ((), ())), preferred_element_type=jnp.float32
        ).astype(jnp.bfloat16),
        "rep",
        scatter_dimension=0,
        tiled=True,
    ).astype(jnp.float32)
    gradient = jnp.where(jnp.abs(weight_codes) <= 126, weight_grad / 16.0, jnp.float32(0.0))
    moment_one = 0.9 * first_moment.astype(jnp.float32) + 0.1 * gradient
    moment_two = 0.95 * second_moment.astype(jnp.float32) + 0.05 * gradient * gradient
    corr_one = 1.0 - 0.9**20
    corr_two = 1.0 - 0.95**20
    weight_step = moment_one / corr_one / (jnp.sqrt(moment_two / corr_two) + 1e-08)
    return (
        input_grad,
        weight_step.astype(jnp.bfloat16),
        moment_one.astype(jnp.bfloat16),
        moment_two.astype(jnp.bfloat16),
    )


def solution(mesh):
    placed = (
        P("rep", None, "hid"),
        P("rep", None, "out"),
        P(("out", "rep"), "hid"),
        P(("out", "rep"), "hid"),
        P(("out", "rep"), None),
        P(("out", "rep"), "hid"),
        P(("out", "rep"), "hid"),
    )
    return jax.shard_map(
        shards,
        mesh=mesh,
        in_specs=placed,
        out_specs=(
            P("rep", "out", "hid"),
            P(("out", "rep"), "hid"),
            P(("out", "rep"), "hid"),
            P(("out", "rep"), "hid"),
        ),
        check_vma=False,
    )
```

profile of v0, /device:TPU:1, one launch (start us, length us, event | category | flops | bytes accessed | tf_op | source)
XLA Modules:
  0.0 774.2 jit_solution(17935834629481688833)
XLA Ops:
  8.0 82.7 %all-gather.2.cloned.1.call-done = bf16[896,896]{1,0:T(8,128)(2,1)} async-done(((bf16[56,896]{1,0:T(8,128)(2,1)}), bf16[896,896]{1,0:T(8,128)(2,1)}) %all-gather.2.cloned.1.call-update) | async-done | bytes 1605648 | tf_op jit(solution)/shard_map/all_gather | solution.py:34
  93.3 12.6 %collective-permute-start.5 = (f32[512,896]{1,0:T(8,128)S(1)}, f32[512,896]{1,0:T(8,128)}, u32[]{:S(2)}, u32[]{:S(2)}) collective-permute-start(f32[512,896]{1,0:T(8,128)S(1)} %fusion.2), channel_id=1, source_target_pairs={{0,16},{16,0},{32,48},{48,32},{64,80},{80,64},{96,112},{112,96},{1... | collective-permute-start | bytes 5505032 | tf_op jit(solution)/shard_map/ppermute | solution.py:18
  105.9 3.5 collective-permute-done.5
  111.6 2.7 collective-permute-start.6
  114.4 40.5 %collective-permute-done.6 = f32[512,896]{1,0:T(8,128)} collective-permute-done((f32[512,896]{1,0:T(8,128)S(1)}, f32[512,896]{1,0:T(8,128)}, u32[]{:S(2)}, u32[]{:S(2)}) %collective-permute-start.6) | collective-permute-done | bytes 1835040 | tf_op jit(solution)/shard_map/ppermute | solution.py:18
  157.1 3.5 collective-permute-start.7
  160.7 80.1 %collective-permute-done.7 = f32[512,896]{1,0:T(8,128)} collective-permute-done((f32[512,896]{1,0:T(8,128)S(1)}, f32[512,896]{1,0:T(8,128)}, u32[]{:S(2)}, u32[]{:S(2)}) %collective-permute-start.7) | collective-permute-done | bytes 1835040 | tf_op jit(solution)/shard_map/ppermute | solution.py:18
  243.0 6.2 collective-permute-start.8
  249.3 198.3 %collective-permute-done.8 = f32[512,896]{1,0:T(8,128)} collective-permute-done((f32[512,896]{1,0:T(8,128)S(1)}, f32[512,896]{1,0:T(8,128)}, u32[]{:S(2)}, u32[]{:S(2)}) %collective-permute-start.8) | collective-permute-done | bytes 1835040 | tf_op jit(solution)/shard_map/ppermute | solution.py:18
  449.9 10.3 %collective-permute-start.9 = (f32[512,896]{1,0:T(8,128)S(1)}, f32[512,896]{1,0:T(8,128)}, u32[]{:S(2)}, u32[]{:S(2)}) collective-permute-start(f32[512,896]{1,0:T(8,128)S(1)} %add_select_fusion), channel_id=1, source_target_pairs={{0,256},{256,0},{16,272},{272,16},{32,288},{288,32},{48,304},{304,... | collective-permute-start | bytes 5505032 | tf_op jit(solution)/shard_map/ppermute | solution.py:18
  460.2 72.9 %collective-permute-done.9 = f32[512,896]{1,0:T(8,128)} collective-permute-done((f32[512,896]{1,0:T(8,128)S(1)}, f32[512,896]{1,0:T(8,128)}, u32[]{:S(2)}, u32[]{:S(2)}) %collective-permute-start.9) | collective-permute-done | bytes 1835040 | tf_op jit(solution)/shard_map/ppermute | solution.py:18
  533.1 3.1 fusion
  538.0 65.4 %reduce-scatter.5.cloned.1.call-done = bf16[256,896]{0,1:T(8,128)(2,1)} async-done(((bf16[512,896]{0,1:T(8,128)(2,1)}), bf16[256,896]{0,1:T(8,128)(2,1)}) %reduce-scatter.5.cloned.1.call-update) | async-done | bytes 458768 | tf_op jit(solution)/shard_map/reduce_scatter | solution.py:60
  605.7 13.4 %all_gather.6 = bf16[512,896]{0,1:T(8,128)(2,1)S(1)} all-gather(bf16[256,896]{0,1:T(8,128)(2,1)S(1)} %get-tuple-element.20), channel_id=1, replica_groups=mesh['hid'=32,'out'=8,'rep'=2] {'rep'}, dimensions={0}, use_global_device_ids=true | all-gather | bytes 1376256 | tf_op jit(solution)/shard_map/all_gather | solution.py:49
  621.5 55.4 %reduce-scatter.7.cloned.1.call-done = f32[64,896]{1,0:T(8,128)} async-done(((f32[512,896]{1,0:T(8,128)}), f32[64,896]{1,0:T(8,128)}) %reduce-scatter.7.cloned.1.call-update) | async-done | bytes 229392
  678.7 3.4 collective-permute-start
  683.2 3.2 collective-permute-start.1
  686.4 5.5 collective-permute-done.1
  691.9 4.2 collective-permute-start.2
  696.1 10.1 %collective-permute-done.2 = f32[64,896]{1,0:T(8,128)S(1)} collective-permute-done((f32[64,896]{1,0:T(8,128)S(1)}, f32[64,896]{1,0:T(8,128)S(1)}, u32[]{:S(2)}, u32[]{:S(2)}) %collective-permute-start.2) | collective-permute-done | bytes 229408 | tf_op jit(solution)/shard_map/ppermute | solution.py:18
  706.2 7.3 collective-permute-start.3
  713.8 19.6 %collective-permute-done.3 = f32[64,896]{1,0:T(8,128)S(1)} collective-permute-done((f32[64,896]{1,0:T(8,128)S(1)}, f32[64,896]{1,0:T(8,128)S(1)}, u32[]{:S(2)}, u32[]{:S(2)}) %collective-permute-start.3) | collective-permute-done | bytes 229408 | tf_op jit(solution)/shard_map/ppermute | solution.py:18
  734.0 11.1 %collective-permute-start.4 = (f32[64,896]{1,0:T(8,128)}, f32[64,896]{1,0:T(8,128)}, u32[]{:S(2)}, u32[]{:S(2)}) collective-permute-start(f32[64,896]{1,0:T(8,128)} %add_select_fusion.4), channel_id=1, source_target_pairs={{0,256},{256,0},{16,272},{272,16},{32,288},{288,32},{48,304},{304,... | collective-permute-start | bytes 688136 | tf_op jit(solution)/shard_map/ppermute | solution.py:18
  749.0 16.9 %collective-permute-done.4 = f32[64,896]{1,0:T(8,128)} collective-permute-done((f32[64,896]{1,0:T(8,128)}, f32[64,896]{1,0:T(8,128)}, u32[]{:S(2)}, u32[]{:S(2)}) %collective-permute-start.4) | collective-permute-done | bytes 229408 | tf_op jit(solution)/shard_map/ppermute | solution.py:18
  (56 shorter events, 28.2 us)
Async XLA Ops:
  7.2 83.5 %copy-start = (bf16[1,512,896]{2,1,0:T(8,128)(2,1)S(1)}, bf16[1,512,896]{2,1,0:T(8,128)(2,1)}, u32[]{:S(2)}) copy-start(bf16[1,512,896]{2,1,0:T(8,128)(2,1)} %param.7) | copy-start | bytes 2752516
  7.2 83.5 %all-gather.2.cloned.1.call-start = ((), (), s32[]{:S(2)}) async-start(), calls=%async_computation.2 | async-start | bytes 1705984 | tf_op jit(solution)/shard_map/all_gather | solution.py:34
  7.9 595.4 %reduce-scatter.5.cloned.1.call-start = ((), (), s32[]{:S(2)}) async-start(), calls=%async_computation.3 | async-start | bytes 1376256 | tf_op jit(solution)/shard_map/reduce_scatter | solution.py:60
  93.3 12.6 %copy-start.6 = (f32[512,896]{1,0:T(8,128)}, f32[512,896]{1,0:T(8,128)S(1)}, u32[]{:S(2)}) copy-start(f32[512,896]{1,0:T(8,128)S(1)} %fusion.2) | copy-start | bytes 5505028
  93.3 16.1 %collective-permute-start.5 = (f32[512,896]{1,0:T(8,128)S(1)}, f32[512,896]{1,0:T(8,128)}, u32[]{:S(2)}, u32[]{:S(2)}) collective-permute-start(f32[512,896]{1,0:T(8,128)S(1)} %fusion.2), channel_id=1, source_target_pairs={{0,16},{16,0},{32,48},{48,32},{64,80},{80,64},{96,112},{112,96},{1... | collective-permute-start | bytes 5505032 | tf_op jit(solution)/shard_map/ppermute | solution.py:18
  111.6 2.7 copy-start.3
  111.6 43.2 %collective-permute-start.6 = (f32[512,896]{1,0:T(8,128)S(1)}, f32[512,896]{1,0:T(8,128)}, u32[]{:S(2)}, u32[]{:S(2)}) collective-permute-start(f32[512,896]{1,0:T(8,128)S(1)} %add_select_fusion.3), channel_id=1, source_target_pairs={{0,32},{32,0},{16,48},{48,16},{64,96},{96,64},{80,112},{112,80},{1... | collective-permute-start | bytes 5505032 | tf_op jit(solution)/shard_map/ppermute | solution.py:18
  157.1 3.6 copy-start.2
  157.1 83.7 %collective-permute-start.7 = (f32[512,896]{1,0:T(8,128)S(1)}, f32[512,896]{1,0:T(8,128)}, u32[]{:S(2)}, u32[]{:S(2)}) collective-permute-start(f32[512,896]{1,0:T(8,128)S(1)} %add_select_fusion.2), channel_id=1, source_target_pairs={{0,64},{64,0},{16,80},{80,16},{32,96},{96,32},{48,112},{112,48},{1... | collective-permute-start | bytes 5505032 | tf_op jit(solution)/shard_map/ppermute | solution.py:18
  243.0 6.3 copy-start.1
  243.0 204.6 %collective-permute-start.8 = (f32[512,896]{1,0:T(8,128)S(1)}, f32[512,896]{1,0:T(8,128)}, u32[]{:S(2)}, u32[]{:S(2)}) collective-permute-start(f32[512,896]{1,0:T(8,128)S(1)} %add_select_fusion.1), channel_id=1, source_target_pairs={{0,128},{128,0},{16,144},{144,16},{32,160},{160,32},{48,176},{176,... | collective-permute-start | bytes 5505032 | tf_op jit(solution)/shard_map/ppermute | solution.py:18
  249.3 283.8 %copy-start.4 = (bf16[1,512,512]{2,1,0:T(8,128)(2,1)S(1)}, bf16[1,512,512]{2,1,0:T(8,128)(2,1)}, u32[]{:S(2)}) copy-start(bf16[1,512,512]{2,1,0:T(8,128)(2,1)} %param.8) | copy-start | bytes 1572868
  449.9 83.2 %collective-permute-start.9 = (f32[512,896]{1,0:T(8,128)S(1)}, f32[512,896]{1,0:T(8,128)}, u32[]{:S(2)}, u32[]{:S(2)}) collective-permute-start(f32[512,896]{1,0:T(8,128)S(1)} %add_select_fusion), channel_id=1, source_target_pairs={{0,256},{256,0},{16,272},{272,16},{32,288},{288,32},{48,304},{304,... | collective-permute-start | bytes 5505032 | tf_op jit(solution)/shard_map/ppermute | solution.py:18
  536.3 140.7 %reduce-scatter.7.cloned.1.call-start = ((), (), s32[]{:S(2)}) async-start(), calls=%async_computation.4 | async-start | bytes 2064384
  603.3 15.8 %copy-start.5 = (bf16[1,512,512]{2,1,0:T(8,128)(2,1)S(1)}, bf16[1,512,512]{2,1,0:T(8,128)(2,1)}, u32[]{:S(2)}) copy-start(bf16[1,512,512]{2,1,0:T(8,128)(2,1)} %param.8) | copy-start | bytes 1572868
  621.5 56.6 %copy-start.9 = (bf16[896,896]{1,0:T(8,128)(2,1)S(1)}, bf16[896,896]{1,0:T(8,128)(2,1)}, u32[]{:S(2)}) copy-start(bf16[896,896]{1,0:T(8,128)(2,1)} %all-gather.2.cloned.1.call-done) | copy-start | bytes 4816900
  678.7 34.9 %copy-start.11 = (bf16[256,896]{1,0:T(8,128)(2,1)S(1)}, bf16[256,896]{1,0:T(8,128)(2,1)}, u32[]{:S(2)}) copy-start(bf16[256,896]{1,0:T(8,128)(2,1)} %param.12) | copy-start | bytes 1376260
  678.7 66.5 %copy-start.7 = (bf16[256,896]{0,1:T(8,128)(2,1)S(1)}, bf16[256,896]{0,1:T(8,128)(2,1)}, u32[]{:S(2)}) copy-start(bf16[256,896]{0,1:T(8,128)(2,1)} %reduce-scatter.5.cloned.1.call-done) | copy-start | bytes 1376260
  678.7 4.5 collective-permute-start
  683.2 8.7 %collective-permute-start.1 = (f32[64,896]{1,0:T(8,128)S(1)}, f32[64,896]{1,0:T(8,128)S(1)}, u32[]{:S(2)}, u32[]{:S(2)}) collective-permute-start(f32[64,896]{1,0:T(8,128)S(1)} %add_select_fusion.7), channel_id=1, source_target_pairs={{0,32},{32,0},{16,48},{48,16},{64,96},{96,64},{80,112},{112,80},{1... | collective-permute-start | bytes 688136 | tf_op jit(solution)/shard_map/ppermute | solution.py:18
  691.9 14.3 %collective-permute-start.2 = (f32[64,896]{1,0:T(8,128)S(1)}, f32[64,896]{1,0:T(8,128)S(1)}, u32[]{:S(2)}, u32[]{:S(2)}) collective-permute-start(f32[64,896]{1,0:T(8,128)S(1)} %add_select_fusion.6), channel_id=1, source_target_pairs={{0,64},{64,0},{16,80},{80,16},{32,96},{96,32},{48,112},{112,48},{1... | collective-permute-start | bytes 688136 | tf_op jit(solution)/shard_map/ppermute | solution.py:18
  706.2 27.1 %collective-permute-start.3 = (f32[64,896]{1,0:T(8,128)S(1)}, f32[64,896]{1,0:T(8,128)S(1)}, u32[]{:S(2)}, u32[]{:S(2)}) collective-permute-start(f32[64,896]{1,0:T(8,128)S(1)} %add_select_fusion.5), channel_id=1, source_target_pairs={{0,128},{128,0},{16,144},{144,16},{32,160},{160,32},{48,176},{176,... | collective-permute-start | bytes 688136 | tf_op jit(solution)/shard_map/ppermute | solution.py:18
  734.0 31.9 %collective-permute-start.4 = (f32[64,896]{1,0:T(8,128)}, f32[64,896]{1,0:T(8,128)}, u32[]{:S(2)}, u32[]{:S(2)}) collective-permute-start(f32[64,896]{1,0:T(8,128)} %add_select_fusion.4), channel_id=1, source_target_pairs={{0,256},{256,0},{16,272},{272,16},{32,288},{288,32},{48,304},{304,... | collective-permute-start | bytes 688136 | tf_op jit(solution)/shard_map/ppermute | solution.py:18
  746.1 2.0 copy-start.8
  (2 other events, 3.1 us)
Sparse Core Ops, SparseCore 0:
  10.1 80.5 all-gather.1
  536.4 66.8 reduce-scatter.4
  621.6 55.2 reduce-scatter.6
where the time goes:
time: 775 us; the launch traced here: 774 us
  waiting for transfers between devices  653 us (84%)
  starting transfers between devices  64.6 us (8%)
  other arithmetic  14.8 us (2%)
  between operations  14.2 us (2%)
  blocking collectives  13.4 us (2%)
    ppermute x10, waiting for transfers between devices, partner_2(): return lax.ppermute(block, axis, route)  448 us
    all_gather x1, waiting for transfers between devices, shards(): factor = lax.all_gather(local_factor, ('out', 'rep'), axis=0, tiled=True)  82.7 us
    reduce_scatter x1, waiting for transfers between devices, shards(): lax.psum_scatter(lax.dot_general(columns, x_rot, (((0,), (0,)), ((), ()))...  65.4 us
    ppermute x10, starting transfers between devices, partner_2(): return lax.ppermute(block, axis, route)  64.4 us
    unnamed x4, waiting for transfers between devices  56.2 us
  transfers between devices with their start and end apart: 13, of which 13 were waited for; matrix products, arithmetic and copies ran while one was open for 1% of the time, Pallas kernels for 0%

commit v1 on v0

v1 whole, which is shorter than its diff:
```python
import math

import jax
import jax.numpy as jnp
from jax import lax
from jax.sharding import PartitionSpec as P

GROUP = 128


def trade(block, axis):
    return lax.all_to_all(block, axis, split_axis=0, concat_axis=0, tiled=True)


def spread(block, axis, count):
    return trade(jnp.broadcast_to(block[None], (count,) + block.shape), axis)


def sign_rows(count, inner):
    index = jnp.arange(count * inner, dtype=jnp.int32)
    upper, lower = index // inner, index % inner
    both = upper[:, None] & upper[None, :]
    parity = lax.population_count(both) % 2
    same = (lower[:, None] == lower[None, :]).astype(jnp.int32)
    return ((1 - 2 * parity) * same).astype(jnp.float32)


def mix_local(rows, signs, count):
    mixed = jnp.dot(signs, rows, precision=lax.Precision.HIGHEST)
    return (mixed / math.sqrt(count)).astype(jnp.bfloat16)


def swap(block):
    return lax.ppermute(block, "rep", [(0, 1), (1, 0)])


def shards(x_act, out_grad, weight_codes, group_exps, local_factor, first_moment, second_moment):
    hid_count, out_count = lax.axis_size("hid"), lax.axis_size("out")
    rep_count = lax.axis_size("rep")
    out_index, rep_index = lax.axis_index("out"), lax.axis_index("rep")
    token_count, width = x_act.shape[1:]
    mine = token_count // out_count
    few = mine // hid_count
    code_rows = weight_codes.shape[0]
    grads_out = out_grad[0]
    signs = sign_rows(hid_count, few)

    scales = jnp.exp2(group_exps.astype(jnp.float32))
    w_deq = (
        weight_codes.astype(jnp.float32).reshape(code_rows, width // GROUP, GROUP)
        * scales[:, :, None]
    )
    w_deq = w_deq.reshape(code_rows, width).astype(jnp.bfloat16)
    w_other = swap(w_deq)
    factor = spread(local_factor, ("out", "rep"), out_count * rep_count).reshape(width, width)

    tokens = lax.dynamic_slice_in_dim(x_act[0], out_index * mine, mine, axis=0)
    rows = trade(tokens.reshape(hid_count, few, width), "hid").reshape(mine, width)

    g_own = lax.dynamic_slice_in_dim(grads_out, rep_index * code_rows, code_rows, axis=1)
    g_other = lax.dynamic_slice_in_dim(grads_out, (1 - rep_index) * code_rows, code_rows, axis=1)
    partial_rot = jnp.dot(g_own, w_deq, preferred_element_type=jnp.float32) + jnp.dot(
        g_other, w_other, preferred_element_type=jnp.float32
    )
    pieces = trade(partial_rot.astype(jnp.bfloat16).reshape(out_count, mine, width), "out")

    pre_mix = jnp.dot(rows, factor, preferred_element_type=jnp.float32)
    rotated = mix_local(pre_mix, signs, hid_count)
    x_part = trade(rotated.reshape(hid_count, few, width), "hid").reshape(mine, width)

    grad_rot = pieces.astype(jnp.float32).sum(axis=0).astype(jnp.bfloat16)
    grad_rows = trade(grad_rot.reshape(hid_count, few, width), "hid").reshape(mine, width)
    x_rot = spread(x_part, "out", out_count).reshape(token_count, width)

    back_pre = lax.dot_general(
        grad_rows, factor, (((1,), (1,)), ((), ())), preferred_element_type=jnp.float32
    )
    back = mix_local(back_pre, signs, hid_count)
    input_grad = trade(back.reshape(hid_count, few, width), "hid").reshape(1, mine, width)

    contract = (((0,), (0,)), ((), ()))
    away = lax.dot_general(g_other, x_rot, contract, preferred_element_type=jnp.float32)
    arrived = swap(away.astype(jnp.bfloat16))
    weight_grad = lax.dot_general(
        g_own, x_rot, contract, preferred_element_type=jnp.float32
    ) + arrived.astype(jnp.float32)

    gradient = jnp.where(jnp.abs(weight_codes) <= 126, weight_grad / 16.0, jnp.float32(0.0))
    moment_one = 0.9 * first_moment.astype(jnp.float32) + 0.1 * gradient
    moment_two = 0.95 * second_moment.astype(jnp.float32) + 0.05 * gradient * gradient
    corr_one = 1.0 - 0.9**20
    corr_two = 1.0 - 0.95**20
    weight_step = moment_one / corr_one / (jnp.sqrt(moment_two / corr_two) + 1e-08)
    return (
        input_grad,
        weight_step.astype(jnp.bfloat16),
        moment_one.astype(jnp.bfloat16),
        moment_two.astype(jnp.bfloat16),
    )


def solution(mesh):
    placed = (
        P("rep", None, "hid"),
        P("rep", None, "out"),
        P(("out", "rep"), "hid"),
        P(("out", "rep"), "hid"),
        P(("out", "rep"), None),
        P(("out", "rep"), "hid"),
        P(("out", "rep"), "hid"),
    )
    return jax.shard_map(
        shards,
        mesh=mesh,
        in_specs=placed,
        out_specs=(
            P("rep", "out", "hid"),
            P(("out", "rep"), "hid"),
            P(("out", "rep"), "hid"),
            P(("out", "rep"), "hid"),
        ),
        check_vma=False,
    )
```

time: 775 us -> 186 us (0.24)
  waiting for transfers between devices: 653 us -> 68.5 us
  blocking collectives: 13.4 us -> 52.5 us
  starting transfers between devices: 64.6 us -> 35.2 us
  between operations: 14.2 us -> 0.81 us
  other arithmetic: 14.8 us -> 2.2 us
  matrix products: 7.04 us -> 15 us
    ppermute x10 -> x2, waiting for transfers between devices: 448 us -> 21.2 us  [swap(): return lax.ppermute(block, 'rep', [(0, 1), (1, 0)])]
    all_gather x1 -> x0, waiting for transfers between devices: 82.7 us -> none  [shards(): factor = lax.all_gather(local_factor, ('out', 'rep'), axis=0, tiled=True)]
    reduce_scatter x1 -> x0, waiting for transfers between devices: 65.4 us -> none  [shards(): lax.psum_scatter(lax.dot_general(columns, x_rot, (((0,), (0,)), ((), ()))...]
    ppermute x10 -> x2, starting transfers between devices: 64.4 us -> 6.81 us  [swap(): return lax.ppermute(block, 'rep', [(0, 1), (1, 0)])]
    unnamed x4 -> x0, waiting for transfers between devices: 56.2 us -> none
    all_to_all x0 -> x2, blocking collectives: none -> 52.5 us  [trade(): return lax.all_to_all(block, axis, split_axis=0, concat_axis=0, tiled=True)]
    all_to_all x0 -> x5, waiting for transfers between devices: none -> 47.2 us  [trade(): return lax.all_to_all(block, axis, split_axis=0, concat_axis=0, tiled=True)]
    all_to_all x0 -> x5, starting transfers between devices: none -> 28.4 us  [trade(): return lax.all_to_all(block, axis, split_axis=0, concat_axis=0, tiled=True)]
  transfers between devices with their start and end apart: 13 -> 7, of which waited for: 13 -> 5; matrix products, arithmetic and copies ran while one was open for 1% -> 9% of each run, Pallas kernels for 0% -> 0%
where the time goes in v1:
time: 186 us; the launch traced here: 185 us
  waiting for transfers between devices  68.5 us (37%)
  blocking collectives  52.5 us (28%)
  starting transfers between devices  35.2 us (19%)
  matrix products  15 us (8%)
  local copies, waits for them, and re-layouts  10.4 us (6%)
  other arithmetic  2.2 us (1%)
    all_to_all x2, blocking collectives, trade(): return lax.all_to_all(block, axis, split_axis=0, concat_axis=0, tiled=True)  52.5 us
    all_to_all x5, waiting for transfers between devices, trade(): return lax.all_to_all(block, axis, split_axis=0, concat_axis=0, tiled=True)  47.2 us
    all_to_all x5, starting transfers between devices, trade(): return lax.all_to_all(block, axis, split_axis=0, concat_axis=0, tiled=True)  28.4 us
    ppermute x2, waiting for transfers between devices, swap(): return lax.ppermute(block, 'rep', [(0, 1), (1, 0)])  21.2 us
    ppermute x2, starting transfers between devices, swap(): return lax.ppermute(block, 'rep', [(0, 1), (1, 0)])  6.81 us
    broadcast_in_dim x3, local copies, waits for them, and re-layouts, spread(): return trade(jnp.broadcast_to(block[None], (count,) + block.shape), axis)  4.18 us
  transfers between devices with their start and end apart: 7, of which 5 were waited for; matrix products, arithmetic and copies ran while one was open for 9% of the time, Pallas kernels for 0%

profile of v1, /device:TPU:1, one launch (start us, length us, event | category | flops | bytes accessed | tf_op | source)
XLA Modules:
  0.0 184.6 jit_solution(3199921322266503160)
XLA Ops:
  0.7 1.2 copy-done
  1.9 31.7 %all_to_all.35 = bf16[32,2,896]{2,1,0:T(2,128)(2,1)S(1)} all-to-all(bf16[32,2,896]{2,1,0:T(2,128)(2,1)S(1)} %reshape.98), channel_id=1, replica_groups=mesh['hid'=32,'out'=8,'rep'=2] {'hid'}, dimensions={0} | all-to-all | bytes 229376 | tf_op jit(solution)/shard_map/all_to_all | solution.py:12
  33.6 2.2 %broadcast_in_dim.9 = bf16[16,56,896]{2,1,0:T(8,128)(2,1)} broadcast(bf16[56,896]{1,0:T(8,128)(2,1)} %param.11), dimensions={1,2} | broadcast | bytes 1705984 | tf_op jit(solution)/shard_map/broadcast_in_dim | solution.py:16
  35.7 6.8 %all-to-all-start.2 = ((bf16[16,56,896]{2,1,0:T(8,128)(2,1)}), bf16[16,56,896]{2,1,0:T(8,128)(2,1)S(1)}, u32[]{:S(2)}, u32[]{:S(2)}) async-start(bf16[16,56,896]{2,1,0:T(8,128)(2,1)} %broadcast_in_dim.9), calls=%async_computation.2 | async-start | bytes 3211264 | tf_op jit(solution)/shard_map/all_to_all | solution.py:12
  42.5 1.5 copy.12
  45.6 4.9 %collective-permute-start = (bf16[256,896]{0,1:T(8,128)(2,1)}, bf16[256,896]{0,1:T(8,128)(2,1)}, u32[]{:S(2)}, u32[]{:S(2)}) collective-permute-start(bf16[256,896]{0,1:T(8,128)(2,1)} %fusion.3), channel_id=1, source_target_pairs={{0,1},{1,0},{2,3},{3,2},{4,5},{5,4},{6,7},{7,6},{8,9},{9,8},{10,11... | collective-permute-start | bytes 1376264 | tf_op jit(solution)/shard_map/ppermute | solution.py:34
  50.5 1.6 fusion.10
  52.0 21.2 %collective-permute-done = bf16[256,896]{0,1:T(8,128)(2,1)} collective-permute-done((bf16[256,896]{0,1:T(8,128)(2,1)}, bf16[256,896]{0,1:T(8,128)(2,1)}, u32[]{:S(2)}, u32[]{:S(2)}) %collective-permute-start) | collective-permute-done | bytes 458784 | tf_op jit(solution)/shard_map/ppermute | solution.py:34
  73.3 2.4 %add_convert_fusion = bf16[512,896]{1,0:T(8,128)(2,1)} fusion(f32[512,896]{1,0:T(8,128)S(1)} %fusion.10, bf16[256,896]{0,1:T(8,128)(2,1)} %collective-permute-done, bf16[1,512,512]{2,1,0:T(8,128)(2,1)S(1)} %copy-done.1, s32[]{:T(128)S(6)} %select_n.57), kind=kOutput, calls=%fused_computation | convolution fusion | flops 235798528 | bytes 3473412 | tf_op jit(solution)/shard_map/dot_general | solution.py:62
  75.7 3.8 %all-to-all-start = ((bf16[8,64,896]{2,1,0:T(8,128)(2,1)}), bf16[8,64,896]{2,1,0:T(8,128)(2,1)S(1)}, u32[]{:S(2)}, u32[]{:S(2)}) async-start(bf16[8,64,896]{2,1,0:T(8,128)(2,1)} %bitcast.35), calls=%async_computation | async-start | bytes 1835008 | tf_op jit(solution)/shard_map/all_to_all | solution.py:12
  80.7 1.3 fusion.36
  83.2 8.3 %all-to-all-done = bf16[8,64,896]{2,1,0:T(8,128)(2,1)S(1)} async-done(((bf16[8,64,896]{2,1,0:T(8,128)(2,1)}), bf16[8,64,896]{2,1,0:T(8,128)(2,1)S(1)}, u32[]{:S(2)}, u32[]{:S(2)}) %all-to-all-start) | async-done | bytes 917536 | tf_op jit(solution)/shard_map/all_to_all | solution.py:12
  91.5 9.2 %all-to-all-start.5 = ((bf16[32,2,896]{2,1,0:T(2,128)(2,1)}), bf16[32,2,896]{2,1,0:T(2,128)(2,1)}, u32[]{:S(2)}, u32[]{:S(2)}) async-start(bf16[32,2,896]{2,1,0:T(2,128)(2,1)} %reshape.100), calls=%async_computation.5 | async-start | bytes 229376 | tf_op jit(solution)/shard_map/all_to_all | solution.py:12
  101.5 14.4 %all-to-all-done.5 = bf16[32,2,896]{2,1,0:T(2,128)(2,1)} async-done(((bf16[32,2,896]{2,1,0:T(2,128)(2,1)}), bf16[32,2,896]{2,1,0:T(2,128)(2,1)}, u32[]{:S(2)}, u32[]{:S(2)}) %all-to-all-start.5) | async-done | bytes 114720 | tf_op jit(solution)/shard_map/all_to_all | solution.py:12
  115.8 5.1 %all-to-all-start.1 = ((bf16[32,2,896]{2,1,0:T(2,128)(2,1)}), bf16[32,2,896]{2,1,0:T(2,128)(2,1)S(1)}, u32[]{:S(2)}, u32[]{:S(2)}) async-start(bf16[32,2,896]{2,1,0:T(2,128)(2,1)} %reshape.93), calls=%async_computation.1 | async-start | bytes 229376 | tf_op jit(solution)/shard_map/all_to_all | solution.py:12
  121.9 14.6 %all-to-all-done.1 = bf16[32,2,896]{2,1,0:T(2,128)(2,1)S(1)} async-done(((bf16[32,2,896]{2,1,0:T(2,128)(2,1)}), bf16[32,2,896]{2,1,0:T(2,128)(2,1)S(1)}, u32[]{:S(2)}, u32[]{:S(2)}) %all-to-all-start.1) | async-done | bytes 114720 | tf_op jit(solution)/shard_map/all_to_all | solution.py:12
  137.6 3.6 %all-to-all-start.6 = ((bf16[8,64,896]{2,1,0:T(8,128)(2,1)}), bf16[8,64,896]{2,1,0:T(8,128)(2,1)S(1)}, u32[]{:S(2)}, u32[]{:S(2)}) async-start(bf16[8,64,896]{2,1,0:T(8,128)(2,1)} %broadcast_in_dim.11), calls=%async_computation.6 | async-start | bytes 1835008 | tf_op jit(solution)/shard_map/all_to_all | solution.py:12
  141.8 2.2 %fusion.35 = f32[64,896]{1,0:T(8,128)} fusion(bf16[64,896]{1,0:T(8,128)(2,1)} %reshape.94, bf16[896,896]{1,0:T(8,128)(2,1)S(1)} %bitcast.32), kind=kOutput, calls=%fused_computation.51 | convolution fusion | flops 102760448 | bytes 1949696 | tf_op jit(solution)/shard_map/dot_general | solution.py:75
  144.0 9.9 %all-to-all-done.6 = bf16[8,64,896]{2,1,0:T(8,128)(2,1)S(1)} async-done(((bf16[8,64,896]{2,1,0:T(8,128)(2,1)}), bf16[8,64,896]{2,1,0:T(8,128)(2,1)S(1)}, u32[]{:S(2)}, u32[]{:S(2)}) %all-to-all-start.6) | async-done | bytes 917536 | tf_op jit(solution)/shard_map/all_to_all | solution.py:12
  153.9 2.2 %convolution_convert_fusion = bf16[256,896]{1,0:T(8,128)(2,1)} fusion(bf16[512,896]{1,0:T(8,128)(2,1)S(1)} %bitcast.33, bf16[1,512,512]{2,1,0:T(8,128)(2,1)} %param.8, s32[]{:T(128)S(6)} %select_n.57), kind=kOutput, calls=%fused_computation.2 | convolution fusion | flops 235110400 | bytes 1638404 | tf_op jit(solution)/shard_map/dot_general | solution.py:82
  156.1 1.9 %collective-permute-start.1 = (bf16[256,896]{1,0:T(8,128)(2,1)}, bf16[256,896]{1,0:T(8,128)(2,1)}, u32[]{:S(2)}, u32[]{:S(2)}) collective-permute-start(bf16[256,896]{1,0:T(8,128)(2,1)} %convolution_convert_fusion), channel_id=1, source_target_pairs={{0,1},{1,0},{2,3},{3,2},{4,5},{5,4},{6,7},{7,6},{8,9},{9,8},{10,11... | collective-permute-start | bytes 1376264 | tf_op jit(solution)/shard_map/ppermute | solution.py:34
  158.1 1.4 fusion
  159.5 20.8 %all_to_all.36 = bf16[32,2,896]{2,1,0:T(2,128)(2,1)S(1)} all-to-all(bf16[32,2,896]{2,1,0:T(2,128)(2,1)S(1)} %reshape.96), channel_id=1, replica_groups=mesh['hid'=32,'out'=8,'rep'=2] {'hid'}, dimensions={0} | all-to-all | bytes 229376 | tf_op jit(solution)/shard_map/all_to_all | solution.py:12
  181.0 3.6 %fusion.5 = (bf16[256,896]{1,0:T(8,128)(2,1)}, bf16[256,896]{1,0:T(8,128)(2,1)}, bf16[256,896]{1,0:T(8,128)(2,1)}) fusion(bf16[256,896]{1,0:T(8,128)(2,1)} %param.13, bf16[256,896]{1,0:T(8,128)(2,1)} %param.12, bf16[256,896]{1,0:T(8,128)(2,1)} %collective-permute-done.1, bf16[512,896]{1,0:T(8,128)(2,1)S(1)} %bitcast.34, ...), kind=kOutput, calls=%fused_computation.15 | convolution fusion | flops 239927296 | bytes 4849668 | tf_op jit(solution)/shard_map/dot_general | solution.py:84
  (32 shorter events, 8.2 us)
Async XLA Ops:
  0.6 1.2 copy-start
  35.7 39.9 %all-to-all-start.2 = ((bf16[16,56,896]{2,1,0:T(8,128)(2,1)}), bf16[16,56,896]{2,1,0:T(8,128)(2,1)S(1)}, u32[]{:S(2)}, u32[]{:S(2)}) async-start(bf16[16,56,896]{2,1,0:T(8,128)(2,1)} %broadcast_in_dim.9), calls=%async_computation.2 | async-start | bytes 3211264 | tf_op jit(solution)/shard_map/all_to_all | solution.py:12
  45.6 27.7 %copy-start.1 = (bf16[1,512,512]{2,1,0:T(8,128)(2,1)S(1)}, bf16[1,512,512]{2,1,0:T(8,128)(2,1)}, u32[]{:S(2)}) copy-start(bf16[1,512,512]{2,1,0:T(8,128)(2,1)} %param.8) | copy-start | bytes 1572868
  45.6 27.7 %collective-permute-start = (bf16[256,896]{0,1:T(8,128)(2,1)}, bf16[256,896]{0,1:T(8,128)(2,1)}, u32[]{:S(2)}, u32[]{:S(2)}) collective-permute-start(bf16[256,896]{0,1:T(8,128)(2,1)} %fusion.3), channel_id=1, source_target_pairs={{0,1},{1,0},{2,3},{3,2},{4,5},{5,4},{6,7},{7,6},{8,9},{9,8},{10,11... | collective-permute-start | bytes 1376264 | tf_op jit(solution)/shard_map/ppermute | solution.py:34
  75.7 15.8 %all-to-all-start = ((bf16[8,64,896]{2,1,0:T(8,128)(2,1)}), bf16[8,64,896]{2,1,0:T(8,128)(2,1)S(1)}, u32[]{:S(2)}, u32[]{:S(2)}) async-start(bf16[8,64,896]{2,1,0:T(8,128)(2,1)} %bitcast.35), calls=%async_computation | async-start | bytes 1835008 | tf_op jit(solution)/shard_map/all_to_all | solution.py:12
  80.7 1.3 copy-start.4
  80.7 1.3 copy-start.6
  91.5 24.4 %all-to-all-start.5 = ((bf16[32,2,896]{2,1,0:T(2,128)(2,1)}), bf16[32,2,896]{2,1,0:T(2,128)(2,1)}, u32[]{:S(2)}, u32[]{:S(2)}) async-start(bf16[32,2,896]{2,1,0:T(2,128)(2,1)} %reshape.100), calls=%async_computation.5 | async-start | bytes 229376 | tf_op jit(solution)/shard_map/all_to_all | solution.py:12
  115.8 20.7 %all-to-all-start.1 = ((bf16[32,2,896]{2,1,0:T(2,128)(2,1)}), bf16[32,2,896]{2,1,0:T(2,128)(2,1)S(1)}, u32[]{:S(2)}, u32[]{:S(2)}) async-start(bf16[32,2,896]{2,1,0:T(2,128)(2,1)} %reshape.93), calls=%async_computation.1 | async-start | bytes 229376 | tf_op jit(solution)/shard_map/all_to_all | solution.py:12
  137.6 16.4 %all-to-all-start.6 = ((bf16[8,64,896]{2,1,0:T(8,128)(2,1)}), bf16[8,64,896]{2,1,0:T(8,128)(2,1)S(1)}, u32[]{:S(2)}, u32[]{:S(2)}) async-start(bf16[8,64,896]{2,1,0:T(8,128)(2,1)} %broadcast_in_dim.11), calls=%async_computation.6 | async-start | bytes 1835008 | tf_op jit(solution)/shard_map/all_to_all | solution.py:12
  144.0 14.0 %copy-start.5 = (s32[64]{0:T(128)S(1)}, s32[64]{0:T(128)}, u32[]{:S(2)}) copy-start(s32[64]{0:T(128)} %get-tuple-element.7) | copy-start | bytes 772
  144.0 14.0 %copy-start.7 = (s32[64]{0:T(128)S(1)}, s32[64]{0:T(128)}, u32[]{:S(2)}) copy-start(s32[64]{0:T(128)} %get-tuple-element.8) | copy-start | bytes 772
  144.0 37.0 %copy-start.2 = (bf16[1,512,512]{2,1,0:T(8,128)(2,1)S(1)}, bf16[1,512,512]{2,1,0:T(8,128)(2,1)}, u32[]{:S(2)}) copy-start(bf16[1,512,512]{2,1,0:T(8,128)(2,1)} %param.8) | copy-start | bytes 1572868
  144.0 37.0 %copy-start.3 = (s32[256,896]{1,0:T(8,128)S(1)}, s32[256,896]{1,0:T(8,128)}, u32[]{:S(2)}) copy-start(s32[256,896]{1,0:T(8,128)} %param.9) | copy-start | bytes 2752516
  156.1 24.9 %collective-permute-start.1 = (bf16[256,896]{1,0:T(8,128)(2,1)}, bf16[256,896]{1,0:T(8,128)(2,1)}, u32[]{:S(2)}, u32[]{:S(2)}) collective-permute-start(bf16[256,896]{1,0:T(8,128)(2,1)} %convolution_convert_fusion), channel_id=1, source_target_pairs={{0,1},{1,0},{2,3},{3,2},{4,5},{5,4},{6,7},{7,6},{8,9},{9,8},{10,11... | collective-permute-start | bytes 1376264 | tf_op jit(solution)/shard_map/ppermute | solution.py:34

commit v2 on v1

v2 whole, which is shorter than its diff:
```python
import math

import jax
import jax.numpy as jnp
import numpy as np
from jax import lax
from jax.sharding import PartitionSpec as P

GROUP = 128


def trade(block, axis):
    return lax.all_to_all(block, axis, split_axis=0, concat_axis=0, tiled=True)


def spread(block, axis, count):
    return trade(jnp.broadcast_to(block[None], (count,) + block.shape), axis)


def partner(block, axis, bit):
    count = lax.axis_size(axis)
    return lax.ppermute(block, axis, [(s, s ^ bit) for s in range(count)])


def join(mine, other, upper, axis=0):
    return jnp.where(
        upper, jnp.stack([other, mine], axis=axis), jnp.stack([mine, other], axis=axis)
    )


def sign_rows(count, inner):
    index = np.arange(count * inner)
    upper, lower = index // inner, index % inner
    both = upper[:, None] & upper[None, :]
    parity = np.zeros_like(both)
    for bit in range(count.bit_length()):
        parity ^= both >> bit & 1
    same = lower[:, None] == lower[None, :]
    return ((1 - 2 * parity) * same).astype(np.float32)


def gather_factor(local_factor):
    core = lax.axis_index("hid") % 2
    rows, width = local_factor.shape
    other = partner(local_factor, "rep", 1)
    block = jnp.where(core == lax.axis_index("rep"), local_factor, other)[None]
    for bit in range(lax.axis_size("out").bit_length() - 1):
        upper = (lax.axis_index("out") >> bit & 1) == 1
        block = join(block, partner(block, "out", 1 << bit), upper).reshape(-1, rows, width)
    return join(block, partner(block, "hid", 1), core == 1, axis=1).reshape(width, width)


def shards(x_act, out_grad, weight_codes, group_exps, local_factor, first_moment, second_moment):
    hid_count, out_count = lax.axis_size("hid"), lax.axis_size("out")
    out_index, rep_index = lax.axis_index("out"), lax.axis_index("rep")
    token_count, width = x_act.shape[1:]
    mine = token_count // out_count
    few = mine // hid_count
    code_rows = weight_codes.shape[0]
    grads_out = out_grad[0]
    signs = sign_rows(hid_count, few)
    root = math.sqrt(hid_count)

    tokens = lax.dynamic_slice_in_dim(x_act[0], out_index * mine, mine, axis=0)
    rows = trade(tokens.reshape(hid_count, few, width), "hid").reshape(mine, width)

    scales = jnp.exp2(group_exps.astype(jnp.float32)).astype(jnp.bfloat16)
    lanes = np.repeat(np.eye(width // GROUP, dtype=np.float32), GROUP, axis=1)
    scales = jnp.dot(scales, lanes.astype(jnp.bfloat16), preferred_element_type=jnp.float32)
    w_deq = (weight_codes.astype(jnp.float32) * scales).astype(jnp.bfloat16)
    w_other = partner(w_deq, "rep", 1)
    factor = gather_factor(local_factor)

    g_own = lax.dynamic_slice_in_dim(grads_out, rep_index * code_rows, code_rows, axis=1)
    g_other = lax.dynamic_slice_in_dim(grads_out, (1 - rep_index) * code_rows, code_rows, axis=1)
    partial_rot = jnp.dot(g_own, w_deq, preferred_element_type=jnp.float32) + jnp.dot(
        g_other, w_other, preferred_element_type=jnp.float32
    )
    pieces = trade(partial_rot.astype(jnp.bfloat16).reshape(out_count, mine, width), "out")

    mixed = jnp.dot(signs.astype(jnp.bfloat16), rows, preferred_element_type=jnp.float32) / root
    mixed = mixed.astype(jnp.bfloat16)
    grad_rot = pieces.astype(jnp.float32).sum(axis=0).astype(jnp.bfloat16)
    sent = jnp.concatenate(
        [mixed.reshape(hid_count, few, width), grad_rot.reshape(hid_count, few, width)], axis=1
    )
    got = trade(sent, "hid")
    mixed, grad_rows = got[:, :few].reshape(mine, width), got[:, few:].reshape(mine, width)

    x_part = jnp.dot(mixed, factor, preferred_element_type=jnp.float32).astype(jnp.bfloat16)
    x_rot = spread(x_part, "out", out_count).reshape(token_count, width)

    back = lax.dot_general(
        grad_rows, factor, (((1,), (1,)), ((), ())), preferred_element_type=jnp.float32
    )
    back = jnp.dot(signs, back, precision=lax.Precision.HIGHEST) / root
    back = back.astype(jnp.bfloat16).reshape(hid_count, few, width)
    input_grad = trade(back, "hid").reshape(1, mine, width)

    contract = (((0,), (0,)), ((), ()))
    away = lax.dot_general(g_other, x_rot, contract, preferred_element_type=jnp.float32)
    arrived = partner(away.astype(jnp.bfloat16), "rep", 1)
    weight_grad = lax.dot_general(
        g_own, x_rot, contract, preferred_element_type=jnp.float32
    ) + arrived.astype(jnp.float32)

    gradient = jnp.where(jnp.abs(weight_codes) <= 126, weight_grad / 16.0, jnp.float32(0.0))
    moment_one = 0.9 * first_moment.astype(jnp.float32) + 0.1 * gradient
    moment_two = 0.95 * second_moment.astype(jnp.float32) + 0.05 * gradient * gradient
    corr_one = 1.0 - 0.9**20
    corr_two = 1.0 - 0.95**20
    weight_step = moment_one / corr_one / (jnp.sqrt(moment_two / corr_two) + 1e-08)
    return (
        input_grad,
        weight_step.astype(jnp.bfloat16),
        moment_one.astype(jnp.bfloat16),
        moment_two.astype(jnp.bfloat16),
    )


def solution(mesh):
    placed = (
        P("rep", None, "hid"),
        P("rep", None, "out"),
        P(("out", "rep"), "hid"),
        P(("out", "rep"), "hid"),
        P(("out", "rep"), None),
        P(("out", "rep"), "hid"),
        P(("out", "rep"), "hid"),
    )
    return jax.shard_map(
        shards,
        mesh=mesh,
        in_specs=placed,
        out_specs=(
            P("rep", "out", "hid"),
            P(("out", "rep"), "hid"),
            P(("out", "rep"), "hid"),
            P(("out", "rep"), "hid"),
        ),
        check_vma=False,
    )
```

time: 186 us -> 159 us (0.85)
  blocking collectives: 52.5 us -> 20.6 us
  starting transfers between devices: 35.2 us -> 63.6 us
  waiting for transfers between devices: 68.5 us -> 45.1 us
  other arithmetic: 2.2 us -> 7.63 us
  local copies, waits for them, and re-layouts: 10.4 us -> 4.98 us
    all_to_all x2 -> x1, blocking collectives: 52.5 us -> 20.6 us  [trade(): return lax.all_to_all(block, axis, split_axis=0, concat_axis=0, tiled=True)]
    ppermute x2 -> x7, starting transfers between devices: 6.81 us -> 27.5 us  [partner(): return lax.ppermute(block, axis, [(s, s ^ bit) for s in range(count)])]
    all_to_all x5 -> x4, waiting for transfers between devices: 47.2 us -> 29 us  [trade(): return lax.all_to_all(block, axis, split_axis=0, concat_axis=0, tiled=True)]
    all_to_all x5 -> x4, starting transfers between devices: 28.4 us -> 36.2 us  [trade(): return lax.all_to_all(block, axis, split_axis=0, concat_axis=0, tiled=True)]
    select_n x1 -> x5, other arithmetic: 0.51 us -> 5.91 us  [join(): jnp.where(upper, jnp.stack([other, mine], axis=axis), jnp.stack([mine, ot...]
    ppermute x2 -> x7, waiting for transfers between devices: 21.2 us -> 16 us  [partner(): return lax.ppermute(block, axis, [(s, s ^ bit) for s in range(count)])]
    broadcast_in_dim x3 -> x1, local copies, waits for them, and re-layouts: 4.18 us -> 1.06 us  [spread(): return trade(jnp.broadcast_to(block[None], (count,) + block.shape), axis)]
    unnamed x17 -> x16, local copies, waits for them, and re-layouts: 2.67 us -> 0.78 us
  transfers between devices with their start and end apart: 7 -> 11, of which waited for: 5 -> 5; matrix products, arithmetic and copies ran while one was open for 9% -> 11% of each run, Pallas kernels for 0% -> 0%
where the time goes in v2:
time: 159 us; the launch traced here: 158 us
  starting transfers between devices  63.6 us (40%)
  waiting for transfers between devices  45.1 us (28%)
  blocking collectives  20.6 us (13%)
  matrix products  15.3 us (10%)
  other arithmetic  7.63 us (5%)
  local copies, waits for them, and re-layouts  4.98 us (3%)
    all_to_all x4, starting transfers between devices, trade(): return lax.all_to_all(block, axis, split_axis=0, concat_axis=0, tiled=True)  36.2 us
    all_to_all x4, waiting for transfers between devices, trade(): return lax.all_to_all(block, axis, split_axis=0, concat_axis=0, tiled=True)  29 us
    ppermute x7, starting transfers between devices, partner(): return lax.ppermute(block, axis, [(s, s ^ bit) for s in range(count)])  27.5 us
    all_to_all x1, blocking collectives, trade(): return lax.all_to_all(block, axis, split_axis=0, concat_axis=0, tiled=True)  20.6 us
    ppermute x7, waiting for transfers between devices, partner(): return lax.ppermute(block, axis, [(s, s ^ bit) for s in range(count)])  16 us
    select_n x5, other arithmetic, join(): jnp.where(upper, jnp.stack([other, mine], axis=axis), jnp.stack([mine, ot...  5.91 us
    dot_general x1, matrix products, shards(): lax.dot_general(g_own, x_rot, contract, preferred_element_type=jnp.float32)  3.6 us
  transfers between devices with their start and end apart: 11, of which 5 were waited for; matrix products, arithmetic and copies ran while one was open for 11% of the time, Pallas kernels for 0%

profile of v2, /device:TPU:1, one launch (start us, length us, event | category | flops | bytes accessed | tf_op | source)
XLA Modules:
  0.0 158.2 jit_solution(13703461664428939336)
XLA Ops:
  0.7 1.6 %fusion = bf16[256,896]{1,0:T(8,128)(2,1)S(1)} fusion(bf16[7,896]{1,0:T(8,128)(2,1)} %constant.75.clone, s32[256,896]{1,0:T(8,128)} %param.12, s32[256,7]{0,1:T(8,128)} %param.13), kind=kOutput, calls=%fused_computation.5 | convolution fusion | flops 3904768 | bytes 1395968 | tf_op jit(solution)/shard_map/dot_general | solution.py:69
  2.3 5.5 %collective-permute-start = (bf16[256,896]{1,0:T(8,128)(2,1)S(1)}, bf16[256,896]{1,0:T(8,128)(2,1)}, u32[]{:S(2)}, u32[]{:S(2)}) collective-permute-start(bf16[256,896]{1,0:T(8,128)(2,1)S(1)} %fusion), channel_id=1, source_target_pairs={{0,1},{1,0},{2,3},{3,2},{4,5},{5,4},{6,7},{7,6},{8,9},{9,8},{10,11... | collective-permute-start | bytes 1376264 | tf_op jit(solution)/shard_map/ppermute | solution.py:22
  7.8 1.9 %collective-permute-start.1 = (bf16[56,896]{1,0:T(8,128)(2,1)}, bf16[56,896]{1,0:T(8,128)(2,1)S(1)}, u32[]{:S(2)}, u32[]{:S(2)}) collective-permute-start(bf16[56,896]{1,0:T(8,128)(2,1)} %param.14), channel_id=1, source_target_pairs={{0,1},{1,0},{2,3},{3,2},{4,5},{5,4},{6,7},{7,6},{8,9},{9,8},{10,11... | collective-permute-start | bytes 301064 | tf_op jit(solution)/shard_map/ppermute | solution.py:22
  10.4 16.7 %all-to-all-start = ((bf16[32,2,896]{2,1,0:T(2,128)(2,1)}), bf16[32,2,896]{2,1,0:T(2,128)(2,1)S(1)}, u32[]{:S(2)}, u32[]{:S(2)}) async-start(bf16[32,2,896]{2,1,0:T(2,128)(2,1)} %reshape.189), calls=%async_computation | async-start | bytes 229376 | tf_op jit(solution)/shard_map/all_to_all | solution.py:13
  27.8 3.1 %collective-permute-start.2 = (bf16[1,56,896]{2,1,0:T(8,128)(2,1)}, bf16[1,56,896]{2,1,0:T(8,128)(2,1)S(1)}, u32[]{:S(2)}, u32[]{:S(2)}) collective-permute-start(bf16[1,56,896]{2,1,0:T(8,128)(2,1)} %get-tuple-element.9), channel_id=1, source_target_pairs={{0,2},{2,0},{4,6},{6,4},{8,10},{10,8},{12,14},{14,12},{1,3},{3,1},... | collective-permute-start | bytes 301064 | tf_op jit(solution)/shard_map/ppermute | solution.py:22
  31.0 1.4 fusion.12
  32.4 1.7 %collective-permute-done.2 = bf16[1,56,896]{2,1,0:T(8,128)(2,1)S(1)} collective-permute-done((bf16[1,56,896]{2,1,0:T(8,128)(2,1)}, bf16[1,56,896]{2,1,0:T(8,128)(2,1)S(1)}, u32[]{:S(2)}, u32[]{:S(2)}) %collective-permute-start.2) | collective-permute-done | bytes 100384 | tf_op jit(solution)/shard_map/ppermute | solution.py:22
  34.1 1.7 %maximum_select_fusion.3 = bf16[2,56,896]{2,1,0:T(8,128)(2,1)} fusion(bf16[1,56,896]{2,1,0:T(8,128)(2,1)} %get-tuple-element.9, bf16[1,56,896]{2,1,0:T(8,128)(2,1)S(1)} %collective-permute-done.2, pred[]{:T(512)S(6)} %eq.20), kind=kLoop, calls=%fused_computation.33 | loop fusion | flops 301056 | bytes 401409 | tf_op jit(solution)/shard_map/jit(_where)/select_n | solution.py:26
  35.8 3.2 %collective-permute-start.3 = (bf16[2,56,896]{2,1,0:T(8,128)(2,1)}, bf16[2,56,896]{2,1,0:T(8,128)(2,1)}, u32[]{:S(2)}, u32[]{:S(2)}) collective-permute-start(bf16[2,56,896]{2,1,0:T(8,128)(2,1)} %maximum_select_fusion.3), channel_id=1, source_target_pairs={{0,4},{2,6},{4,0},{6,2},{8,12},{10,14},{12,8},{14,10},{1,5},{3,7},... | collective-permute-start | bytes 602120 | tf_op jit(solution)/shard_map/ppermute | solution.py:22
  39.0 2.5 %add_convert_fusion = bf16[512,896]{1,0:T(8,128)(2,1)} fusion(f32[512,896]{1,0:T(8,128)S(1)} %fusion.12, bf16[256,896]{1,0:T(8,128)(2,1)} %collective-permute-done, bf16[1,512,512]{2,1,0:T(8,128)(2,1)} %param.11, s32[]{:T(128)S(6)} %select_n.118), kind=kOutput, calls=%fused_computation | convolution fusion | flops 235798528 | bytes 3473412 | tf_op jit(solution)/shard_map/dot_general | solution.py:76
  42.3 5.2 %all-to-all-start.1 = ((bf16[8,64,896]{2,1,0:T(8,128)(2,1)}), bf16[8,64,896]{2,1,0:T(8,128)(2,1)S(1)}, u32[]{:S(2)}, u32[]{:S(2)}) async-start(bf16[8,64,896]{2,1,0:T(8,128)(2,1)} %bitcast.48), calls=%async_computation.1 | async-start | bytes 1835008 | tf_op jit(solution)/shard_map/all_to_all | solution.py:13
  48.7 4.9 %collective-permute-start.4 = (bf16[4,56,896]{2,1,0:T(8,128)(2,1)S(1)}, bf16[4,56,896]{2,1,0:T(8,128)(2,1)S(1)}, u32[]{:S(2)}, u32[]{:S(2)}) collective-permute-start(bf16[4,56,896]{2,1,0:T(8,128)(2,1)S(1)} %bitcast.53), channel_id=1, source_target_pairs={{0,8},{2,10},{4,12},{6,14},{8,0},{10,2},{12,4},{14,6},{1,9},{3,11}... | collective-permute-start | bytes 1204232 | tf_op jit(solution)/shard_map/ppermute | solution.py:22
  53.9 14.3 %collective-permute-done.4 = bf16[4,56,896]{2,1,0:T(8,128)(2,1)S(1)} collective-permute-done((bf16[4,56,896]{2,1,0:T(8,128)(2,1)S(1)}, bf16[4,56,896]{2,1,0:T(8,128)(2,1)S(1)}, u32[]{:S(2)}, u32[]{:S(2)}) %collective-permute-start.4) | collective-permute-done | bytes 401440 | tf_op jit(solution)/shard_map/ppermute | solution.py:22
  70.2 4.5 %collective-permute-start.5 = (bf16[8,56,896]{2,1,0:T(8,128)(2,1)S(1)}, bf16[8,56,896]{2,1,0:T(8,128)(2,1)}, u32[]{:S(2)}, u32[]{:S(2)}) collective-permute-start(bf16[8,56,896]{2,1,0:T(8,128)(2,1)S(1)} %bitcast.51), channel_id=1, source_target_pairs={{0,16},{16,0},{32,48},{48,32},{64,80},{80,64},{96,112},{112,96},{1... | collective-permute-start | bytes 2408456 | tf_op jit(solution)/shard_map/ppermute | solution.py:22
  75.8 10.7 %all-to-all-start.2 = ((bf16[32,4,896]{2,1,0:T(4,128)(2,1)}), bf16[32,4,896]{2,1,0:T(4,128)(2,1)S(1)}, u32[]{:S(2)}, u32[]{:S(2)}) async-start(bf16[32,4,896]{2,1,0:T(4,128)(2,1)} %pad_maximum_fusion), calls=%async_computation.2 | async-start | bytes 458752 | tf_op jit(solution)/shard_map/all_to_all | solution.py:13
  86.5 1.8 %maximum_select_fusion = bf16[8,2,56,896]{3,2,1,0:T(8,128)(2,1)S(1)} fusion(bf16[8,1,56,896]{3,2,1,0:T(8,128)(2,1)S(1)} %bitcast.52, bf16[8,1,56,896]{3,2,1,0:T(8,128)(2,1)} %bitcast.12, pred[]{:T(512)S(6)} %eq.17), kind=kLoop, calls=%fused_computation.1 | loop fusion | flops 2408448 | bytes 3211265 | tf_op jit(solution)/shard_map/jit(_where)/select_n | solution.py:26
  88.3 18.5 %all-to-all-done.2 = bf16[32,4,896]{2,1,0:T(4,128)(2,1)S(1)} async-done(((bf16[32,4,896]{2,1,0:T(4,128)(2,1)}), bf16[32,4,896]{2,1,0:T(4,128)(2,1)S(1)}, u32[]{:S(2)}, u32[]{:S(2)}) %all-to-all-start.2) | async-done | bytes 229408 | tf_op jit(solution)/shard_map/all_to_all | solution.py:13
  109.1 3.6 %all-to-all-start.4 = ((bf16[8,64,896]{2,1,0:T(8,128)(2,1)}), bf16[8,64,896]{2,1,0:T(8,128)(2,1)S(1)}, u32[]{:S(2)}, u32[]{:S(2)}) async-start(bf16[8,64,896]{2,1,0:T(8,128)(2,1)} %broadcast_in_dim.14), calls=%async_computation.4 | async-start | bytes 1835008 | tf_op jit(solution)/shard_map/all_to_all | solution.py:13
  113.4 2.2 %fusion.29 = f32[64,896]{1,0:T(8,128)} fusion(bf16[64,896]{1,0:T(8,128)(2,1)} %reshape.194, bf16[896,896]{1,0:T(8,128)(2,1)S(1)} %bitcast.47), kind=kOutput, calls=%fused_computation.47 | convolution fusion | flops 102760448 | bytes 1949696 | tf_op jit(solution)/shard_map/dot_general | solution.py:93
  115.6 9.8 %all-to-all-done.4 = bf16[8,64,896]{2,1,0:T(8,128)(2,1)S(1)} async-done(((bf16[8,64,896]{2,1,0:T(8,128)(2,1)}), bf16[8,64,896]{2,1,0:T(8,128)(2,1)S(1)}, u32[]{:S(2)}, u32[]{:S(2)}) %all-to-all-start.4) | async-done | bytes 917536 | tf_op jit(solution)/shard_map/all_to_all | solution.py:13
  125.4 2.2 %convolution_convert_fusion = bf16[256,896]{1,0:T(8,128)(2,1)} fusion(bf16[512,896]{1,0:T(8,128)(2,1)S(1)} %bitcast.49, bf16[1,512,512]{2,1,0:T(8,128)(2,1)} %param.11, s32[]{:T(128)S(6)} %select_n.118), kind=kOutput, calls=%fused_computation.4 | convolution fusion | flops 235110400 | bytes 1638404 | tf_op jit(solution)/shard_map/dot_general | solution.py:101
  127.6 4.3 %collective-permute-start.6 = (bf16[256,896]{1,0:T(8,128)(2,1)}, bf16[256,896]{1,0:T(8,128)(2,1)}, u32[]{:S(2)}, u32[]{:S(2)}) collective-permute-start(bf16[256,896]{1,0:T(8,128)(2,1)} %convolution_convert_fusion), channel_id=1, source_target_pairs={{0,1},{1,0},{2,3},{3,2},{4,5},{5,4},{6,7},{7,6},{8,9},{9,8},{10,11... | collective-permute-start | bytes 1376264 | tf_op jit(solution)/shard_map/ppermute | solution.py:22
  133.3 20.6 %all_to_all.25 = bf16[32,2,896]{2,1,0:T(2,128)(2,1)S(1)} all-to-all(bf16[32,2,896]{2,1,0:T(2,128)(2,1)S(1)} %reshape.195), channel_id=1, replica_groups=mesh['hid'=32,'out'=8,'rep'=2] {'hid'}, dimensions={0} | all-to-all | bytes 229376 | tf_op jit(solution)/shard_map/all_to_all | solution.py:13
  154.6 3.6 %fusion.7 = (bf16[256,896]{1,0:T(8,128)(2,1)}, bf16[256,896]{1,0:T(8,128)(2,1)}, bf16[256,896]{1,0:T(8,128)(2,1)}) fusion(bf16[256,896]{1,0:T(8,128)(2,1)} %param.16, bf16[256,896]{1,0:T(8,128)(2,1)} %param.15, bf16[256,896]{1,0:T(8,128)(2,1)} %collective-permute-done.6, bf16[512,896]{1,0:T(8,128)(2,1)S(1)} %bitcast.50, ...), kind=kOutput, calls=%fused_computation.20 | convolution fusion | flops 239927296 | bytes 4849668 | tf_op jit(solution)/shard_map/dot_general | solution.py:103
  (43 shorter events, 11.7 us)
Async XLA Ops:
  0.6 9.1 %copy-start = (bf16[1,512,896]{2,1,0:T(8,128)(2,1)S(1)}, bf16[1,512,896]{2,1,0:T(8,128)(2,1)}, u32[]{:S(2)}) copy-start(bf16[1,512,896]{2,1,0:T(8,128)(2,1)} %param.10) | copy-start | bytes 2752516
  0.6 26.5 %copy-start.5 = (bf16[56,896]{1,0:T(8,128)(2,1)S(1)}, bf16[56,896]{1,0:T(8,128)(2,1)}, u32[]{:S(2)}) copy-start(bf16[56,896]{1,0:T(8,128)(2,1)} %param.14) | copy-start | bytes 301060
  2.3 36.7 %collective-permute-start = (bf16[256,896]{1,0:T(8,128)(2,1)S(1)}, bf16[256,896]{1,0:T(8,128)(2,1)}, u32[]{:S(2)}, u32[]{:S(2)}) collective-permute-start(bf16[256,896]{1,0:T(8,128)(2,1)S(1)} %fusion), channel_id=1, source_target_pairs={{0,1},{1,0},{2,3},{3,2},{4,5},{5,4},{6,7},{7,6},{8,9},{9,8},{10,11... | collective-permute-start | bytes 1376264 | tf_op jit(solution)/shard_map/ppermute | solution.py:22
  7.8 19.4 %collective-permute-start.1 = (bf16[56,896]{1,0:T(8,128)(2,1)}, bf16[56,896]{1,0:T(8,128)(2,1)S(1)}, u32[]{:S(2)}, u32[]{:S(2)}) collective-permute-start(bf16[56,896]{1,0:T(8,128)(2,1)} %param.14), channel_id=1, source_target_pairs={{0,1},{1,0},{2,3},{3,2},{4,5},{5,4},{6,7},{7,6},{8,9},{9,8},{10,11... | collective-permute-start | bytes 301064 | tf_op jit(solution)/shard_map/ppermute | solution.py:22
  10.4 31.8 %all-to-all-start = ((bf16[32,2,896]{2,1,0:T(2,128)(2,1)}), bf16[32,2,896]{2,1,0:T(2,128)(2,1)S(1)}, u32[]{:S(2)}, u32[]{:S(2)}) async-start(bf16[32,2,896]{2,1,0:T(2,128)(2,1)} %reshape.189), calls=%async_computation | async-start | bytes 229376 | tf_op jit(solution)/shard_map/all_to_all | solution.py:13
  27.8 6.3 %collective-permute-start.2 = (bf16[1,56,896]{2,1,0:T(8,128)(2,1)}, bf16[1,56,896]{2,1,0:T(8,128)(2,1)S(1)}, u32[]{:S(2)}, u32[]{:S(2)}) collective-permute-start(bf16[1,56,896]{2,1,0:T(8,128)(2,1)} %get-tuple-element.9), channel_id=1, source_target_pairs={{0,2},{2,0},{4,6},{6,4},{8,10},{10,8},{12,14},{14,12},{1,3},{3,1},... | collective-permute-start | bytes 301064 | tf_op jit(solution)/shard_map/ppermute | solution.py:22
  35.8 11.8 %collective-permute-start.3 = (bf16[2,56,896]{2,1,0:T(8,128)(2,1)}, bf16[2,56,896]{2,1,0:T(8,128)(2,1)}, u32[]{:S(2)}, u32[]{:S(2)}) collective-permute-start(bf16[2,56,896]{2,1,0:T(8,128)(2,1)} %maximum_select_fusion.3), channel_id=1, source_target_pairs={{0,4},{2,6},{4,0},{6,2},{8,12},{10,14},{12,8},{14,10},{1,5},{3,7},... | collective-permute-start | bytes 602120 | tf_op jit(solution)/shard_map/ppermute | solution.py:22
  42.3 11.4 %copy-start.7 = (bf16[64,64]{1,0:T(8,128)(2,1)S(1)}, bf16[64,64]{1,0:T(8,128)(2,1)}, u32[]{:S(2)}) copy-start(bf16[64,64]{1,0:T(8,128)(2,1)} %constant.76.clone) | copy-start | bytes 24580
  42.3 32.4 %all-to-all-start.1 = ((bf16[8,64,896]{2,1,0:T(8,128)(2,1)}), bf16[8,64,896]{2,1,0:T(8,128)(2,1)S(1)}, u32[]{:S(2)}, u32[]{:S(2)}) async-start(bf16[8,64,896]{2,1,0:T(8,128)(2,1)} %bitcast.48), calls=%async_computation.1 | async-start | bytes 1835008 | tf_op jit(solution)/shard_map/all_to_all | solution.py:13
  48.7 19.5 %collective-permute-start.4 = (bf16[4,56,896]{2,1,0:T(8,128)(2,1)S(1)}, bf16[4,56,896]{2,1,0:T(8,128)(2,1)S(1)}, u32[]{:S(2)}, u32[]{:S(2)}) collective-permute-start(bf16[4,56,896]{2,1,0:T(8,128)(2,1)S(1)} %bitcast.53), channel_id=1, source_target_pairs={{0,8},{2,10},{4,12},{6,14},{8,0},{10,2},{12,4},{14,6},{1,9},{3,11}... | collective-permute-start | bytes 1204232 | tf_op jit(solution)/shard_map/ppermute | solution.py:22
  68.1 0.7 copy-start.4
  70.2 16.4 %collective-permute-start.5 = (bf16[8,56,896]{2,1,0:T(8,128)(2,1)S(1)}, bf16[8,56,896]{2,1,0:T(8,128)(2,1)}, u32[]{:S(2)}, u32[]{:S(2)}) collective-permute-start(bf16[8,56,896]{2,1,0:T(8,128)(2,1)S(1)} %bitcast.51), channel_id=1, source_target_pairs={{0,16},{16,0},{32,48},{48,32},{64,80},{80,64},{96,112},{112,96},{1... | collective-permute-start | bytes 2408456 | tf_op jit(solution)/shard_map/ppermute | solution.py:22
  75.8 31.0 %all-to-all-start.2 = ((bf16[32,4,896]{2,1,0:T(4,128)(2,1)}), bf16[32,4,896]{2,1,0:T(4,128)(2,1)S(1)}, u32[]{:S(2)}, u32[]{:S(2)}) async-start(bf16[32,4,896]{2,1,0:T(4,128)(2,1)} %pad_maximum_fusion), calls=%async_computation.2 | async-start | bytes 458752 | tf_op jit(solution)/shard_map/all_to_all | solution.py:13
  108.1 4.6 %copy-start.3 = (bf16[32,2,896]{2,1,0:T(2,128)(2,1)S(1)}, bf16[32,2,896]{2,1,0:T(2,128)(2,1)}, u32[]{:S(2)}) copy-start(bf16[32,2,896]{2,1,0:T(2,128)(2,1)} %get-tuple-element.8) | copy-start | bytes 344068
  109.1 16.3 %all-to-all-start.4 = ((bf16[8,64,896]{2,1,0:T(8,128)(2,1)}), bf16[8,64,896]{2,1,0:T(8,128)(2,1)S(1)}, u32[]{:S(2)}, u32[]{:S(2)}) async-start(bf16[8,64,896]{2,1,0:T(8,128)(2,1)} %broadcast_in_dim.14), calls=%async_computation.4 | async-start | bytes 1835008 | tf_op jit(solution)/shard_map/all_to_all | solution.py:13
  115.6 16.3 %copy-start.6 = (f32[64,64]{1,0:T(8,128)S(1)}, f32[64,64]{1,0:T(8,128)}, u32[]{:S(2)}) copy-start(f32[64,64]{1,0:T(8,128)} %constant.77.clone) | copy-start | bytes 49156
  115.6 39.0 %copy-start.1 = (bf16[1,512,512]{2,1,0:T(8,128)(2,1)S(1)}, bf16[1,512,512]{2,1,0:T(8,128)(2,1)}, u32[]{:S(2)}) copy-start(bf16[1,512,512]{2,1,0:T(8,128)(2,1)} %param.11) | copy-start | bytes 1572868
  115.6 39.0 %copy-start.2 = (s32[256,896]{1,0:T(8,128)S(1)}, s32[256,896]{1,0:T(8,128)}, u32[]{:S(2)}) copy-start(s32[256,896]{1,0:T(8,128)} %param.12) | copy-start | bytes 2752516
  127.6 27.0 %collective-permute-start.6 = (bf16[256,896]{1,0:T(8,128)(2,1)}, bf16[256,896]{1,0:T(8,128)(2,1)}, u32[]{:S(2)}, u32[]{:S(2)}) collective-permute-start(bf16[256,896]{1,0:T(8,128)(2,1)} %convolution_convert_fusion), channel_id=1, source_target_pairs={{0,1},{1,0},{2,3},{3,2},{4,5},{5,4},{6,7},{7,6},{8,9},{9,8},{10,11... | collective-permute-start | bytes 1376264 | tf_op jit(solution)/shard_map/ppermute | solution.py:22

commit v3 on v2

--- a/solution.py
+++ b/solution.py
@@ -6,15 +6,12 @@
 from jax import lax
 from jax.sharding import PartitionSpec as P
 
+
 GROUP = 128
 
 
 def trade(block, axis):
     return lax.all_to_all(block, axis, split_axis=0, concat_axis=0, tiled=True)
-
-
-def spread(block, axis, count):
-    return trade(jnp.broadcast_to(block[None], (count,) + block.shape), axis)
 
 
 def partner(block, axis, bit):
@@ -46,11 +43,12 @@
     block = jnp.where(core == lax.axis_index("rep"), local_factor, other)[None]
     for bit in range(lax.axis_size("out").bit_length() - 1):
         upper = (lax.axis_index("out") >> bit & 1) == 1
-        block = join(block, partner(block, "out", 1 << bit), upper).reshape(-1, rows, width)
+        other = partner(block, "out", 1 << bit)
+        block = join(block, other, upper).reshape(-1, rows, width)
     return join(block, partner(block, "hid", 1), core == 1, axis=1).reshape(width, width)
 
 
-def shards(x_act, out_grad, weight_codes, group_exps, local_factor, first_moment, second_moment):
+def step(x_act, out_grad, weight_codes, group_exps, local_factor, first_moment, second_moment):
     hid_count, out_count = lax.axis_size("hid"), lax.axis_size("out")
     out_index, rep_index = lax.axis_index("out"), lax.axis_index("rep")
     token_count, width = x_act.shape[1:]
@@ -71,12 +69,17 @@
     w_other = partner(w_deq, "rep", 1)
     factor = gather_factor(local_factor)
 
+    grads_t = grads_out.T
     g_own = lax.dynamic_slice_in_dim(grads_out, rep_index * code_rows, code_rows, axis=1)
     g_other = lax.dynamic_slice_in_dim(grads_out, (1 - rep_index) * code_rows, code_rows, axis=1)
+    gt_own = lax.dynamic_slice_in_dim(grads_t, rep_index * code_rows, code_rows, axis=0)
+    gt_other = lax.dynamic_slice_in_dim(grads_t, (1 - rep_index) * code_rows, code_rows, axis=0)
+    g_own, g_other, gt_own, gt_other = lax.optimization_barrier((g_own, g_other, gt_own, gt_other))
     partial_rot = jnp.dot(g_own, w_deq, preferred_element_type=jnp.float32) + jnp.dot(
         g_other, w_other, preferred_element_type=jnp.float32
     )
-    pieces = trade(partial_rot.astype(jnp.bfloat16).reshape(out_count, mine, width), "out")
+    partial_rot = partial_rot.astype(jnp.bfloat16).reshape(out_count, mine, width)
+    pieces = trade(partial_rot, "out")
 
     mixed = jnp.dot(signs.astype(jnp.bfloat16), rows, preferred_element_type=jnp.float32) / root
     mixed = mixed.astype(jnp.bfloat16)
@@ -86,9 +89,8 @@
     )
     got = trade(sent, "hid")
     mixed, grad_rows = got[:, :few].reshape(mine, width), got[:, few:].reshape(mine, width)
-
-    x_part = jnp.dot(mixed, factor, preferred_element_type=jnp.float32).astype(jnp.bfloat16)
-    x_rot = spread(x_part, "out", out_count).reshape(token_count, width)
+    mixed = jnp.broadcast_to(mixed[None], (out_count, mine, width))
+    mixed = trade(mixed, "out").reshape(token_count, width)
 
     back = lax.dot_general(
         grad_rows, factor, (((1,), (1,)), ((), ())), preferred_element_type=jnp.float32
@@ -97,13 +99,17 @@
     back = back.astype(jnp.bfloat16).reshape(hid_count, few, width)
     input_grad = trade(back, "hid").reshape(1, mine, width)
 
-    contract = (((0,), (0,)), ((), ()))
-    away = lax.dot_general(g_other, x_rot, contract, preferred_element_type=jnp.float32)
-    arrived = partner(away.astype(jnp.bfloat16), "rep", 1)
-    weight_grad = lax.dot_general(
-        g_own, x_rot, contract, preferred_element_type=jnp.float32
-    ) + arrived.astype(jnp.float32)
+    away = jnp.dot(gt_other, mixed, preferred_element_type=jnp.float32)
+    away = away.astype(jnp.bfloat16)
+    arrived = partner(away, "rep", 1)
+    own = jnp.dot(gt_own, mixed, preferred_element_type=jnp.float32)
+    own = lax.optimization_barrier(own)
+    weight_grad = (own + arrived.astype(jnp.float32)).astype(jnp.bfloat16)
+    weight_grad = jnp.dot(weight_grad, factor, preferred_element_type=jnp.float32)
+    return (input_grad,) + adam(weight_grad, weight_codes, first_moment, second_moment)
 
+
+def adam(weight_grad, weight_codes, first_moment, second_moment):
     gradient = jnp.where(jnp.abs(weight_codes) <= 126, weight_grad / 16.0, jnp.float32(0.0))
     moment_one = 0.9 * first_moment.astype(jnp.float32) + 0.1 * gradient
     moment_two = 0.95 * second_moment.astype(jnp.float32) + 0.05 * gradient * gradient
@@ -111,7 +117,6 @@
     corr_two = 1.0 - 0.95**20
     weight_step = moment_one / corr_one / (jnp.sqrt(moment_two / corr_two) + 1e-08)
     return (
-        input_grad,
         weight_step.astype(jnp.bfloat16),
         moment_one.astype(jnp.bfloat16),
         moment_two.astype(jnp.bfloat16),
@@ -129,7 +134,7 @@
         P(("out", "rep"), "hid"),
     )
     return jax.shard_map(
-        shards,
+        step,
         mesh=mesh,
         in_specs=placed,
         out_specs=(

time: 159 us -> 145 us (0.912)
  blocking collectives: 20.6 us -> 0 us
  waiting for transfers between devices: 45.1 us -> 55.8 us
  other arithmetic: 7.63 us -> 4.55 us
  matrix products: 15.3 us -> 13.7 us
    all_to_all x1 -> x0, blocking collectives: 20.6 us -> none  [trade(): return lax.all_to_all(block, axis, split_axis=0, concat_axis=0, tiled=True)]
    all_to_all x4 -> x5, waiting for transfers between devices: 29 us -> 44.2 us  [trade(): return lax.all_to_all(block, axis, split_axis=0, concat_axis=0, tiled=True)]
    ppermute x7, waiting for transfers between devices: 16 us -> 11.6 us  [partner(): return lax.ppermute(block, axis, [(s, s ^ bit) for s in range(count)])]
    select_n x5, other arithmetic: 5.91 us -> 2.56 us  [join(): jnp.where(upper, jnp.stack([other, mine], axis=axis), jnp.stack([mine, ot...]
    ppermute x7, starting transfers between devices: 27.5 us -> 24.6 us  [partner(): return lax.ppermute(block, axis, [(s, s ^ bit) for s in range(count)])]
    all_to_all x4 -> x5, starting transfers between devices: 36.2 us -> 38.6 us  [trade(): return lax.all_to_all(block, axis, split_axis=0, concat_axis=0, tiled=True)]
    dot_general x9, matrix products: 15.3 us -> 13.7 us  [the longest x1 3.4 us: step(): jnp.dot(weight_grad, factor, preferred_element_type=jnp.float32)]
    reshape x8 -> x7, local copies, waits for them, and re-layouts: 2.31 us -> 3.81 us  [the longest x1 0.95 us: step(): trade(tokens.reshape(hid_count, few, width), 'hid').reshape(mine, width)]
  transfers between devices with their start and end apart: 11 -> 12, of which waited for: 5 -> 6; matrix products, arithmetic and copies ran while one was open for 11% -> 13% of each run, Pallas kernels for 0% -> 0%
where the time goes in v3:
time: 145 us; the launch traced here: 144 us
  starting transfers between devices  63.2 us (44%)
  waiting for transfers between devices  55.8 us (38%)
  matrix products  13.7 us (9%)
  local copies, waits for them, and re-layouts  6 us (4%)
  other arithmetic  4.55 us (3%)
    all_to_all x5, waiting for transfers between devices, trade(): return lax.all_to_all(block, axis, split_axis=0, concat_axis=0, tiled=True)  44.2 us
    all_to_all x5, starting transfers between devices, trade(): return lax.all_to_all(block, axis, split_axis=0, concat_axis=0, tiled=True)  38.6 us
    ppermute x7, starting transfers between devices, partner(): return lax.ppermute(block, axis, [(s, s ^ bit) for s in range(count)])  24.6 us
    ppermute x7, waiting for transfers between devices, partner(): return lax.ppermute(block, axis, [(s, s ^ bit) for s in range(count)])  11.6 us
    dot_general x1, matrix products, step(): jnp.dot(weight_grad, factor, preferred_element_type=jnp.float32)  3.4 us
  transfers between devices with their start and end apart: 12, of which 6 were waited for; matrix products, arithmetic and copies ran while one was open for 13% of the time, Pallas kernels for 0%

profile of v3, /device:TPU:1, one launch (start us, length us, event | category | flops | bytes accessed | tf_op | source)
XLA Modules:
  0.0 144.1 jit_solution(5081523688379645900)
XLA Ops:
  0.7 1.7 %fusion.1 = bf16[256,896]{1,0:T(8,128)(2,1)S(1)} fusion(bf16[7,896]{1,0:T(8,128)(2,1)} %constant.77.clone, s32[256,896]{1,0:T(8,128)} %param.12, s32[256,7]{0,1:T(8,128)} %param.13), kind=kOutput, calls=%fused_computation.7 | convolution fusion | flops 3904768 | bytes 1395968 | tf_op jit(solution)/shard_map/dot_general | solution.py:67
  2.3 5.5 %collective-permute-start = (bf16[256,896]{1,0:T(8,128)(2,1)S(1)}, bf16[256,896]{1,0:T(8,128)(2,1)}, u32[]{:S(2)}, u32[]{:S(2)}) collective-permute-start(bf16[256,896]{1,0:T(8,128)(2,1)S(1)} %fusion.1), channel_id=1, source_target_pairs={{0,1},{1,0},{2,3},{3,2},{4,5},{5,4},{6,7},{7,6},{8,9},{9,8},{10,11... | collective-permute-start | bytes 1376264 | tf_op jit(solution)/shard_map/ppermute | solution.py:19
  8.5 16.2 %all-to-all-start = ((bf16[32,2,896]{2,1,0:T(2,128)(2,1)}), bf16[32,2,896]{2,1,0:T(2,128)(2,1)}, u32[]{:S(2)}, u32[]{:S(2)}) async-start(bf16[32,2,896]{2,1,0:T(2,128)(2,1)} %reshape.186), calls=%async_computation | async-start | bytes 229376 | tf_op jit(solution)/shard_map/all_to_all | solution.py:14
  24.8 2.1 %collective-permute-start.1 = (bf16[56,896]{1,0:T(8,128)(2,1)}, bf16[56,896]{1,0:T(8,128)(2,1)}, u32[]{:S(2)}, u32[]{:S(2)}) collective-permute-start(bf16[56,896]{1,0:T(8,128)(2,1)} %param.14), channel_id=1, source_target_pairs={{0,1},{1,0},{2,3},{3,2},{4,5},{5,4},{6,7},{7,6},{8,9},{9,8},{10,11... | collective-permute-start | bytes 301064 | tf_op jit(solution)/shard_map/ppermute | solution.py:19
  28.3 2.4 %add_convert_fusion = bf16[512,896]{1,0:T(8,128)(2,1)} fusion(f32[512,896]{1,0:T(8,128)S(1)} %fusion.14, bf16[512,256]{1,0:T(8,128)(2,1)S(1)} %get-tuple-element.9, bf16[256,896]{1,0:T(8,128)(2,1)} %collective-permute-done), kind=kOutput, calls=%fused_computation | convolution fusion | flops 235798528 | bytes 3473408 | tf_op jit(solution)/shard_map/dot_general | solution.py:78
  30.7 9.3 %all-to-all-done = bf16[32,2,896]{2,1,0:T(2,128)(2,1)} async-done(((bf16[32,2,896]{2,1,0:T(2,128)(2,1)}), bf16[32,2,896]{2,1,0:T(2,128)(2,1)}, u32[]{:S(2)}, u32[]{:S(2)}) %all-to-all-start) | async-done | bytes 114720 | tf_op jit(solution)/shard_map/all_to_all | solution.py:14
  40.0 4.3 %all-to-all-start.1 = ((bf16[8,64,896]{2,1,0:T(8,128)(2,1)}), bf16[8,64,896]{2,1,0:T(8,128)(2,1)S(1)}, u32[]{:S(2)}, u32[]{:S(2)}) async-start(bf16[8,64,896]{2,1,0:T(8,128)(2,1)} %bitcast.49), calls=%async_computation.1 | async-start | bytes 1835008 | tf_op jit(solution)/shard_map/all_to_all | solution.py:14
  45.3 3.4 %collective-permute-start.2 = (bf16[1,56,896]{2,1,0:T(8,128)(2,1)S(1)}, bf16[1,56,896]{2,1,0:T(8,128)(2,1)S(1)}, u32[]{:S(2)}, u32[]{:S(2)}) collective-permute-start(bf16[1,56,896]{2,1,0:T(8,128)(2,1)S(1)} %get-tuple-element.21), channel_id=1, source_target_pairs={{0,2},{2,0},{4,6},{6,4},{8,10},{10,8},{12,14},{14,12},{1,3},{3,1},... | collective-permute-start | bytes 301064 | tf_op jit(solution)/shard_map/ppermute | solution.py:19
  48.6 8.4 %collective-permute-done.2 = bf16[1,56,896]{2,1,0:T(8,128)(2,1)S(1)} collective-permute-done((bf16[1,56,896]{2,1,0:T(8,128)(2,1)S(1)}, bf16[1,56,896]{2,1,0:T(8,128)(2,1)S(1)}, u32[]{:S(2)}, u32[]{:S(2)}) %collective-permute-start.2) | collective-permute-done | bytes 100384 | tf_op jit(solution)/shard_map/ppermute | solution.py:19
  57.1 3.2 %collective-permute-start.3 = (bf16[2,56,896]{2,1,0:T(8,128)(2,1)S(1)}, bf16[2,56,896]{2,1,0:T(8,128)(2,1)S(1)}, u32[]{:S(2)}, u32[]{:S(2)}) collective-permute-start(bf16[2,56,896]{2,1,0:T(8,128)(2,1)S(1)} %maximum_select_fusion.3), channel_id=1, source_target_pairs={{0,4},{2,6},{4,0},{6,2},{8,12},{10,14},{12,8},{14,10},{1,5},{3,7},... | collective-permute-start | bytes 602120 | tf_op jit(solution)/shard_map/ppermute | solution.py:19
  60.3 3.2 %collective-permute-done.3 = bf16[2,56,896]{2,1,0:T(8,128)(2,1)S(1)} collective-permute-done((bf16[2,56,896]{2,1,0:T(8,128)(2,1)S(1)}, bf16[2,56,896]{2,1,0:T(8,128)(2,1)S(1)}, u32[]{:S(2)}, u32[]{:S(2)}) %collective-permute-start.3) | collective-permute-done | bytes 200736 | tf_op jit(solution)/shard_map/ppermute | solution.py:19
  63.6 4.6 %collective-permute-start.4 = (bf16[4,56,896]{2,1,0:T(8,128)(2,1)S(1)}, bf16[4,56,896]{2,1,0:T(8,128)(2,1)S(1)}, u32[]{:S(2)}, u32[]{:S(2)}) collective-permute-start(bf16[4,56,896]{2,1,0:T(8,128)(2,1)S(1)} %bitcast.52), channel_id=1, source_target_pairs={{0,8},{2,10},{4,12},{6,14},{8,0},{10,2},{12,4},{14,6},{1,9},{3,11}... | collective-permute-start | bytes 1204232 | tf_op jit(solution)/shard_map/ppermute | solution.py:19
  70.5 8.4 %all-to-all-start.2 = ((bf16[32,4,896]{2,1,0:T(4,128)(2,1)}), bf16[32,4,896]{2,1,0:T(4,128)(2,1)S(1)}, u32[]{:S(2)}, u32[]{:S(2)}) async-start(bf16[32,4,896]{2,1,0:T(4,128)(2,1)} %pad_maximum_fusion), calls=%async_computation.2 | async-start | bytes 458752 | tf_op jit(solution)/shard_map/all_to_all | solution.py:14
  79.2 2.1 %collective-permute-start.5 = (bf16[8,56,896]{2,1,0:T(8,128)(2,1)S(1)}, bf16[8,56,896]{2,1,0:T(8,128)(2,1)}, u32[]{:S(2)}, u32[]{:S(2)}) collective-permute-start(bf16[8,56,896]{2,1,0:T(8,128)(2,1)S(1)} %bitcast.50), channel_id=1, source_target_pairs={{0,16},{16,0},{32,48},{48,32},{64,80},{80,64},{96,112},{112,96},{1... | collective-permute-start | bytes 2408456 | tf_op jit(solution)/shard_map/ppermute | solution.py:19
  81.3 18.0 %all-to-all-done.2 = bf16[32,4,896]{2,1,0:T(4,128)(2,1)S(1)} async-done(((bf16[32,4,896]{2,1,0:T(4,128)(2,1)}), bf16[32,4,896]{2,1,0:T(4,128)(2,1)S(1)}, u32[]{:S(2)}, u32[]{:S(2)}) %all-to-all-start.2) | async-done | bytes 229408 | tf_op jit(solution)/shard_map/all_to_all | solution.py:14
  100.6 3.6 %all-to-all-start.4 = ((bf16[8,64,896]{2,1,0:T(8,128)(2,1)}), bf16[8,64,896]{2,1,0:T(8,128)(2,1)S(1)}, u32[]{:S(2)}, u32[]{:S(2)}) async-start(bf16[8,64,896]{2,1,0:T(8,128)(2,1)} %broadcast_in_dim.16), calls=%async_computation.4 | async-start | bytes 1835008 | tf_op jit(solution)/shard_map/all_to_all | solution.py:14
  104.2 2.2 %maximum_select_fusion = bf16[8,2,56,896]{3,2,1,0:T(8,128)(2,1)S(1)} fusion(bf16[8,1,56,896]{3,2,1,0:T(8,128)(2,1)} %bitcast.51, bf16[8,1,56,896]{3,2,1,0:T(8,128)(2,1)} %bitcast.14, pred[]{:T(512)S(6)} %eq.17), kind=kLoop, calls=%fused_computation.1 | loop fusion | flops 2408448 | bytes 3211265 | tf_op jit(solution)/shard_map/jit(_where)/select_n | solution.py:23
  109.6 7.2 %all-to-all-done.4 = bf16[8,64,896]{2,1,0:T(8,128)(2,1)S(1)} async-done(((bf16[8,64,896]{2,1,0:T(8,128)(2,1)}), bf16[8,64,896]{2,1,0:T(8,128)(2,1)S(1)}, u32[]{:S(2)}, u32[]{:S(2)}) %all-to-all-start.4) | async-done | bytes 917536 | tf_op jit(solution)/shard_map/all_to_all | solution.py:14
  116.8 6.0 %all-to-all-start.3 = ((bf16[32,2,896]{2,1,0:T(2,128)(2,1)}), bf16[32,2,896]{2,1,0:T(2,128)(2,1)S(1)}, u32[]{:S(2)}, u32[]{:S(2)}) async-start(bf16[32,2,896]{2,1,0:T(2,128)(2,1)} %reshape.192), calls=%async_computation.3 | async-start | bytes 229376 | tf_op jit(solution)/shard_map/all_to_all | solution.py:14
  122.8 2.2 %convolution_convert_fusion = bf16[256,896]{1,0:T(8,128)(2,1)} fusion(bf16[256,512]{0,1:T(8,128)(2,1)} %get-tuple-element.11, bf16[512,896]{1,0:T(8,128)(2,1)S(1)} %bitcast.45), kind=kOutput, calls=%fused_computation.6 | convolution fusion | flops 235110400 | bytes 1638400 | tf_op jit(solution)/shard_map/dot_general | solution.py:102
  125.0 3.6 %collective-permute-start.6 = (bf16[256,896]{1,0:T(8,128)(2,1)}, bf16[256,896]{1,0:T(8,128)(2,1)}, u32[]{:S(2)}, u32[]{:S(2)}) collective-permute-start(bf16[256,896]{1,0:T(8,128)(2,1)} %convolution_convert_fusion), channel_id=1, source_target_pairs={{0,1},{1,0},{2,3},{3,2},{4,5},{5,4},{6,7},{7,6},{8,9},{9,8},{10,11... | collective-permute-start | bytes 1376264 | tf_op jit(solution)/shard_map/ppermute | solution.py:19
  128.7 9.8 %all-to-all-done.3 = bf16[32,2,896]{2,1,0:T(2,128)(2,1)S(1)} async-done(((bf16[32,2,896]{2,1,0:T(2,128)(2,1)}), bf16[32,2,896]{2,1,0:T(2,128)(2,1)S(1)}, u32[]{:S(2)}, u32[]{:S(2)}) %all-to-all-start.3) | async-done | bytes 114720 | tf_op jit(solution)/shard_map/all_to_all | solution.py:14
  139.1 1.5 %fusion.16 = f32[256,896]{1,0:T(8,128)S(1)} fusion(bf16[256,512]{0,1:T(8,128)(2,1)} %get-tuple-element.10, bf16[512,896]{1,0:T(8,128)(2,1)S(1)} %bitcast.46), kind=kOutput, calls=%fused_computation.40 | convolution fusion | flops 234881024 | bytes 2097152 | tf_op jit(solution)/shard_map/dot_general | solution.py:105
  140.7 3.4 %fusion.8 = (bf16[256,896]{1,0:T(8,128)(2,1)}, bf16[256,896]{1,0:T(8,128)(2,1)}, bf16[256,896]{1,0:T(8,128)(2,1)}) fusion(bf16[256,896]{1,0:T(8,128)(2,1)S(1)} %copy-done.6, bf16[256,896]{1,0:T(8,128)(2,1)S(1)} %copy-done.7, bf16[896,896]{1,0:T(8,128)(2,1)S(1)} %bitcast.48, f32[256,896]{1,0:T(8,128)S(1)} %fusion.16, ...), kind=kOutput, calls=%fused_computation.21 | convolution fusion | flops 416317440 | bytes 6193152 | tf_op jit(solution)/shard_map/dot_general | solution.py:108
  (45 shorter events, 10.8 us)
Async XLA Ops:
  0.6 7.2 %copy-start = (bf16[1,512,896]{2,1,0:T(8,128)(2,1)S(1)}, bf16[1,512,896]{2,1,0:T(8,128)(2,1)}, u32[]{:S(2)}) copy-start(bf16[1,512,896]{2,1,0:T(8,128)(2,1)} %param.10) | copy-start | bytes 2752516
  0.6 26.3 %copy-start.3 = (bf16[1,512,512]{2,1,0:T(8,128)(2,1)S(1)}, bf16[1,512,512]{2,1,0:T(8,128)(2,1)}, u32[]{:S(2)}) copy-start(bf16[1,512,512]{2,1,0:T(8,128)(2,1)} %param.11) | copy-start | bytes 1572868
  2.3 26.0 %collective-permute-start = (bf16[256,896]{1,0:T(8,128)(2,1)S(1)}, bf16[256,896]{1,0:T(8,128)(2,1)}, u32[]{:S(2)}, u32[]{:S(2)}) collective-permute-start(bf16[256,896]{1,0:T(8,128)(2,1)S(1)} %fusion.1), channel_id=1, source_target_pairs={{0,1},{1,0},{2,3},{3,2},{4,5},{5,4},{6,7},{7,6},{8,9},{9,8},{10,11... | collective-permute-start | bytes 1376264 | tf_op jit(solution)/shard_map/ppermute | solution.py:19
  8.5 31.4 %all-to-all-start = ((bf16[32,2,896]{2,1,0:T(2,128)(2,1)}), bf16[32,2,896]{2,1,0:T(2,128)(2,1)}, u32[]{:S(2)}, u32[]{:S(2)}) async-start(bf16[32,2,896]{2,1,0:T(2,128)(2,1)} %reshape.186), calls=%async_computation | async-start | bytes 229376 | tf_op jit(solution)/shard_map/all_to_all | solution.py:14
  24.8 19.5 %collective-permute-start.1 = (bf16[56,896]{1,0:T(8,128)(2,1)}, bf16[56,896]{1,0:T(8,128)(2,1)}, u32[]{:S(2)}, u32[]{:S(2)}) collective-permute-start(bf16[56,896]{1,0:T(8,128)(2,1)} %param.14), channel_id=1, source_target_pairs={{0,1},{1,0},{2,3},{3,2},{4,5},{5,4},{6,7},{7,6},{8,9},{9,8},{10,11... | collective-permute-start | bytes 301064 | tf_op jit(solution)/shard_map/ppermute | solution.py:19
  40.0 29.2 %copy-start.5 = (bf16[64,64]{1,0:T(8,128)(2,1)S(1)}, bf16[64,64]{1,0:T(8,128)(2,1)}, u32[]{:S(2)}) copy-start(bf16[64,64]{1,0:T(8,128)(2,1)} %constant.78.clone) | copy-start | bytes 24580
  40.0 29.4 %all-to-all-start.1 = ((bf16[8,64,896]{2,1,0:T(8,128)(2,1)}), bf16[8,64,896]{2,1,0:T(8,128)(2,1)S(1)}, u32[]{:S(2)}, u32[]{:S(2)}) async-start(bf16[8,64,896]{2,1,0:T(8,128)(2,1)} %bitcast.49), calls=%async_computation.1 | async-start | bytes 1835008 | tf_op jit(solution)/shard_map/all_to_all | solution.py:14
  45.3 11.7 %collective-permute-start.2 = (bf16[1,56,896]{2,1,0:T(8,128)(2,1)S(1)}, bf16[1,56,896]{2,1,0:T(8,128)(2,1)S(1)}, u32[]{:S(2)}, u32[]{:S(2)}) collective-permute-start(bf16[1,56,896]{2,1,0:T(8,128)(2,1)S(1)} %get-tuple-element.21), channel_id=1, source_target_pairs={{0,2},{2,0},{4,6},{6,4},{8,10},{10,8},{12,14},{14,12},{1,3},{3,1},... | collective-permute-start | bytes 301064 | tf_op jit(solution)/shard_map/ppermute | solution.py:19
  57.1 6.5 %collective-permute-start.3 = (bf16[2,56,896]{2,1,0:T(8,128)(2,1)S(1)}, bf16[2,56,896]{2,1,0:T(8,128)(2,1)S(1)}, u32[]{:S(2)}, u32[]{:S(2)}) collective-permute-start(bf16[2,56,896]{2,1,0:T(8,128)(2,1)S(1)} %maximum_select_fusion.3), channel_id=1, source_target_pairs={{0,4},{2,6},{4,0},{6,2},{8,12},{10,14},{12,8},{14,10},{1,5},{3,7},... | collective-permute-start | bytes 602120 | tf_op jit(solution)/shard_map/ppermute | solution.py:19
  63.6 15.4 %collective-permute-start.4 = (bf16[4,56,896]{2,1,0:T(8,128)(2,1)S(1)}, bf16[4,56,896]{2,1,0:T(8,128)(2,1)S(1)}, u32[]{:S(2)}, u32[]{:S(2)}) collective-permute-start(bf16[4,56,896]{2,1,0:T(8,128)(2,1)S(1)} %bitcast.52), channel_id=1, source_target_pairs={{0,8},{2,10},{4,12},{6,14},{8,0},{10,2},{12,4},{14,6},{1,9},{3,11}... | collective-permute-start | bytes 1204232 | tf_op jit(solution)/shard_map/ppermute | solution.py:19
  70.5 28.7 %all-to-all-start.2 = ((bf16[32,4,896]{2,1,0:T(4,128)(2,1)}), bf16[32,4,896]{2,1,0:T(4,128)(2,1)S(1)}, u32[]{:S(2)}, u32[]{:S(2)}) async-start(bf16[32,4,896]{2,1,0:T(4,128)(2,1)} %pad_maximum_fusion), calls=%async_computation.2 | async-start | bytes 458752 | tf_op jit(solution)/shard_map/all_to_all | solution.py:14
  79.2 21.4 %copy-start.1 = (bf16[2,4,56,896]{3,2,1,0:T(8,128)(2,1)}, bf16[2,4,56,896]{3,2,1,0:T(8,128)(2,1)S(1)}, u32[]{:S(2)}) copy-start(bf16[2,4,56,896]{3,2,1,0:T(8,128)(2,1)S(1)} %maximum_select_fusion.1) | copy-start | bytes 2408452
  79.2 25.0 %collective-permute-start.5 = (bf16[8,56,896]{2,1,0:T(8,128)(2,1)S(1)}, bf16[8,56,896]{2,1,0:T(8,128)(2,1)}, u32[]{:S(2)}, u32[]{:S(2)}) collective-permute-start(bf16[8,56,896]{2,1,0:T(8,128)(2,1)S(1)} %bitcast.50), channel_id=1, source_target_pairs={{0,16},{16,0},{32,48},{48,32},{64,80},{80,64},{96,112},{112,96},{1... | collective-permute-start | bytes 2408456 | tf_op jit(solution)/shard_map/ppermute | solution.py:19
  100.6 16.3 %all-to-all-start.4 = ((bf16[8,64,896]{2,1,0:T(8,128)(2,1)}), bf16[8,64,896]{2,1,0:T(8,128)(2,1)S(1)}, u32[]{:S(2)}, u32[]{:S(2)}) async-start(bf16[8,64,896]{2,1,0:T(8,128)(2,1)} %broadcast_in_dim.16), calls=%async_computation.4 | async-start | bytes 1835008 | tf_op jit(solution)/shard_map/all_to_all | solution.py:14
  107.1 1.5 %copy-start.4 = (f32[64,64]{1,0:T(8,128)S(1)}, f32[64,64]{1,0:T(8,128)}, u32[]{:S(2)}) copy-start(f32[64,64]{1,0:T(8,128)} %constant.79.clone) | copy-start | bytes 49156
  116.8 21.6 %all-to-all-start.3 = ((bf16[32,2,896]{2,1,0:T(2,128)(2,1)}), bf16[32,2,896]{2,1,0:T(2,128)(2,1)S(1)}, u32[]{:S(2)}, u32[]{:S(2)}) async-start(bf16[32,2,896]{2,1,0:T(2,128)(2,1)} %reshape.192), calls=%async_computation.3 | async-start | bytes 229376 | tf_op jit(solution)/shard_map/all_to_all | solution.py:14
  125.0 15.6 %collective-permute-start.6 = (bf16[256,896]{1,0:T(8,128)(2,1)}, bf16[256,896]{1,0:T(8,128)(2,1)}, u32[]{:S(2)}, u32[]{:S(2)}) collective-permute-start(bf16[256,896]{1,0:T(8,128)(2,1)} %convolution_convert_fusion), channel_id=1, source_target_pairs={{0,1},{1,0},{2,3},{3,2},{4,5},{5,4},{6,7},{7,6},{8,9},{9,8},{10,11... | collective-permute-start | bytes 1376264 | tf_op jit(solution)/shard_map/ppermute | solution.py:19
  139.1 1.6 %copy-start.2 = (s32[256,896]{1,0:T(8,128)S(1)}, s32[256,896]{1,0:T(8,128)}, u32[]{:S(2)}) copy-start(s32[256,896]{1,0:T(8,128)} %param.12) | copy-start | bytes 2752516
  139.1 1.6 %copy-start.6 = (bf16[256,896]{1,0:T(8,128)(2,1)S(1)}, bf16[256,896]{1,0:T(8,128)(2,1)}, u32[]{:S(2)}) copy-start(bf16[256,896]{1,0:T(8,128)(2,1)} %param.16) | copy-start | bytes 1376260
  139.1 1.6 %copy-start.7 = (bf16[256,896]{1,0:T(8,128)(2,1)S(1)}, bf16[256,896]{1,0:T(8,128)(2,1)}, u32[]{:S(2)}) copy-start(bf16[256,896]{1,0:T(8,128)(2,1)} %param.15) | copy-start | bytes 1376260

commit v4 on v3

--- a/solution.py
+++ b/solution.py
@@ -4,6 +4,8 @@
 import jax.numpy as jnp
 import numpy as np
 from jax import lax
+from jax.experimental import pallas as pl
+from jax.experimental.pallas import tpu as pltpu
 from jax.sharding import PartitionSpec as P
 
 
@@ -19,10 +21,34 @@
     return lax.ppermute(block, axis, [(s, s ^ bit) for s in range(count)])
 
 
-def join(mine, other, upper, axis=0):
-    return jnp.where(
-        upper, jnp.stack([other, mine], axis=axis), jnp.stack([mine, other], axis=axis)
-    )
+def order_kernel(place, mine, other, out):
+    spot, core = place[0], place[1]
+    for index in range(mine.shape[0]):
+        source = index ^ spot
+
+        @pl.when(core == 0)
+        def _():
+            out[index, 0] = mine[source]
+            out[index, 1] = other[source]
+
+        @pl.when(core == 1)
+        def _():
+            out[index, 0] = other[source]
+            out[index, 1] = mine[source]
+
+
+def in_order(mine, other, spot, core):
+    count, rows, width = mine.shape
+    whole = pl.BlockSpec(memory_space=pltpu.VMEM)
+    return pl.pallas_call(
+        order_kernel,
+        out_shape=jax.ShapeDtypeStruct((count, 2, rows, width), mine.dtype),
+        in_specs=[pl.BlockSpec(memory_space=pltpu.SMEM), whole, whole],
+        out_specs=whole,
+        cost_estimate=pl.CostEstimate(
+            flops=0, bytes_accessed=8 * count * rows * width, transcendentals=0
+        ),
+    )(jnp.stack([spot, core]), mine, other)
 
 
 def sign_rows(count, inner):
@@ -37,15 +63,28 @@
 
 
 def gather_factor(local_factor):
-    core = lax.axis_index("hid") % 2
-    rows, width = local_factor.shape
+    core, spot = lax.axis_index("hid") % 2, lax.axis_index("out")
+    _, width = local_factor.shape
+    bits = lax.axis_size("out").bit_length() - 1
     other = partner(local_factor, "rep", 1)
     block = jnp.where(core == lax.axis_index("rep"), local_factor, other)[None]
-    for bit in range(lax.axis_size("out").bit_length() - 1):
-        upper = (lax.axis_index("out") >> bit & 1) == 1
+    for bit in range(bits):
         other = partner(block, "out", 1 << bit)
-        block = join(block, other, upper).reshape(-1, rows, width)
-    return join(block, partner(block, "hid", 1), core == 1, axis=1).reshape(width, width)
+        block = jnp.concatenate([block, other], axis=0)
+    other = partner(block, "hid", 1)
+    return in_order(block, other, spot, core).reshape(width, width)
+
+
+def mix_blocks(block):
+    where = lax.axis_index("hid")
+    count = lax.axis_size("hid")
+    total = block
+    for bit in reversed(range(count.bit_length() - 1)):
+        sent = total if bit < 3 else total.astype(jnp.bfloat16)
+        other = partner(sent, "hid", 1 << bit).astype(jnp.float32)
+        sign = 1.0 - 2.0 * (where >> bit & 1).astype(jnp.float32)
+        total = other + sign * total.astype(jnp.float32)
+    return (total / math.sqrt(count)).astype(jnp.bfloat16)
 
 
 def step(x_act, out_grad, weight_codes, group_exps, local_factor, first_moment, second_moment):
@@ -60,7 +99,7 @@
     root = math.sqrt(hid_count)
 
     tokens = lax.dynamic_slice_in_dim(x_act[0], out_index * mine, mine, axis=0)
-    rows = trade(tokens.reshape(hid_count, few, width), "hid").reshape(mine, width)
+    mixed = mix_blocks(tokens)
 
     scales = jnp.exp2(group_exps.astype(jnp.float32)).astype(jnp.bfloat16)
     lanes = np.repeat(np.eye(width // GROUP, dtype=np.float32), GROUP, axis=1)
@@ -81,14 +120,9 @@
     partial_rot = partial_rot.astype(jnp.bfloat16).reshape(out_count, mine, width)
     pieces = trade(partial_rot, "out")
 
-    mixed = jnp.dot(signs.astype(jnp.bfloat16), rows, preferred_element_type=jnp.float32) / root
-    mixed = mixed.astype(jnp.bfloat16)
     grad_rot = pieces.astype(jnp.float32).sum(axis=0).astype(jnp.bfloat16)
-    sent = jnp.concatenate(
-        [mixed.reshape(hid_count, few, width), grad_rot.reshape(hid_count, few, width)], axis=1
-    )
-    got = trade(sent, "hid")
-    mixed, grad_rows = got[:, :few].reshape(mine, width), got[:, few:].reshape(mine, width)
+    grad_rows = trade(grad_rot.reshape(hid_count, few, width), "hid")
+    grad_rows = grad_rows.reshape(mine, width)
     mixed = jnp.broadcast_to(mixed[None], (out_count, mine, width))
     mixed = trade(mixed, "out").reshape(token_count, width)
 

time: 145 us -> 163 us (1.12)
  starting transfers between devices: 63.2 us -> 89.6 us
  waiting for transfers between devices: 55.8 us -> 44.1 us
  Pallas kernels: 0 us -> 2.75 us
    ppermute x7 -> x12, starting transfers between devices: 24.6 us -> 64.8 us  [partner(): return lax.ppermute(block, axis, [(s, s ^ bit) for s in range(count)])]
    all_to_all x5 -> x4, starting transfers between devices: 38.6 us -> 24.8 us  [trade(): return lax.all_to_all(block, axis, split_axis=0, concat_axis=0, tiled=True)]
    all_to_all x5 -> x4, waiting for transfers between devices: 44.2 us -> 31.4 us  [trade(): return lax.all_to_all(block, axis, split_axis=0, concat_axis=0, tiled=True)]
    pallas_call x0 -> x1, Pallas kernels: none -> 2.75 us  [in_order(): pl.pallas_call(order_kernel, out_shape=jax.ShapeDtypeStruct((count, 2, ro...]
    select_n x5 -> x0, other arithmetic: 2.56 us -> none  [join(): jnp.where(upper, jnp.stack([other, mine], axis=axis), jnp.stack([mine, ot...]
    add x0 -> x3, other arithmetic: none -> 2.02 us  [mix_blocks(): total = other + sign * total.astype(jnp.float32)]
    convert_element_type x0 -> x2, other arithmetic: none -> 1.95 us  [the longest x1 0.98 us: mix_blocks(): sent = total if bit < 3 else total.astype(jnp.bfloat16)]
    reshape x5 -> x2, local copies, waits for them, and re-layouts: 2.43 us -> 0.74 us  [the longest x1 0.69 us: step(): grad_rows = trade(grad_rot.reshape(hid_count, few, width), 'hid')]
  transfers between devices with their start and end apart: 12 -> 16, of which waited for: 6 -> 6; matrix products, arithmetic and copies ran while one was open for 13% -> 10% of each run, Pallas kernels for 0% -> 2%
where the time goes in v4:
time: 163 us; the launch traced here: 162 us
  starting transfers between devices  89.6 us (55%)
  waiting for transfers between devices  44.1 us (27%)
  matrix products  13.7 us (8%)
  other arithmetic  5.88 us (4%)
  local copies, waits for them, and re-layouts  5.1 us (3%)
  Pallas kernels  2.75 us (2%)
    ppermute x12, starting transfers between devices, partner(): return lax.ppermute(block, axis, [(s, s ^ bit) for s in range(count)])  64.8 us
    all_to_all x4, waiting for transfers between devices, trade(): return lax.all_to_all(block, axis, split_axis=0, concat_axis=0, tiled=True)  31.4 us
    all_to_all x4, starting transfers between devices, trade(): return lax.all_to_all(block, axis, split_axis=0, concat_axis=0, tiled=True)  24.8 us
    ppermute x12, waiting for transfers between devices, partner(): return lax.ppermute(block, axis, [(s, s ^ bit) for s in range(count)])  12.6 us
    dot_general x1, matrix products, step(): jnp.dot(weight_grad, factor, preferred_element_type=jnp.float32)  4.23 us
  transfers between devices with their start and end apart: 16, of which 6 were waited for; matrix products, arithmetic and copies ran while one was open for 10% of the time, Pallas kernels for 2%

profile of v4, /device:TPU:1, one launch (start us, length us, event | category | flops | bytes accessed | tf_op | source)
XLA Modules:
  0.0 162.1 jit_solution(7793580586249660071)
XLA Ops:
  2.3 5.5 %collective-permute-start = (bf16[256,896]{1,0:T(8,128)(2,1)S(1)}, bf16[256,896]{1,0:T(8,128)(2,1)}, u32[]{:S(2)}, u32[]{:S(2)}) collective-permute-start(bf16[256,896]{1,0:T(8,128)(2,1)S(1)} %fusion.1), channel_id=1, source_target_pairs={{0,1},{1,0},{2,3},{3,2},{4,5},{5,4},{6,7},{7,6},{8,9},{9,8},{10,11... | collective-permute-start | bytes 1376264 | tf_op jit(solution)/shard_map/ppermute | solution.py:21
  7.7 1.9 %collective-permute-start.1 = (bf16[56,896]{1,0:T(8,128)(2,1)}, bf16[56,896]{1,0:T(8,128)(2,1)S(1)}, u32[]{:S(2)}, u32[]{:S(2)}) collective-permute-start(bf16[56,896]{1,0:T(8,128)(2,1)} %param.13), channel_id=1, source_target_pairs={{0,1},{1,0},{2,3},{3,2},{4,5},{5,4},{6,7},{7,6},{8,9},{9,8},{10,11... | collective-permute-start | bytes 301064 | tf_op jit(solution)/shard_map/ppermute | solution.py:21
  10.6 15.7 %collective-permute-start.6 = (bf16[64,896]{1,0:T(8,128)(2,1)S(1)}, bf16[64,896]{1,0:T(8,128)(2,1)S(1)}, u32[]{:S(2)}, u32[]{:S(2)}) collective-permute-start(bf16[64,896]{1,0:T(8,128)(2,1)S(1)} %dynamic-slice_bitcast_fusion.4), channel_id=1, source_target_pairs={{0,256},{16,272},{32,288},{48,304},{64,320},{80,336},{96,352},{112... | collective-permute-start | bytes 344072 | tf_op jit(solution)/shard_map/ppermute | solution.py:21
  29.7 10.8 %collective-permute-start.7 = (bf16[64,896]{1,0:T(8,128)(2,1)S(1)}, bf16[64,896]{1,0:T(8,128)(2,1)S(1)}, u32[]{:S(2)}, u32[]{:S(2)}) collective-permute-start(bf16[64,896]{1,0:T(8,128)(2,1)S(1)} %fusion.7), channel_id=1, source_target_pairs={{0,128},{16,144},{32,160},{48,176},{64,192},{80,208},{96,224},{112... | collective-permute-start | bytes 344072 | tf_op jit(solution)/shard_map/ppermute | solution.py:21
  40.6 3.1 %collective-permute-start.2 = (bf16[1,56,896]{2,1,0:T(8,128)(2,1)S(1)}, bf16[1,56,896]{2,1,0:T(8,128)(2,1)S(1)}, u32[]{:S(2)}, u32[]{:S(2)}) collective-permute-start(bf16[1,56,896]{2,1,0:T(8,128)(2,1)S(1)} %select_bitcast_fusion), channel_id=1, source_target_pairs={{0,2},{2,0},{4,6},{6,4},{8,10},{10,8},{12,14},{14,12},{1,3},{3,1},... | collective-permute-start | bytes 301064 | tf_op jit(solution)/shard_map/ppermute | solution.py:21
  43.7 2.1 %collective-permute-done.7 = bf16[64,896]{1,0:T(8,128)(2,1)S(1)} collective-permute-done((bf16[64,896]{1,0:T(8,128)(2,1)S(1)}, bf16[64,896]{1,0:T(8,128)(2,1)S(1)}, u32[]{:S(2)}, u32[]{:S(2)}) %collective-permute-start.7) | collective-permute-done | bytes 114720 | tf_op jit(solution)/shard_map/ppermute | solution.py:21
  46.9 6.9 %collective-permute-start.8 = (f32[64,896]{1,0:T(8,128)S(1)}, f32[64,896]{1,0:T(8,128)}, u32[]{:S(2)}, u32[]{:S(2)}) collective-permute-start(f32[64,896]{1,0:T(8,128)S(1)} %multiply_add_fusion.3), channel_id=1, source_target_pairs={{0,64},{16,80},{32,96},{48,112},{64,0},{80,16},{96,32},{112,48},{1... | collective-permute-start | bytes 688136 | tf_op jit(solution)/shard_map/ppermute | solution.py:21
  53.8 2.4 %add_convert_fusion = bf16[512,896]{1,0:T(8,128)(2,1)} fusion(f32[512,896]{1,0:T(8,128)S(1)} %fusion.10, bf16[512,256]{1,0:T(8,128)(2,1)S(1)} %get-tuple-element.9, bf16[256,896]{1,0:T(8,128)(2,1)} %collective-permute-done), kind=kOutput, calls=%fused_computation | convolution fusion | flops 235798528 | bytes 3473408 | tf_op jit(solution)/shard_map/dot_general | solution.py:117
  56.2 5.1 %all-to-all-start = ((bf16[8,64,896]{2,1,0:T(8,128)(2,1)}), bf16[8,64,896]{2,1,0:T(8,128)(2,1)S(1)}, u32[]{:S(2)}, u32[]{:S(2)}) async-start(bf16[8,64,896]{2,1,0:T(8,128)(2,1)} %bitcast.4), calls=%async_computation | async-start | bytes 1835008 | tf_op jit(solution)/shard_map/all_to_all | solution.py:16
  61.3 3.4 %collective-permute-start.3 = (bf16[2,56,896]{2,1,0:T(8,128)(2,1)S(1)}, bf16[2,56,896]{2,1,0:T(8,128)(2,1)S(1)}, u32[]{:S(2)}, u32[]{:S(2)}) collective-permute-start(bf16[2,56,896]{2,1,0:T(8,128)(2,1)S(1)} %pad_maximum_fusion.2), channel_id=1, source_target_pairs={{0,4},{2,6},{4,0},{6,2},{8,12},{10,14},{12,8},{14,10},{1,5},{3,7},... | collective-permute-start | bytes 602120 | tf_op jit(solution)/shard_map/ppermute | solution.py:21
  67.6 8.6 %collective-permute-done.3 = bf16[2,56,896]{2,1,0:T(8,128)(2,1)S(1)} collective-permute-done((bf16[2,56,896]{2,1,0:T(8,128)(2,1)S(1)}, bf16[2,56,896]{2,1,0:T(8,128)(2,1)S(1)}, u32[]{:S(2)}, u32[]{:S(2)}) %collective-permute-start.3) | collective-permute-done | bytes 200736 | tf_op jit(solution)/shard_map/ppermute | solution.py:21
  76.2 4.0 %collective-permute-start.4 = (bf16[4,56,896]{2,1,0:T(8,128)(2,1)S(1)}, bf16[4,56,896]{2,1,0:T(8,128)(2,1)}, u32[]{:S(2)}, u32[]{:S(2)}) collective-permute-start(bf16[4,56,896]{2,1,0:T(8,128)(2,1)S(1)} %pad_maximum_fusion.1), channel_id=1, source_target_pairs={{0,8},{2,10},{4,12},{6,14},{8,0},{10,2},{12,4},{14,6},{1,9},{3,11}... | collective-permute-start | bytes 1204232 | tf_op jit(solution)/shard_map/ppermute | solution.py:21
  80.3 5.1 %collective-permute-start.10 = (f32[64,896]{1,0:T(8,128)S(1)}, f32[64,896]{1,0:T(8,128)}, u32[]{:S(2)}, u32[]{:S(2)}) collective-permute-start(f32[64,896]{1,0:T(8,128)S(1)} %multiply_add_fusion.1), channel_id=1, source_target_pairs={{0,16},{16,0},{32,48},{48,32},{64,80},{80,64},{96,112},{112,96},{1... | collective-permute-start | bytes 688136 | tf_op jit(solution)/shard_map/ppermute | solution.py:21
  86.2 9.8 %all-to-all-start.1 = ((bf16[32,2,896]{2,1,0:T(2,128)(2,1)}), bf16[32,2,896]{2,1,0:T(2,128)(2,1)S(1)}, u32[]{:S(2)}, u32[]{:S(2)}) async-start(bf16[32,2,896]{2,1,0:T(2,128)(2,1)} %reshape.36), calls=%async_computation.1 | async-start | bytes 229376 | tf_op jit(solution)/shard_map/all_to_all | solution.py:16
  97.1 2.1 %collective-permute-start.5 = (bf16[8,56,896]{2,1,0:T(8,128)(2,1)S(1)}, bf16[8,56,896]{2,1,0:T(8,128)(2,1)S(1)}, u32[]{:S(2)}, u32[]{:S(2)}) collective-permute-start(bf16[8,56,896]{2,1,0:T(8,128)(2,1)S(1)} %pad_maximum_fusion.mine), channel_id=1, source_target_pairs={{0,16},{16,0},{32,48},{48,32},{64,80},{80,64},{96,112},{112,96},{1... | collective-permute-start | bytes 2408456 | tf_op jit(solution)/shard_map/ppermute | solution.py:21
  100.3 10.9 %all-to-all-done.1 = bf16[32,2,896]{2,1,0:T(2,128)(2,1)S(1)} async-done(((bf16[32,2,896]{2,1,0:T(2,128)(2,1)}), bf16[32,2,896]{2,1,0:T(2,128)(2,1)S(1)}, u32[]{:S(2)}, u32[]{:S(2)}) %all-to-all-start.1) | async-done | bytes 114720 | tf_op jit(solution)/shard_map/all_to_all | solution.py:16
  112.2 3.6 %all-to-all-start.3 = ((bf16[8,64,896]{2,1,0:T(8,128)(2,1)}), bf16[8,64,896]{2,1,0:T(8,128)(2,1)S(1)}, u32[]{:S(2)}, u32[]{:S(2)}) async-start(bf16[8,64,896]{2,1,0:T(8,128)(2,1)} %broadcast_in_dim.14), calls=%async_computation.3 | async-start | bytes 1835008 | tf_op jit(solution)/shard_map/all_to_all | solution.py:16
  117.3 2.7 %shard_map.120 = bf16[8,2,56,896]{3,2,1,0:T(8,128)(2,1)} custom-call(s32[2]{0:T(128)} %pad_add_fusion.place, bf16[8,56,896]{2,1,0:T(8,128)(2,1)} %copy-done.1, bf16[8,56,896]{2,1,0:T(8,128)(2,1)} %copy-done.2), custom_call_target="tpu_custom_call" | custom-call | bytes 3211264 | tf_op jit(solution)/shard_map/pallas_call | solution.py:43
  120.1 2.0 %fusion.11 = f32[64,896]{1,0:T(8,128)S(1)} fusion(bf16[64,896]{1,0:T(8,128)(2,1)S(1)} %reshape.37, bf16[896,896]{1,0:T(8,128)(2,1)} %bitcast.41), kind=kOutput, calls=%fused_computation.37 | convolution fusion | flops 102760448 | bytes 1949696 | tf_op jit(solution)/shard_map/dot_general | solution.py:129
  122.1 6.4 %all-to-all-done.3 = bf16[8,64,896]{2,1,0:T(8,128)(2,1)S(1)} async-done(((bf16[8,64,896]{2,1,0:T(8,128)(2,1)}), bf16[8,64,896]{2,1,0:T(8,128)(2,1)S(1)}, u32[]{:S(2)}, u32[]{:S(2)}) %all-to-all-start.3) | async-done | bytes 917536 | tf_op jit(solution)/shard_map/all_to_all | solution.py:16
  129.7 4.5 %collective-permute-start.11 = (bf16[256,896]{1,0:T(8,128)(2,1)}, bf16[256,896]{1,0:T(8,128)(2,1)}, u32[]{:S(2)}, u32[]{:S(2)}) collective-permute-start(bf16[256,896]{1,0:T(8,128)(2,1)} %convolution_convert_fusion), channel_id=1, source_target_pairs={{0,1},{1,0},{2,3},{3,2},{4,5},{5,4},{6,7},{7,6},{8,9},{9,8},{10,11... | collective-permute-start | bytes 1376264 | tf_op jit(solution)/shard_map/ppermute | solution.py:21
  135.3 6.2 %all-to-all-start.2 = ((bf16[32,2,896]{2,1,0:T(2,128)(2,1)}), bf16[32,2,896]{2,1,0:T(2,128)(2,1)S(1)}, u32[]{:S(2)}, u32[]{:S(2)}) async-start(bf16[32,2,896]{2,1,0:T(2,128)(2,1)} %reshape.39), calls=%async_computation.2 | async-start | bytes 229376 | tf_op jit(solution)/shard_map/all_to_all | solution.py:16
  142.9 14.2 %all-to-all-done.2 = bf16[32,2,896]{2,1,0:T(2,128)(2,1)S(1)} async-done(((bf16[32,2,896]{2,1,0:T(2,128)(2,1)}), bf16[32,2,896]{2,1,0:T(2,128)(2,1)S(1)}, u32[]{:S(2)}, u32[]{:S(2)}) %all-to-all-start.2) | async-done | bytes 114720 | tf_op jit(solution)/shard_map/all_to_all | solution.py:16
  157.8 4.2 %fusion.6 = (bf16[256,896]{1,0:T(8,128)(2,1)}, bf16[256,896]{1,0:T(8,128)(2,1)}, bf16[256,896]{1,0:T(8,128)(2,1)}) fusion(bf16[256,896]{1,0:T(8,128)(2,1)} %param.15, bf16[256,896]{1,0:T(8,128)(2,1)} %param.14, bf16[896,896]{1,0:T(8,128)(2,1)S(1)} %bitcast.42, f32[256,896]{1,0:T(8,128)} %fusion.12, bf16[256,896]{1,0:T(8,128)(2,1)} %collective-permute-done.11, ...), kind=kOutput, calls=%fused_computation.17 | convolution fusion | flops 416317440 | bytes 6193152 | tf_op jit(solution)/shard_map/dot_general | solution.py:142
  (49 shorter events, 19.8 us)
Async XLA Ops:
  0.6 25.6 %copy-start.3 = (bf16[1,512,512]{2,1,0:T(8,128)(2,1)S(1)}, bf16[1,512,512]{2,1,0:T(8,128)(2,1)}, u32[]{:S(2)}) copy-start(bf16[1,512,512]{2,1,0:T(8,128)(2,1)} %param.10) | copy-start | bytes 1572868
  2.3 51.5 %collective-permute-start = (bf16[256,896]{1,0:T(8,128)(2,1)S(1)}, bf16[256,896]{1,0:T(8,128)(2,1)}, u32[]{:S(2)}, u32[]{:S(2)}) collective-permute-start(bf16[256,896]{1,0:T(8,128)(2,1)S(1)} %fusion.1), channel_id=1, source_target_pairs={{0,1},{1,0},{2,3},{3,2},{4,5},{5,4},{6,7},{7,6},{8,9},{9,8},{10,11... | collective-permute-start | bytes 1376264 | tf_op jit(solution)/shard_map/ppermute | solution.py:21
  7.7 32.8 %collective-permute-start.1 = (bf16[56,896]{1,0:T(8,128)(2,1)}, bf16[56,896]{1,0:T(8,128)(2,1)S(1)}, u32[]{:S(2)}, u32[]{:S(2)}) collective-permute-start(bf16[56,896]{1,0:T(8,128)(2,1)} %param.13), channel_id=1, source_target_pairs={{0,1},{1,0},{2,3},{3,2},{4,5},{5,4},{6,7},{7,6},{8,9},{9,8},{10,11... | collective-permute-start | bytes 301064 | tf_op jit(solution)/shard_map/ppermute | solution.py:21
  10.6 18.1 %collective-permute-start.6 = (bf16[64,896]{1,0:T(8,128)(2,1)S(1)}, bf16[64,896]{1,0:T(8,128)(2,1)S(1)}, u32[]{:S(2)}, u32[]{:S(2)}) collective-permute-start(bf16[64,896]{1,0:T(8,128)(2,1)S(1)} %dynamic-slice_bitcast_fusion.4), channel_id=1, source_target_pairs={{0,256},{16,272},{32,288},{48,304},{64,320},{80,336},{96,352},{112... | collective-permute-start | bytes 344072 | tf_op jit(solution)/shard_map/ppermute | solution.py:21
  26.4 14.2 %copy-start.5 = (bf16[56,896]{1,0:T(8,128)(2,1)S(1)}, bf16[56,896]{1,0:T(8,128)(2,1)}, u32[]{:S(2)}) copy-start(bf16[56,896]{1,0:T(8,128)(2,1)} %param.13) | copy-start | bytes 301060
  28.7 11.8 %copy-start.4 = (bf16[64,896]{1,0:T(8,128)(2,1)}, bf16[64,896]{1,0:T(8,128)(2,1)S(1)}, u32[]{:S(2)}) copy-start(bf16[64,896]{1,0:T(8,128)(2,1)S(1)} %collective-permute-done.6) | copy-start | bytes 344068
  29.7 16.1 %collective-permute-start.7 = (bf16[64,896]{1,0:T(8,128)(2,1)S(1)}, bf16[64,896]{1,0:T(8,128)(2,1)S(1)}, u32[]{:S(2)}, u32[]{:S(2)}) collective-permute-start(bf16[64,896]{1,0:T(8,128)(2,1)S(1)} %fusion.7), channel_id=1, source_target_pairs={{0,128},{16,144},{32,160},{48,176},{64,192},{80,208},{96,224},{112... | collective-permute-start | bytes 344072 | tf_op jit(solution)/shard_map/ppermute | solution.py:21
  40.6 20.7 %collective-permute-start.2 = (bf16[1,56,896]{2,1,0:T(8,128)(2,1)S(1)}, bf16[1,56,896]{2,1,0:T(8,128)(2,1)S(1)}, u32[]{:S(2)}, u32[]{:S(2)}) collective-permute-start(bf16[1,56,896]{2,1,0:T(8,128)(2,1)S(1)} %select_bitcast_fusion), channel_id=1, source_target_pairs={{0,2},{2,0},{4,6},{6,4},{8,10},{10,8},{12,14},{14,12},{1,3},{3,1},... | collective-permute-start | bytes 301064 | tf_op jit(solution)/shard_map/ppermute | solution.py:21
  46.9 17.8 %collective-permute-start.8 = (f32[64,896]{1,0:T(8,128)S(1)}, f32[64,896]{1,0:T(8,128)}, u32[]{:S(2)}, u32[]{:S(2)}) collective-permute-start(f32[64,896]{1,0:T(8,128)S(1)} %multiply_add_fusion.3), channel_id=1, source_target_pairs={{0,64},{16,80},{32,96},{48,112},{64,0},{80,16},{96,32},{112,48},{1... | collective-permute-start | bytes 688136 | tf_op jit(solution)/shard_map/ppermute | solution.py:21
  56.2 29.2 %all-to-all-start = ((bf16[8,64,896]{2,1,0:T(8,128)(2,1)}), bf16[8,64,896]{2,1,0:T(8,128)(2,1)S(1)}, u32[]{:S(2)}, u32[]{:S(2)}) async-start(bf16[8,64,896]{2,1,0:T(8,128)(2,1)} %bitcast.4), calls=%async_computation | async-start | bytes 1835008 | tf_op jit(solution)/shard_map/all_to_all | solution.py:16
  61.3 14.9 %collective-permute-start.3 = (bf16[2,56,896]{2,1,0:T(8,128)(2,1)S(1)}, bf16[2,56,896]{2,1,0:T(8,128)(2,1)S(1)}, u32[]{:S(2)}, u32[]{:S(2)}) collective-permute-start(bf16[2,56,896]{2,1,0:T(8,128)(2,1)S(1)} %pad_maximum_fusion.2), channel_id=1, source_target_pairs={{0,4},{2,6},{4,0},{6,2},{8,12},{10,14},{12,8},{14,10},{1,5},{3,7},... | collective-permute-start | bytes 602120 | tf_op jit(solution)/shard_map/ppermute | solution.py:21
  65.7 14.6 %collective-permute-start.9 = (f32[64,896]{1,0:T(8,128)S(1)}, f32[64,896]{1,0:T(8,128)S(1)}, u32[]{:S(2)}, u32[]{:S(2)}) collective-permute-start(f32[64,896]{1,0:T(8,128)S(1)} %multiply_add_fusion.2), channel_id=1, source_target_pairs={{0,32},{16,48},{32,0},{48,16},{64,96},{80,112},{96,64},{112,80},{1... | collective-permute-start | bytes 688136 | tf_op jit(solution)/shard_map/ppermute | solution.py:21
  76.2 19.8 %collective-permute-start.4 = (bf16[4,56,896]{2,1,0:T(8,128)(2,1)S(1)}, bf16[4,56,896]{2,1,0:T(8,128)(2,1)}, u32[]{:S(2)}, u32[]{:S(2)}) collective-permute-start(bf16[4,56,896]{2,1,0:T(8,128)(2,1)S(1)} %pad_maximum_fusion.1), channel_id=1, source_target_pairs={{0,8},{2,10},{4,12},{6,14},{8,0},{10,2},{12,4},{14,6},{1,9},{3,11}... | collective-permute-start | bytes 1204232 | tf_op jit(solution)/shard_map/ppermute | solution.py:21
  80.3 19.0 %collective-permute-start.10 = (f32[64,896]{1,0:T(8,128)S(1)}, f32[64,896]{1,0:T(8,128)}, u32[]{:S(2)}, u32[]{:S(2)}) collective-permute-start(f32[64,896]{1,0:T(8,128)S(1)} %multiply_add_fusion.1), channel_id=1, source_target_pairs={{0,16},{16,0},{32,48},{48,32},{64,80},{80,64},{96,112},{112,96},{1... | collective-permute-start | bytes 688136 | tf_op jit(solution)/shard_map/ppermute | solution.py:21
  86.2 25.0 %all-to-all-start.1 = ((bf16[32,2,896]{2,1,0:T(2,128)(2,1)}), bf16[32,2,896]{2,1,0:T(2,128)(2,1)S(1)}, u32[]{:S(2)}, u32[]{:S(2)}) async-start(bf16[32,2,896]{2,1,0:T(2,128)(2,1)} %reshape.36), calls=%async_computation.1 | async-start | bytes 229376 | tf_op jit(solution)/shard_map/all_to_all | solution.py:16
  97.1 15.1 %copy-start.1 = (bf16[8,56,896]{2,1,0:T(8,128)(2,1)}, bf16[8,56,896]{2,1,0:T(8,128)(2,1)S(1)}, u32[]{:S(2)}) copy-start(bf16[8,56,896]{2,1,0:T(8,128)(2,1)S(1)} %pad_maximum_fusion.mine) | copy-start | bytes 2408452
  97.1 19.2 %collective-permute-start.5 = (bf16[8,56,896]{2,1,0:T(8,128)(2,1)S(1)}, bf16[8,56,896]{2,1,0:T(8,128)(2,1)S(1)}, u32[]{:S(2)}, u32[]{:S(2)}) collective-permute-start(bf16[8,56,896]{2,1,0:T(8,128)(2,1)S(1)} %pad_maximum_fusion.mine), channel_id=1, source_target_pairs={{0,16},{16,0},{32,48},{48,32},{64,80},{80,64},{96,112},{112,96},{1... | collective-permute-start | bytes 2408456 | tf_op jit(solution)/shard_map/ppermute | solution.py:21
  112.2 16.3 %all-to-all-start.3 = ((bf16[8,64,896]{2,1,0:T(8,128)(2,1)}), bf16[8,64,896]{2,1,0:T(8,128)(2,1)S(1)}, u32[]{:S(2)}, u32[]{:S(2)}) async-start(bf16[8,64,896]{2,1,0:T(8,128)(2,1)} %broadcast_in_dim.14), calls=%async_computation.3 | async-start | bytes 1835008 | tf_op jit(solution)/shard_map/all_to_all | solution.py:16
  116.4 0.9 copy-start.2
  120.0 14.2 %copy-start.6 = (f32[64,64]{1,0:T(8,128)S(1)}, f32[64,64]{1,0:T(8,128)}, u32[]{:S(2)}) copy-start(f32[64,64]{1,0:T(8,128)} %constant.84.clone) | copy-start | bytes 49156
  129.7 28.1 %copy-start = (bf16[8,2,56,896]{3,2,1,0:T(8,128)(2,1)S(1)}, bf16[8,2,56,896]{3,2,1,0:T(8,128)(2,1)}, u32[]{:S(2)}) copy-start(bf16[8,2,56,896]{3,2,1,0:T(8,128)(2,1)} %shard_map.120) | copy-start | bytes 4816900
  129.7 28.1 %collective-permute-start.11 = (bf16[256,896]{1,0:T(8,128)(2,1)}, bf16[256,896]{1,0:T(8,128)(2,1)}, u32[]{:S(2)}, u32[]{:S(2)}) collective-permute-start(bf16[256,896]{1,0:T(8,128)(2,1)} %convolution_convert_fusion), channel_id=1, source_target_pairs={{0,1},{1,0},{2,3},{3,2},{4,5},{5,4},{6,7},{7,6},{8,9},{9,8},{10,11... | collective-permute-start | bytes 1376264 | tf_op jit(solution)/shard_map/ppermute | solution.py:21
  135.3 21.8 %all-to-all-start.2 = ((bf16[32,2,896]{2,1,0:T(2,128)(2,1)}), bf16[32,2,896]{2,1,0:T(2,128)(2,1)S(1)}, u32[]{:S(2)}, u32[]{:S(2)}) async-start(bf16[32,2,896]{2,1,0:T(2,128)(2,1)} %reshape.39), calls=%async_computation.2 | async-start | bytes 229376 | tf_op jit(solution)/shard_map/all_to_all | solution.py:16

commit v5 on v4

--- a/solution.py
+++ b/solution.py
@@ -80,11 +80,11 @@
     count = lax.axis_size("hid")
     total = block
     for bit in reversed(range(count.bit_length() - 1)):
-        sent = total if bit < 3 else total.astype(jnp.bfloat16)
+        sent = total if bit < 2 else total.astype(jnp.bfloat16)
         other = partner(sent, "hid", 1 << bit).astype(jnp.float32)
         sign = 1.0 - 2.0 * (where >> bit & 1).astype(jnp.float32)
         total = other + sign * total.astype(jnp.float32)
-    return (total / math.sqrt(count)).astype(jnp.bfloat16)
+    return total / math.sqrt(count)
 
 
 def step(x_act, out_grad, weight_codes, group_exps, local_factor, first_moment, second_moment):
@@ -99,7 +99,7 @@
     root = math.sqrt(hid_count)
 
     tokens = lax.dynamic_slice_in_dim(x_act[0], out_index * mine, mine, axis=0)
-    mixed = mix_blocks(tokens)
+    rows = trade(tokens.reshape(hid_count, few, width), "hid").reshape(mine, width)
 
     scales = jnp.exp2(group_exps.astype(jnp.float32)).astype(jnp.bfloat16)
     lanes = np.repeat(np.eye(width // GROUP, dtype=np.float32), GROUP, axis=1)
@@ -121,17 +121,21 @@
     pieces = trade(partial_rot, "out")
 
     grad_rot = pieces.astype(jnp.float32).sum(axis=0).astype(jnp.bfloat16)
-    grad_rows = trade(grad_rot.reshape(hid_count, few, width), "hid")
-    grad_rows = grad_rows.reshape(mine, width)
+    grad_mix = mix_blocks(grad_rot)
+
+    mixed = jnp.dot(signs.astype(jnp.bfloat16), rows, preferred_element_type=jnp.float32)
+    mixed = (mixed / root).astype(jnp.bfloat16).reshape(hid_count, few, width)
+    mixed = trade(mixed, "hid").reshape(mine, width)
     mixed = jnp.broadcast_to(mixed[None], (out_count, mine, width))
     mixed = trade(mixed, "out").reshape(token_count, width)
 
+    high = lax.reduce_precision(grad_mix, exponent_bits=8, mantissa_bits=7)
+    low = (grad_mix - high).astype(jnp.bfloat16)
+    across = (((1,), (1,)), ((), ()))
     back = lax.dot_general(
-        grad_rows, factor, (((1,), (1,)), ((), ())), preferred_element_type=jnp.float32
-    )
-    back = jnp.dot(signs, back, precision=lax.Precision.HIGHEST) / root
-    back = back.astype(jnp.bfloat16).reshape(hid_count, few, width)
-    input_grad = trade(back, "hid").reshape(1, mine, width)
+        high.astype(jnp.bfloat16), factor, across, preferred_element_type=jnp.float32
+    ) + lax.dot_general(low, factor, across, preferred_element_type=jnp.float32)
+    input_grad = back.astype(jnp.bfloat16)[None]
 
     away = jnp.dot(gt_other, mixed, preferred_element_type=jnp.float32)
     away = away.astype(jnp.bfloat16)

time: 163 us -> 162 us (level)
  waiting for transfers between devices: 44.1 us -> 58.6 us
  starting transfers between devices: 89.6 us -> 81.4 us
  matrix products: 13.7 us -> 9.79 us
  other arithmetic: 5.88 us -> 3.56 us
    ppermute x12, waiting for transfers between devices: 12.6 us -> 46.9 us  [partner(): return lax.ppermute(block, axis, [(s, s ^ bit) for s in range(count)])]
    all_to_all x4, waiting for transfers between devices: 31.4 us -> 11.6 us  [trade(): return lax.all_to_all(block, axis, split_axis=0, concat_axis=0, tiled=True)]
    ppermute x12, starting transfers between devices: 64.8 us -> 47.5 us  [partner(): return lax.ppermute(block, axis, [(s, s ^ bit) for s in range(count)])]
    all_to_all x4, starting transfers between devices: 24.8 us -> 34 us  [trade(): return lax.all_to_all(block, axis, split_axis=0, concat_axis=0, tiled=True)]
    dot_general x1, matrix products: 4.23 us -> 2.36 us  [step(): jnp.dot(weight_grad, factor, preferred_element_type=jnp.float32)]
  transfers between devices with their start and end apart: 16 -> 16, of which waited for: 6 -> 9; matrix products, arithmetic and copies ran while one was open for 10% -> 9% of each run, Pallas kernels for 2% -> 2%
where the time goes in v5:
time: 162 us
  starting transfers between devices  81.4 us (50%)
  waiting for transfers between devices  58.6 us (36%)
  matrix products  9.79 us (6%)
  local copies, waits for them, and re-layouts  4.36 us (3%)
  other arithmetic  3.56 us (2%)
  Pallas kernels  2.81 us (2%)
    ppermute x12, starting transfers between devices, partner(): return lax.ppermute(block, axis, [(s, s ^ bit) for s in range(count)])  47.5 us
    ppermute x12, waiting for transfers between devices, partner(): return lax.ppermute(block, axis, [(s, s ^ bit) for s in range(count)])  46.9 us
    all_to_all x4, starting transfers between devices, trade(): return lax.all_to_all(block, axis, split_axis=0, concat_axis=0, tiled=True)  34 us
    all_to_all x4, waiting for transfers between devices, trade(): return lax.all_to_all(block, axis, split_axis=0, concat_axis=0, tiled=True)  11.6 us
  transfers between devices with their start and end apart: 16, of which 9 were waited for; matrix products, arithmetic and copies ran while one was open for 9% of the time, Pallas kernels for 2%

profile of v5, /device:TPU:1, one launch (start us, length us, event | category | flops | bytes accessed | tf_op | source)
XLA Modules:
  0.0 161.6 jit_solution(9428930133049324636)
XLA Ops:
  0.7 5.6 %collective-permute-start.6 = (bf16[56,896]{1,0:T(8,128)(2,1)}, bf16[56,896]{1,0:T(8,128)(2,1)}, u32[]{:S(2)}, u32[]{:S(2)}) collective-permute-start(bf16[56,896]{1,0:T(8,128)(2,1)} %param.13), channel_id=1, source_target_pairs={{0,1},{1,0},{2,3},{3,2},{4,5},{5,4},{6,7},{7,6},{8,9},{9,8},{10,11... | collective-permute-start | bytes 301064 | tf_op jit(solution)/shard_map/ppermute | solution.py:21
  7.8 1.9 %collective-permute-start = (bf16[256,896]{1,0:T(8,128)(2,1)S(1)}, bf16[256,896]{1,0:T(8,128)(2,1)}, u32[]{:S(2)}, u32[]{:S(2)}) collective-permute-start(bf16[256,896]{1,0:T(8,128)(2,1)S(1)} %fusion.1), channel_id=1, source_target_pairs={{0,1},{1,0},{2,3},{3,2},{4,5},{5,4},{6,7},{7,6},{8,9},{9,8},{10,11... | collective-permute-start | bytes 1376264 | tf_op jit(solution)/shard_map/ppermute | solution.py:21
  10.5 16.7 %all-to-all-start.1 = ((bf16[32,2,896]{2,1,0:T(2,128)(2,1)}), bf16[32,2,896]{2,1,0:T(2,128)(2,1)}, u32[]{:S(2)}, u32[]{:S(2)}) async-start(bf16[32,2,896]{2,1,0:T(2,128)(2,1)} %reshape.35), calls=%async_computation.1 | async-start | bytes 229376 | tf_op jit(solution)/shard_map/all_to_all | solution.py:16
  28.6 2.5 %add_convert_fusion = bf16[512,896]{1,0:T(8,128)(2,1)} fusion(f32[512,896]{1,0:T(8,128)S(1)} %fusion.18, bf16[512,256]{1,0:T(8,128)(2,1)} %get-tuple-element.9, bf16[256,896]{1,0:T(8,128)(2,1)} %collective-permute-done), kind=kOutput, calls=%fused_computation | convolution fusion | flops 235798528 | bytes 3473408 | tf_op jit(solution)/shard_map/dot_general | solution.py:117
  31.1 11.4 %all-to-all-done.1 = bf16[32,2,896]{2,1,0:T(2,128)(2,1)} async-done(((bf16[32,2,896]{2,1,0:T(2,128)(2,1)}), bf16[32,2,896]{2,1,0:T(2,128)(2,1)}, u32[]{:S(2)}, u32[]{:S(2)}) %all-to-all-start.1) | async-done | bytes 114720 | tf_op jit(solution)/shard_map/all_to_all | solution.py:16
  42.4 5.2 %all-to-all-start = ((bf16[8,64,896]{2,1,0:T(8,128)(2,1)}), bf16[8,64,896]{2,1,0:T(8,128)(2,1)S(1)}, u32[]{:S(2)}, u32[]{:S(2)}) async-start(bf16[8,64,896]{2,1,0:T(8,128)(2,1)} %bitcast.40), calls=%async_computation | async-start | bytes 1835008 | tf_op jit(solution)/shard_map/all_to_all | solution.py:16
  48.6 3.4 %collective-permute-start.7 = (bf16[1,56,896]{2,1,0:T(8,128)(2,1)S(1)}, bf16[1,56,896]{2,1,0:T(8,128)(2,1)S(1)}, u32[]{:S(2)}, u32[]{:S(2)}) collective-permute-start(bf16[1,56,896]{2,1,0:T(8,128)(2,1)S(1)} %select_bitcast_fusion), channel_id=1, source_target_pairs={{0,2},{2,0},{4,6},{6,4},{8,10},{10,8},{12,14},{14,12},{1,3},{3,1},... | collective-permute-start | bytes 301064 | tf_op jit(solution)/shard_map/ppermute | solution.py:21
  52.0 8.4 %collective-permute-done.7 = bf16[1,56,896]{2,1,0:T(8,128)(2,1)S(1)} collective-permute-done((bf16[1,56,896]{2,1,0:T(8,128)(2,1)S(1)}, bf16[1,56,896]{2,1,0:T(8,128)(2,1)S(1)}, u32[]{:S(2)}, u32[]{:S(2)}) %collective-permute-start.7) | collective-permute-done | bytes 100384 | tf_op jit(solution)/shard_map/ppermute | solution.py:21
  60.4 3.2 %collective-permute-start.8 = (bf16[2,56,896]{2,1,0:T(8,128)(2,1)S(1)}, bf16[2,56,896]{2,1,0:T(8,128)(2,1)S(1)}, u32[]{:S(2)}, u32[]{:S(2)}) collective-permute-start(bf16[2,56,896]{2,1,0:T(8,128)(2,1)S(1)} %pad_maximum_fusion.2), channel_id=1, source_target_pairs={{0,4},{2,6},{4,0},{6,2},{8,12},{10,14},{12,8},{14,10},{1,5},{3,7},... | collective-permute-start | bytes 602120 | tf_op jit(solution)/shard_map/ppermute | solution.py:21
  63.6 3.3 %collective-permute-done.8 = bf16[2,56,896]{2,1,0:T(8,128)(2,1)S(1)} collective-permute-done((bf16[2,56,896]{2,1,0:T(8,128)(2,1)S(1)}, bf16[2,56,896]{2,1,0:T(8,128)(2,1)S(1)}, u32[]{:S(2)}, u32[]{:S(2)}) %collective-permute-start.8) | collective-permute-done | bytes 200736 | tf_op jit(solution)/shard_map/ppermute | solution.py:21
  66.9 4.6 %collective-permute-start.9 = (bf16[4,56,896]{2,1,0:T(8,128)(2,1)S(1)}, bf16[4,56,896]{2,1,0:T(8,128)(2,1)S(1)}, u32[]{:S(2)}, u32[]{:S(2)}) collective-permute-start(bf16[4,56,896]{2,1,0:T(8,128)(2,1)S(1)} %pad_maximum_fusion.1), channel_id=1, source_target_pairs={{0,8},{2,10},{4,12},{6,14},{8,0},{10,2},{12,4},{14,6},{1,9},{3,11}... | collective-permute-start | bytes 1204232 | tf_op jit(solution)/shard_map/ppermute | solution.py:21
  73.4 8.4 %all-to-all-start.2 = ((bf16[32,2,896]{2,1,0:T(2,128)(2,1)}), bf16[32,2,896]{2,1,0:T(2,128)(2,1)S(1)}, u32[]{:S(2)}, u32[]{:S(2)}) async-start(bf16[32,2,896]{2,1,0:T(2,128)(2,1)} %reshape.37), calls=%async_computation.2 | async-start | bytes 229376 | tf_op jit(solution)/shard_map/all_to_all | solution.py:16
  81.9 12.0 %collective-permute-start.1 = (bf16[64,896]{1,0:T(8,128)(2,1)S(1)}, bf16[64,896]{1,0:T(8,128)(2,1)S(1)}, u32[]{:S(2)}, u32[]{:S(2)}) collective-permute-start(bf16[64,896]{1,0:T(8,128)(2,1)S(1)} %reduce_sum.12), channel_id=1, source_target_pairs={{0,256},{16,272},{32,288},{48,304},{64,320},{80,336},{96,352},{112... | collective-permute-start | bytes 344072 | tf_op jit(solution)/shard_map/ppermute | solution.py:21
  94.1 2.6 %collective-permute-start.10 = (bf16[8,56,896]{2,1,0:T(8,128)(2,1)S(1)}, bf16[8,56,896]{2,1,0:T(8,128)(2,1)}, u32[]{:S(2)}, u32[]{:S(2)}) collective-permute-start(bf16[8,56,896]{2,1,0:T(8,128)(2,1)S(1)} %pad_maximum_fusion.mine), channel_id=1, source_target_pairs={{0,16},{16,0},{32,48},{48,32},{64,80},{80,64},{96,112},{112,96},{1... | collective-permute-start | bytes 2408456 | tf_op jit(solution)/shard_map/ppermute | solution.py:21
  98.0 3.6 %all-to-all-start.3 = ((bf16[8,64,896]{2,1,0:T(8,128)(2,1)}), bf16[8,64,896]{2,1,0:T(8,128)(2,1)S(1)}, u32[]{:S(2)}, u32[]{:S(2)}) async-start(bf16[8,64,896]{2,1,0:T(8,128)(2,1)} %broadcast_in_dim.20), calls=%async_computation.3 | async-start | bytes 1835008 | tf_op jit(solution)/shard_map/all_to_all | solution.py:16
  101.6 6.2 %collective-permute-done.1 = bf16[64,896]{1,0:T(8,128)(2,1)S(1)} collective-permute-done((bf16[64,896]{1,0:T(8,128)(2,1)S(1)}, bf16[64,896]{1,0:T(8,128)(2,1)S(1)}, u32[]{:S(2)}, u32[]{:S(2)}) %collective-permute-start.1) | collective-permute-done | bytes 114720 | tf_op jit(solution)/shard_map/ppermute | solution.py:21
  109.8 12.5 %collective-permute-done.2 = bf16[64,896]{1,0:T(8,128)(2,1)S(1)} collective-permute-done((bf16[64,896]{1,0:T(8,128)(2,1)S(1)}, bf16[64,896]{1,0:T(8,128)(2,1)S(1)}, u32[]{:S(2)}, u32[]{:S(2)}) %collective-permute-start.2) | collective-permute-done | bytes 114720 | tf_op jit(solution)/shard_map/ppermute | solution.py:21
  125.6 2.8 %shard_map.120 = bf16[8,2,56,896]{3,2,1,0:T(8,128)(2,1)} custom-call(s32[2]{0:T(128)} %pad_add_fusion.place, bf16[8,56,896]{2,1,0:T(8,128)(2,1)} %copy-done.2, bf16[8,56,896]{2,1,0:T(8,128)(2,1)} %collective-permute-done.10.other), custom_call_target="tpu_custom_call" | custom-call | bytes 3211264 | tf_op jit(solution)/shard_map/pallas_call | solution.py:43
  128.4 2.1 %collective-permute-done.3 = bf16[64,896]{1,0:T(8,128)(2,1)} collective-permute-done((bf16[64,896]{1,0:T(8,128)(2,1)}, bf16[64,896]{1,0:T(8,128)(2,1)}, u32[]{:S(2)}, u32[]{:S(2)}) %collective-permute-start.3) | collective-permute-done | bytes 114720 | tf_op jit(solution)/shard_map/ppermute | solution.py:21
  133.8 5.3 %collective-permute-done.4 = f32[64,896]{1,0:T(8,128)S(1)} collective-permute-done((f32[64,896]{1,0:T(8,128)S(1)}, f32[64,896]{1,0:T(8,128)S(1)}, u32[]{:S(2)}, u32[]{:S(2)}) %collective-permute-start.4) | collective-permute-done | bytes 229408 | tf_op jit(solution)/shard_map/ppermute | solution.py:21
  139.2 4.1 %collective-permute-start.5 = (f32[64,896]{1,0:T(8,128)S(1)}, f32[64,896]{1,0:T(8,128)S(1)}, u32[]{:S(2)}, u32[]{:S(2)}) collective-permute-start(f32[64,896]{1,0:T(8,128)S(1)} %multiply_add_fusion.1), channel_id=1, source_target_pairs={{0,16},{16,0},{32,48},{48,32},{64,80},{80,64},{96,112},{112,96},{1... | collective-permute-start | bytes 688136 | tf_op jit(solution)/shard_map/ppermute | solution.py:21
  143.7 4.4 %collective-permute-start.11 = (bf16[256,896]{1,0:T(8,128)(2,1)S(1)}, bf16[256,896]{1,0:T(8,128)(2,1)S(1)}, u32[]{:S(2)}, u32[]{:S(2)}) collective-permute-start(bf16[256,896]{1,0:T(8,128)(2,1)S(1)} %convolution_convert_fusion), channel_id=1, source_target_pairs={{0,1},{1,0},{2,3},{3,2},{4,5},{5,4},{6,7},{7,6},{8,9},{9,8},{10,11... | collective-permute-start | bytes 1376264 | tf_op jit(solution)/shard_map/ppermute | solution.py:21
  150.0 9.2 %collective-permute-done.11 = bf16[256,896]{1,0:T(8,128)(2,1)S(1)} collective-permute-done((bf16[256,896]{1,0:T(8,128)(2,1)S(1)}, bf16[256,896]{1,0:T(8,128)(2,1)S(1)}, u32[]{:S(2)}, u32[]{:S(2)}) %collective-permute-start.11) | collective-permute-done | bytes 458784 | tf_op jit(solution)/shard_map/ppermute | solution.py:21
  159.2 2.4 %fusion.8 = (bf16[256,896]{1,0:T(8,128)(2,1)}, bf16[256,896]{1,0:T(8,128)(2,1)}, bf16[256,896]{1,0:T(8,128)(2,1)}) fusion(bf16[256,896]{1,0:T(8,128)(2,1)S(1)} %copy-done.8, bf16[256,896]{1,0:T(8,128)(2,1)S(1)} %copy-done.9, bf16[896,896]{1,0:T(8,128)(2,1)S(1)} %bitcast.37, f32[256,896]{1,0:T(8,128)S(1)} %fusion.19, ...), kind=kOutput, calls=%fused_computation.20 | convolution fusion | flops 416317440 | bytes 6193152 | tf_op jit(solution)/shard_map/dot_general | solution.py:146
  (55 shorter events, 18.9 us)
Async XLA Ops:
  0.6 26.6 %copy-start.5 = (bf16[1,512,512]{2,1,0:T(8,128)(2,1)S(1)}, bf16[1,512,512]{2,1,0:T(8,128)(2,1)}, u32[]{:S(2)}) copy-start(bf16[1,512,512]{2,1,0:T(8,128)(2,1)} %param.10) | copy-start | bytes 1572868
  0.7 47.0 %collective-permute-start.6 = (bf16[56,896]{1,0:T(8,128)(2,1)}, bf16[56,896]{1,0:T(8,128)(2,1)}, u32[]{:S(2)}, u32[]{:S(2)}) collective-permute-start(bf16[56,896]{1,0:T(8,128)(2,1)} %param.13), channel_id=1, source_target_pairs={{0,1},{1,0},{2,3},{3,2},{4,5},{5,4},{6,7},{7,6},{8,9},{9,8},{10,11... | collective-permute-start | bytes 301064 | tf_op jit(solution)/shard_map/ppermute | solution.py:21
  7.8 20.7 %collective-permute-start = (bf16[256,896]{1,0:T(8,128)(2,1)S(1)}, bf16[256,896]{1,0:T(8,128)(2,1)}, u32[]{:S(2)}, u32[]{:S(2)}) collective-permute-start(bf16[256,896]{1,0:T(8,128)(2,1)S(1)} %fusion.1), channel_id=1, source_target_pairs={{0,1},{1,0},{2,3},{3,2},{4,5},{5,4},{6,7},{7,6},{8,9},{9,8},{10,11... | collective-permute-start | bytes 1376264 | tf_op jit(solution)/shard_map/ppermute | solution.py:21
  10.5 31.9 %all-to-all-start.1 = ((bf16[32,2,896]{2,1,0:T(2,128)(2,1)}), bf16[32,2,896]{2,1,0:T(2,128)(2,1)}, u32[]{:S(2)}, u32[]{:S(2)}) async-start(bf16[32,2,896]{2,1,0:T(2,128)(2,1)} %reshape.35), calls=%async_computation.1 | async-start | bytes 229376 | tf_op jit(solution)/shard_map/all_to_all | solution.py:16
  31.1 16.6 %copy-start.6 = (bf16[56,896]{1,0:T(8,128)(2,1)S(1)}, bf16[56,896]{1,0:T(8,128)(2,1)}, u32[]{:S(2)}) copy-start(bf16[56,896]{1,0:T(8,128)(2,1)} %param.13) | copy-start | bytes 301060
  42.4 30.0 %copy-start.7 = (bf16[64,64]{1,0:T(8,128)(2,1)S(1)}, bf16[64,64]{1,0:T(8,128)(2,1)}, u32[]{:S(2)}) copy-start(bf16[64,64]{1,0:T(8,128)(2,1)} %constant.84.clone) | copy-start | bytes 24580
  42.4 30.9 %all-to-all-start = ((bf16[8,64,896]{2,1,0:T(8,128)(2,1)}), bf16[8,64,896]{2,1,0:T(8,128)(2,1)S(1)}, u32[]{:S(2)}, u32[]{:S(2)}) async-start(bf16[8,64,896]{2,1,0:T(8,128)(2,1)} %bitcast.40), calls=%async_computation | async-start | bytes 1835008 | tf_op jit(solution)/shard_map/all_to_all | solution.py:16
  48.6 11.7 %collective-permute-start.7 = (bf16[1,56,896]{2,1,0:T(8,128)(2,1)S(1)}, bf16[1,56,896]{2,1,0:T(8,128)(2,1)S(1)}, u32[]{:S(2)}, u32[]{:S(2)}) collective-permute-start(bf16[1,56,896]{2,1,0:T(8,128)(2,1)S(1)} %select_bitcast_fusion), channel_id=1, source_target_pairs={{0,2},{2,0},{4,6},{6,4},{8,10},{10,8},{12,14},{14,12},{1,3},{3,1},... | collective-permute-start | bytes 301064 | tf_op jit(solution)/shard_map/ppermute | solution.py:21
  60.4 6.5 %collective-permute-start.8 = (bf16[2,56,896]{2,1,0:T(8,128)(2,1)S(1)}, bf16[2,56,896]{2,1,0:T(8,128)(2,1)S(1)}, u32[]{:S(2)}, u32[]{:S(2)}) collective-permute-start(bf16[2,56,896]{2,1,0:T(8,128)(2,1)S(1)} %pad_maximum_fusion.2), channel_id=1, source_target_pairs={{0,4},{2,6},{4,0},{6,2},{8,12},{10,14},{12,8},{14,10},{1,5},{3,7},... | collective-permute-start | bytes 602120 | tf_op jit(solution)/shard_map/ppermute | solution.py:21
  66.9 27.1 %collective-permute-start.9 = (bf16[4,56,896]{2,1,0:T(8,128)(2,1)S(1)}, bf16[4,56,896]{2,1,0:T(8,128)(2,1)S(1)}, u32[]{:S(2)}, u32[]{:S(2)}) collective-permute-start(bf16[4,56,896]{2,1,0:T(8,128)(2,1)S(1)} %pad_maximum_fusion.1), channel_id=1, source_target_pairs={{0,8},{2,10},{4,12},{6,14},{8,0},{10,2},{12,4},{14,6},{1,9},{3,11}... | collective-permute-start | bytes 1204232 | tf_op jit(solution)/shard_map/ppermute | solution.py:21
  73.4 23.6 %all-to-all-start.2 = ((bf16[32,2,896]{2,1,0:T(2,128)(2,1)}), bf16[32,2,896]{2,1,0:T(2,128)(2,1)S(1)}, u32[]{:S(2)}, u32[]{:S(2)}) async-start(bf16[32,2,896]{2,1,0:T(2,128)(2,1)} %reshape.37), calls=%async_computation.2 | async-start | bytes 229376 | tf_op jit(solution)/shard_map/all_to_all | solution.py:16
  81.9 25.8 %collective-permute-start.1 = (bf16[64,896]{1,0:T(8,128)(2,1)S(1)}, bf16[64,896]{1,0:T(8,128)(2,1)S(1)}, u32[]{:S(2)}, u32[]{:S(2)}) collective-permute-start(bf16[64,896]{1,0:T(8,128)(2,1)S(1)} %reduce_sum.12), channel_id=1, source_target_pairs={{0,256},{16,272},{32,288},{48,304},{64,320},{80,336},{96,352},{112... | collective-permute-start | bytes 344072 | tf_op jit(solution)/shard_map/ppermute | solution.py:21
  94.1 13.8 %copy-start.2 = (bf16[8,56,896]{2,1,0:T(8,128)(2,1)}, bf16[8,56,896]{2,1,0:T(8,128)(2,1)S(1)}, u32[]{:S(2)}) copy-start(bf16[8,56,896]{2,1,0:T(8,128)(2,1)S(1)} %pad_maximum_fusion.mine) | copy-start | bytes 2408452
  94.1 31.5 %collective-permute-start.10 = (bf16[8,56,896]{2,1,0:T(8,128)(2,1)S(1)}, bf16[8,56,896]{2,1,0:T(8,128)(2,1)}, u32[]{:S(2)}, u32[]{:S(2)}) collective-permute-start(bf16[8,56,896]{2,1,0:T(8,128)(2,1)S(1)} %pad_maximum_fusion.mine), channel_id=1, source_target_pairs={{0,16},{16,0},{32,48},{48,32},{64,80},{80,64},{96,112},{112,96},{1... | collective-permute-start | bytes 2408456 | tf_op jit(solution)/shard_map/ppermute | solution.py:21
  98.0 35.3 %all-to-all-start.3 = ((bf16[8,64,896]{2,1,0:T(8,128)(2,1)}), bf16[8,64,896]{2,1,0:T(8,128)(2,1)S(1)}, u32[]{:S(2)}, u32[]{:S(2)}) async-start(bf16[8,64,896]{2,1,0:T(8,128)(2,1)} %broadcast_in_dim.20), calls=%async_computation.3 | async-start | bytes 1835008 | tf_op jit(solution)/shard_map/all_to_all | solution.py:16
  107.8 14.5 %collective-permute-start.2 = (bf16[64,896]{1,0:T(8,128)(2,1)S(1)}, bf16[64,896]{1,0:T(8,128)(2,1)S(1)}, u32[]{:S(2)}, u32[]{:S(2)}) collective-permute-start(bf16[64,896]{1,0:T(8,128)(2,1)S(1)} %fusion.10), channel_id=1, source_target_pairs={{0,128},{16,144},{32,160},{48,176},{64,192},{80,208},{96,224},{112... | collective-permute-start | bytes 344072 | tf_op jit(solution)/shard_map/ppermute | solution.py:21
  123.0 7.4 %collective-permute-start.3 = (bf16[64,896]{1,0:T(8,128)(2,1)}, bf16[64,896]{1,0:T(8,128)(2,1)}, u32[]{:S(2)}, u32[]{:S(2)}) collective-permute-start(bf16[64,896]{1,0:T(8,128)(2,1)} %fusion.11), channel_id=1, source_target_pairs={{0,64},{16,80},{32,96},{48,112},{64,0},{80,16},{96,32},{112,48},{1... | collective-permute-start | bytes 344072 | tf_op jit(solution)/shard_map/ppermute | solution.py:21
  131.4 7.8 %collective-permute-start.4 = (f32[64,896]{1,0:T(8,128)S(1)}, f32[64,896]{1,0:T(8,128)S(1)}, u32[]{:S(2)}, u32[]{:S(2)}) collective-permute-start(f32[64,896]{1,0:T(8,128)S(1)} %multiply_add_fusion.2), channel_id=1, source_target_pairs={{0,32},{16,48},{32,0},{48,16},{64,96},{80,112},{96,64},{112,80},{1... | collective-permute-start | bytes 688136 | tf_op jit(solution)/shard_map/ppermute | solution.py:21
  133.8 14.3 %copy-start.1 = (bf16[8,2,56,896]{3,2,1,0:T(8,128)(2,1)S(1)}, bf16[8,2,56,896]{3,2,1,0:T(8,128)(2,1)}, u32[]{:S(2)}) copy-start(bf16[8,2,56,896]{3,2,1,0:T(8,128)(2,1)} %shard_map.120) | copy-start | bytes 4816900
  139.2 8.9 %collective-permute-start.5 = (f32[64,896]{1,0:T(8,128)S(1)}, f32[64,896]{1,0:T(8,128)S(1)}, u32[]{:S(2)}, u32[]{:S(2)}) collective-permute-start(f32[64,896]{1,0:T(8,128)S(1)} %multiply_add_fusion.1), channel_id=1, source_target_pairs={{0,16},{16,0},{32,48},{48,32},{64,80},{80,64},{96,112},{112,96},{1... | collective-permute-start | bytes 688136 | tf_op jit(solution)/shard_map/ppermute | solution.py:21
  143.7 15.5 %collective-permute-start.11 = (bf16[256,896]{1,0:T(8,128)(2,1)S(1)}, bf16[256,896]{1,0:T(8,128)(2,1)S(1)}, u32[]{:S(2)}, u32[]{:S(2)}) collective-permute-start(bf16[256,896]{1,0:T(8,128)(2,1)S(1)} %convolution_convert_fusion), channel_id=1, source_target_pairs={{0,1},{1,0},{2,3},{3,2},{4,5},{5,4},{6,7},{7,6},{8,9},{9,8},{10,11... | collective-permute-start | bytes 1376264 | tf_op jit(solution)/shard_map/ppermute | solution.py:21
  148.7 10.5 %copy-start.4 = (s32[256,896]{1,0:T(8,128)S(1)}, s32[256,896]{1,0:T(8,128)}, u32[]{:S(2)}) copy-start(s32[256,896]{1,0:T(8,128)} %param.11) | copy-start | bytes 2752516
  148.7 10.5 %copy-start.8 = (bf16[256,896]{1,0:T(8,128)(2,1)S(1)}, bf16[256,896]{1,0:T(8,128)(2,1)}, u32[]{:S(2)}) copy-start(bf16[256,896]{1,0:T(8,128)(2,1)} %param.15) | copy-start | bytes 1376260
  148.7 10.5 %copy-start.9 = (bf16[256,896]{1,0:T(8,128)(2,1)S(1)}, bf16[256,896]{1,0:T(8,128)(2,1)}, u32[]{:S(2)}) copy-start(bf16[256,896]{1,0:T(8,128)(2,1)} %param.14) | copy-start | bytes 1376260
  (2 other events, 16.9 us)

commit v6 on v5

--- a/solution.py
+++ b/solution.py
@@ -19,6 +19,34 @@
 def partner(block, axis, bit):
     count = lax.axis_size(axis)
     return lax.ppermute(block, axis, [(s, s ^ bit) for s in range(count)])
+
+
+KERNEL_VMEM = pltpu.CompilerParams(vmem_limit_bytes=8 * 1024 * 1024)
+
+
+def dequant_kernel(codes, exps, factor, out):
+    rows = codes.shape[0]
+    scales = jnp.exp2(exps[...].astype(jnp.float32))
+    for group in range(exps.shape[1]):
+        lanes = slice(group * GROUP, (group + 1) * GROUP)
+        values = codes[:, lanes].astype(jnp.float32) * scales[:, group : group + 1]
+        out[0:rows, lanes] = values.astype(out.dtype)
+    out[rows:, :] = factor[...]
+
+
+def dequantize(codes, exps, factor):
+    rows, width = codes.shape
+    whole = pl.BlockSpec(memory_space=pltpu.VMEM)
+    return pl.pallas_call(
+        dequant_kernel,
+        out_shape=jax.ShapeDtypeStruct((rows + factor.shape[0], width), factor.dtype),
+        in_specs=[whole] * 3,
+        out_specs=whole,
+        compiler_params=KERNEL_VMEM,
+        cost_estimate=pl.CostEstimate(
+            flops=2 * rows * width, bytes_accessed=6 * rows * width, transcendentals=0
+        ),
+    )(codes, exps, factor)
 
 
 def order_kernel(place, mine, other, out):
@@ -45,6 +73,7 @@
         out_shape=jax.ShapeDtypeStruct((count, 2, rows, width), mine.dtype),
         in_specs=[pl.BlockSpec(memory_space=pltpu.SMEM), whole, whole],
         out_specs=whole,
+        compiler_params=KERNEL_VMEM,
         cost_estimate=pl.CostEstimate(
             flops=0, bytes_accessed=8 * count * rows * width, transcendentals=0
         ),
@@ -62,11 +91,10 @@
     return ((1 - 2 * parity) * same).astype(np.float32)
 
 
-def gather_factor(local_factor):
+def gather_factor(local_factor, other):
     core, spot = lax.axis_index("hid") % 2, lax.axis_index("out")
     _, width = local_factor.shape
     bits = lax.axis_size("out").bit_length() - 1
-    other = partner(local_factor, "rep", 1)
     block = jnp.where(core == lax.axis_index("rep"), local_factor, other)[None]
     for bit in range(bits):
         other = partner(block, "out", 1 << bit)
@@ -101,12 +129,10 @@
     tokens = lax.dynamic_slice_in_dim(x_act[0], out_index * mine, mine, axis=0)
     rows = trade(tokens.reshape(hid_count, few, width), "hid").reshape(mine, width)
 
-    scales = jnp.exp2(group_exps.astype(jnp.float32)).astype(jnp.bfloat16)
-    lanes = np.repeat(np.eye(width // GROUP, dtype=np.float32), GROUP, axis=1)
-    scales = jnp.dot(scales, lanes.astype(jnp.bfloat16), preferred_element_type=jnp.float32)
-    w_deq = (weight_codes.astype(jnp.float32) * scales).astype(jnp.bfloat16)
-    w_other = partner(w_deq, "rep", 1)
-    factor = gather_factor(local_factor)
+    sent = dequantize(weight_codes, group_exps, local_factor)
+    arrived = partner(sent, "rep", 1)
+    w_deq, w_other = sent[:code_rows], arrived[:code_rows]
+    factor = gather_factor(local_factor, arrived[code_rows:])
 
     grads_t = grads_out.T
     g_own = lax.dynamic_slice_in_dim(grads_out, rep_index * code_rows, code_rows, axis=1)

time: 162 us -> 151 us (0.932)
  waiting for transfers between devices: 58.6 us -> 43.1 us
  starting transfers between devices: 81.4 us -> 84.6 us
  local copies, waits for them, and re-layouts: 4.36 us -> 7.54 us
  Pallas kernels: 2.81 us -> 1.03 us
    ppermute x12 -> x11, waiting for transfers between devices: 46.9 us -> 23.5 us  [partner(): return lax.ppermute(block, axis, [(s, s ^ bit) for s in range(count)])]
    all_to_all x4, waiting for transfers between devices: 11.6 us -> 19.6 us  [trade(): return lax.all_to_all(block, axis, split_axis=0, concat_axis=0, tiled=True)]
    ppermute x12 -> x11, starting transfers between devices: 47.5 us -> 54 us  [partner(): return lax.ppermute(block, axis, [(s, s ^ bit) for s in range(count)])]
    unnamed x20 -> x35, local copies, waits for them, and re-layouts: 0.05 us -> 4.13 us
    all_to_all x4, starting transfers between devices: 34 us -> 30.6 us  [trade(): return lax.all_to_all(block, axis, split_axis=0, concat_axis=0, tiled=True)]
    pallas_call x1, Pallas kernels: 2.81 us -> 0.72 us  [in_order(): pl.pallas_call(order_kernel, out_shape=jax.ShapeDtypeStruct((count, 2, ro...]
    concatenate x3, other arithmetic: 0.18 us -> 1.96 us  [gather_factor(): block = jnp.concatenate([block, other], axis=0)]
  transfers between devices with their start and end apart: 16 -> 15, of which waited for: 9 -> 5; matrix products, arithmetic and copies ran while one was open for 9% -> 10% of each run, Pallas kernels for 2% -> 1%
where the time goes in v6:
time: 151 us
  starting transfers between devices  84.6 us (56%)
  waiting for transfers between devices  43.1 us (29%)
  matrix products  8.17 us (5%)
  local copies, waits for them, and re-layouts  7.54 us (5%)
  other arithmetic  4.89 us (3%)
    ppermute x11, starting transfers between devices, partner(): return lax.ppermute(block, axis, [(s, s ^ bit) for s in range(count)])  54 us
    all_to_all x4, starting transfers between devices, trade(): return lax.all_to_all(block, axis, split_axis=0, concat_axis=0, tiled=True)  30.6 us
    ppermute x11, waiting for transfers between devices, partner(): return lax.ppermute(block, axis, [(s, s ^ bit) for s in range(count)])  23.5 us
    all_to_all x4, waiting for transfers between devices, trade(): return lax.all_to_all(block, axis, split_axis=0, concat_axis=0, tiled=True)  19.6 us
    unnamed x35, local copies, waits for them, and re-layouts  4.13 us
  transfers between devices with their start and end apart: 15, of which 5 were waited for; matrix products, arithmetic and copies ran while one was open for 10% of the time, Pallas kernels for 1%

profile of v6, /device:TPU:1, one launch (start us, length us, event | category | flops | bytes accessed | tf_op | source)
XLA Modules:
  0.0 150.5 jit_solution(14513341149013813113)
XLA Ops:
  2.5 16.7 %all-to-all-start.1 = ((bf16[32,2,896]{2,1,0:T(2,128)(2,1)}), bf16[32,2,896]{2,1,0:T(2,128)(2,1)S(1)}, u32[]{:S(2)}, u32[]{:S(2)}) async-start(bf16[32,2,896]{2,1,0:T(2,128)(2,1)} %reshape.35), calls=%async_computation.1 | async-start | bytes 229376 | tf_op jit(solution)/shard_map/all_to_all | solution.py:16
  22.5 4.7 %collective-permute-start = (bf16[312,896]{1,0:T(8,128)(2,1)S(1)}, bf16[312,896]{1,0:T(8,128)(2,1)S(1)}, u32[]{:S(2)}, u32[]{:S(2)}) collective-permute-start(bf16[312,896]{1,0:T(8,128)(2,1)S(1)} %shard_map.111), channel_id=1, source_target_pairs={{0,1},{1,0},{2,3},{3,2},{4,5},{5,4},{6,7},{7,6},{8,9},{9,8},{10,11... | collective-permute-start | bytes 1677320 | tf_op jit(solution)/shard_map/ppermute | solution.py:21
  28.0 6.3 %all-to-all-done.1 = bf16[32,2,896]{2,1,0:T(2,128)(2,1)S(1)} async-done(((bf16[32,2,896]{2,1,0:T(2,128)(2,1)}), bf16[32,2,896]{2,1,0:T(2,128)(2,1)S(1)}, u32[]{:S(2)}, u32[]{:S(2)}) %all-to-all-start.1) | async-done | bytes 114720 | tf_op jit(solution)/shard_map/all_to_all | solution.py:16
  35.3 6.1 %all-to-all-start.2 = ((bf16[32,2,896]{2,1,0:T(2,128)(2,1)}), bf16[32,2,896]{2,1,0:T(2,128)(2,1)S(1)}, u32[]{:S(2)}, u32[]{:S(2)}) async-start(bf16[32,2,896]{2,1,0:T(2,128)(2,1)} %reshape.37), calls=%async_computation.2 | async-start | bytes 229376 | tf_op jit(solution)/shard_map/all_to_all | solution.py:16
  41.9 1.4 add_convert_fusion
  43.3 13.3 %all-to-all-done.2 = bf16[32,2,896]{2,1,0:T(2,128)(2,1)S(1)} async-done(((bf16[32,2,896]{2,1,0:T(2,128)(2,1)}), bf16[32,2,896]{2,1,0:T(2,128)(2,1)S(1)}, u32[]{:S(2)}, u32[]{:S(2)}) %all-to-all-start.2) | async-done | bytes 114720 | tf_op jit(solution)/shard_map/all_to_all | solution.py:16
  56.6 4.2 %all-to-all-start = ((bf16[8,64,896]{2,1,0:T(8,128)(2,1)}), bf16[8,64,896]{2,1,0:T(8,128)(2,1)S(1)}, u32[]{:S(2)}, u32[]{:S(2)}) async-start(bf16[8,64,896]{2,1,0:T(8,128)(2,1)} %bitcast.37), calls=%async_computation | async-start | bytes 1835008 | tf_op jit(solution)/shard_map/all_to_all | solution.py:16
  60.8 3.4 %collective-permute-start.6 = (bf16[1,56,896]{2,1,0:T(8,128)(2,1)S(1)}, bf16[1,56,896]{2,1,0:T(8,128)(2,1)S(1)}, u32[]{:S(2)}, u32[]{:S(2)}) collective-permute-start(bf16[1,56,896]{2,1,0:T(8,128)(2,1)S(1)} %fusion.16), channel_id=1, source_target_pairs={{0,2},{2,0},{4,6},{6,4},{8,10},{10,8},{12,14},{14,12},{1,3},{3,1},... | collective-permute-start | bytes 301064 | tf_op jit(solution)/shard_map/ppermute | solution.py:21
  64.2 9.3 %collective-permute-done.6 = bf16[1,56,896]{2,1,0:T(8,128)(2,1)S(1)} collective-permute-done((bf16[1,56,896]{2,1,0:T(8,128)(2,1)S(1)}, bf16[1,56,896]{2,1,0:T(8,128)(2,1)S(1)}, u32[]{:S(2)}, u32[]{:S(2)}) %collective-permute-start.6) | collective-permute-done | bytes 100384 | tf_op jit(solution)/shard_map/ppermute | solution.py:21
  73.5 3.2 %collective-permute-start.7 = (bf16[2,56,896]{2,1,0:T(8,128)(2,1)S(1)}, bf16[2,56,896]{2,1,0:T(8,128)(2,1)S(1)}, u32[]{:S(2)}, u32[]{:S(2)}) collective-permute-start(bf16[2,56,896]{2,1,0:T(8,128)(2,1)S(1)} %pad_maximum_fusion.2), channel_id=1, source_target_pairs={{0,4},{2,6},{4,0},{6,2},{8,12},{10,14},{12,8},{14,10},{1,5},{3,7},... | collective-permute-start | bytes 602120 | tf_op jit(solution)/shard_map/ppermute | solution.py:21
  77.8 3.6 %all-to-all-start.3 = ((bf16[8,64,896]{2,1,0:T(8,128)(2,1)}), bf16[8,64,896]{2,1,0:T(8,128)(2,1)S(1)}, u32[]{:S(2)}, u32[]{:S(2)}) async-start(bf16[8,64,896]{2,1,0:T(8,128)(2,1)} %broadcast_in_dim.20), calls=%async_computation.3 | async-start | bytes 1835008 | tf_op jit(solution)/shard_map/all_to_all | solution.py:16
  82.2 4.8 %collective-permute-start.8 = (bf16[4,56,896]{2,1,0:T(8,128)(2,1)}, bf16[4,56,896]{2,1,0:T(8,128)(2,1)}, u32[]{:S(2)}, u32[]{:S(2)}) collective-permute-start(bf16[4,56,896]{2,1,0:T(8,128)(2,1)} %pad_maximum_fusion.1), channel_id=1, source_target_pairs={{0,8},{2,10},{4,12},{6,14},{8,0},{10,2},{12,4},{14,6},{1,9},{3,11}... | collective-permute-start | bytes 1204232 | tf_op jit(solution)/shard_map/ppermute | solution.py:21
  87.1 4.4 %collective-permute-start.1 = (bf16[64,896]{1,0:T(8,128)(2,1)S(1)}, bf16[64,896]{1,0:T(8,128)(2,1)S(1)}, u32[]{:S(2)}, u32[]{:S(2)}) collective-permute-start(bf16[64,896]{1,0:T(8,128)(2,1)S(1)} %reduce_sum.12), channel_id=1, source_target_pairs={{0,256},{16,272},{32,288},{48,304},{64,320},{80,336},{96,352},{112... | collective-permute-start | bytes 344072 | tf_op jit(solution)/shard_map/ppermute | solution.py:21
  91.6 10.2 %collective-permute-done.1 = bf16[64,896]{1,0:T(8,128)(2,1)S(1)} collective-permute-done((bf16[64,896]{1,0:T(8,128)(2,1)S(1)}, bf16[64,896]{1,0:T(8,128)(2,1)S(1)}, u32[]{:S(2)}, u32[]{:S(2)}) %collective-permute-start.1) | collective-permute-done | bytes 114720 | tf_op jit(solution)/shard_map/ppermute | solution.py:21
  101.9 4.8 %collective-permute-start.2 = (bf16[64,896]{1,0:T(8,128)(2,1)S(1)}, bf16[64,896]{1,0:T(8,128)(2,1)S(1)}, u32[]{:S(2)}, u32[]{:S(2)}) collective-permute-start(bf16[64,896]{1,0:T(8,128)(2,1)S(1)} %fusion.12), channel_id=1, source_target_pairs={{0,128},{16,144},{32,160},{48,176},{64,192},{80,208},{96,224},{112... | collective-permute-start | bytes 344072 | tf_op jit(solution)/shard_map/ppermute | solution.py:21
  107.9 8.6 %collective-permute-start.9 = (bf16[8,56,896]{2,1,0:T(8,128)(2,1)S(1)}, bf16[8,56,896]{2,1,0:T(8,128)(2,1)S(1)}, u32[]{:S(2)}, u32[]{:S(2)}) collective-permute-start(bf16[8,56,896]{2,1,0:T(8,128)(2,1)S(1)} %pad_maximum_fusion.mine), channel_id=1, source_target_pairs={{0,16},{16,0},{32,48},{48,32},{64,80},{80,64},{96,112},{112,96},{1... | collective-permute-start | bytes 2408456 | tf_op jit(solution)/shard_map/ppermute | solution.py:21
  116.5 1.7 %fusion.13 = bf16[64,896]{1,0:T(8,128)(2,1)} fusion(bf16[64,896]{1,0:T(8,128)(2,1)} %copy-done.5, bf16[64,896]{1,0:T(8,128)(2,1)S(1)} %copy-done.9, bf16[64,896]{1,0:T(8,128)(2,1)S(1)} %collective-permute-done.2, f32[]{:T(128)S(6)} %sub.24, f32[]{:T(128)S(6)} %sub.23), kind=kLoop, calls=%fused_computation.37 | loop fusion | flops 458752 | bytes 458760 | tf_op jit(solution)/shard_map/convert_element_type | solution.py:111
  118.1 4.5 %collective-permute-start.3 = (bf16[64,896]{1,0:T(8,128)(2,1)}, bf16[64,896]{1,0:T(8,128)(2,1)}, u32[]{:S(2)}, u32[]{:S(2)}) collective-permute-start(bf16[64,896]{1,0:T(8,128)(2,1)} %fusion.13), channel_id=1, source_target_pairs={{0,64},{16,80},{32,96},{48,112},{64,0},{80,16},{96,32},{112,48},{1... | collective-permute-start | bytes 344072 | tf_op jit(solution)/shard_map/ppermute | solution.py:21
  122.7 1.5 convolution_convert_fusion
  124.2 3.5 %collective-permute-start.10 = (bf16[256,896]{1,0:T(8,128)(2,1)S(1)}, bf16[256,896]{1,0:T(8,128)(2,1)S(1)}, u32[]{:S(2)}, u32[]{:S(2)}) collective-permute-start(bf16[256,896]{1,0:T(8,128)(2,1)S(1)} %convolution_convert_fusion), channel_id=1, source_target_pairs={{0,1},{1,0},{2,3},{3,2},{4,5},{5,4},{6,7},{7,6},{8,9},{9,8},{10,11... | collective-permute-start | bytes 1376264 | tf_op jit(solution)/shard_map/ppermute | solution.py:21
  128.8 2.6 %collective-permute-start.4 = (f32[64,896]{1,0:T(8,128)S(1)}, f32[64,896]{1,0:T(8,128)S(1)}, u32[]{:S(2)}, u32[]{:S(2)}) collective-permute-start(f32[64,896]{1,0:T(8,128)S(1)} %multiply_add_fusion.2), channel_id=1, source_target_pairs={{0,32},{16,48},{32,0},{48,16},{64,96},{80,112},{96,64},{112,80},{1... | collective-permute-start | bytes 688136 | tf_op jit(solution)/shard_map/ppermute | solution.py:21
  131.8 4.0 %collective-permute-done.4 = f32[64,896]{1,0:T(8,128)S(1)} collective-permute-done((f32[64,896]{1,0:T(8,128)S(1)}, f32[64,896]{1,0:T(8,128)S(1)}, u32[]{:S(2)}, u32[]{:S(2)}) %collective-permute-start.4) | collective-permute-done | bytes 229408 | tf_op jit(solution)/shard_map/ppermute | solution.py:21
  135.9 9.6 %collective-permute-start.5 = (f32[64,896]{1,0:T(8,128)S(1)}, f32[64,896]{1,0:T(8,128)S(1)}, u32[]{:S(2)}, u32[]{:S(2)}) collective-permute-start(f32[64,896]{1,0:T(8,128)S(1)} %multiply_add_fusion.1), channel_id=1, source_target_pairs={{0,16},{16,0},{32,48},{48,32},{64,80},{80,64},{96,112},{112,96},{1... | collective-permute-start | bytes 688136 | tf_op jit(solution)/shard_map/ppermute | solution.py:21
  146.3 2.4 %fusion.7 = (bf16[256,896]{1,0:T(8,128)(2,1)}, bf16[256,896]{1,0:T(8,128)(2,1)}, bf16[256,896]{1,0:T(8,128)(2,1)}) fusion(bf16[256,896]{1,0:T(8,128)(2,1)S(1)} %copy-done.15, bf16[256,896]{1,0:T(8,128)(2,1)S(1)} %copy-done.16, bf16[896,896]{1,0:T(8,128)(2,1)S(1)} %bitcast.32, f32[256,896]{1,0:T(8,128)S(1)} %fusion.19, ...), kind=kOutput, calls=%fused_computation.18 | convolution fusion | flops 416317440 | bytes 6193152 | tf_op jit(solution)/shard_map/dot_general | solution.py:172
  (68 shorter events, 14.8 us)
Async XLA Ops:
  0.6 26.5 %copy-start.11 = (bf16[1,512,512]{2,1,0:T(8,128)(2,1)S(1)}, bf16[1,512,512]{2,1,0:T(8,128)(2,1)}, u32[]{:S(2)}) copy-start(bf16[1,512,512]{2,1,0:T(8,128)(2,1)} %param.9) | copy-start | bytes 1572868
  2.5 31.9 %all-to-all-start.1 = ((bf16[32,2,896]{2,1,0:T(2,128)(2,1)}), bf16[32,2,896]{2,1,0:T(2,128)(2,1)S(1)}, u32[]{:S(2)}, u32[]{:S(2)}) async-start(bf16[32,2,896]{2,1,0:T(2,128)(2,1)} %reshape.35), calls=%async_computation.1 | async-start | bytes 229376 | tf_op jit(solution)/shard_map/all_to_all | solution.py:16
  22.2 12.3 %copy-start.14 = (bf16[64,64]{1,0:T(8,128)(2,1)S(1)}, bf16[64,64]{1,0:T(8,128)(2,1)}, u32[]{:S(2)}) copy-start(bf16[64,64]{1,0:T(8,128)(2,1)} %constant.79.clone) | copy-start | bytes 24580
  22.5 19.4 %collective-permute-start = (bf16[312,896]{1,0:T(8,128)(2,1)S(1)}, bf16[312,896]{1,0:T(8,128)(2,1)S(1)}, u32[]{:S(2)}, u32[]{:S(2)}) collective-permute-start(bf16[312,896]{1,0:T(8,128)(2,1)S(1)} %shard_map.111), channel_id=1, source_target_pairs={{0,1},{1,0},{2,3},{3,2},{4,5},{5,4},{6,7},{7,6},{8,9},{9,8},{10,11... | collective-permute-start | bytes 1677320 | tf_op jit(solution)/shard_map/ppermute | solution.py:21
  35.3 21.2 %all-to-all-start.2 = ((bf16[32,2,896]{2,1,0:T(2,128)(2,1)}), bf16[32,2,896]{2,1,0:T(2,128)(2,1)S(1)}, u32[]{:S(2)}, u32[]{:S(2)}) async-start(bf16[32,2,896]{2,1,0:T(2,128)(2,1)} %reshape.37), calls=%async_computation.2 | async-start | bytes 229376 | tf_op jit(solution)/shard_map/all_to_all | solution.py:16
  43.3 17.5 %copy-start.4 = (bf16[56,896]{1,0:T(8,128)(2,1)S(1)}, bf16[56,896]{1,0:T(8,128)(2,1)}, u32[]{:S(2)}) copy-start(bf16[56,896]{1,0:T(8,128)(2,1)} %factor.1) | copy-start | bytes 301060
  56.6 20.2 %all-to-all-start = ((bf16[8,64,896]{2,1,0:T(8,128)(2,1)}), bf16[8,64,896]{2,1,0:T(8,128)(2,1)S(1)}, u32[]{:S(2)}, u32[]{:S(2)}) async-start(bf16[8,64,896]{2,1,0:T(8,128)(2,1)} %bitcast.37), calls=%async_computation | async-start | bytes 1835008 | tf_op jit(solution)/shard_map/all_to_all | solution.py:16
  60.8 12.6 %collective-permute-start.6 = (bf16[1,56,896]{2,1,0:T(8,128)(2,1)S(1)}, bf16[1,56,896]{2,1,0:T(8,128)(2,1)S(1)}, u32[]{:S(2)}, u32[]{:S(2)}) collective-permute-start(bf16[1,56,896]{2,1,0:T(8,128)(2,1)S(1)} %fusion.16), channel_id=1, source_target_pairs={{0,2},{2,0},{4,6},{6,4},{8,10},{10,8},{12,14},{14,12},{1,3},{3,1},... | collective-permute-start | bytes 301064 | tf_op jit(solution)/shard_map/ppermute | solution.py:21
  73.5 7.9 %collective-permute-start.7 = (bf16[2,56,896]{2,1,0:T(8,128)(2,1)S(1)}, bf16[2,56,896]{2,1,0:T(8,128)(2,1)S(1)}, u32[]{:S(2)}, u32[]{:S(2)}) collective-permute-start(bf16[2,56,896]{2,1,0:T(8,128)(2,1)S(1)} %pad_maximum_fusion.2), channel_id=1, source_target_pairs={{0,4},{2,6},{4,0},{6,2},{8,12},{10,14},{12,8},{14,10},{1,5},{3,7},... | collective-permute-start | bytes 602120 | tf_op jit(solution)/shard_map/ppermute | solution.py:21
  77.8 44.9 %all-to-all-start.3 = ((bf16[8,64,896]{2,1,0:T(8,128)(2,1)}), bf16[8,64,896]{2,1,0:T(8,128)(2,1)S(1)}, u32[]{:S(2)}, u32[]{:S(2)}) async-start(bf16[8,64,896]{2,1,0:T(8,128)(2,1)} %broadcast_in_dim.20), calls=%async_computation.3 | async-start | bytes 1835008 | tf_op jit(solution)/shard_map/all_to_all | solution.py:16
  82.2 24.5 %collective-permute-start.8 = (bf16[4,56,896]{2,1,0:T(8,128)(2,1)}, bf16[4,56,896]{2,1,0:T(8,128)(2,1)}, u32[]{:S(2)}, u32[]{:S(2)}) collective-permute-start(bf16[4,56,896]{2,1,0:T(8,128)(2,1)} %pad_maximum_fusion.1), channel_id=1, source_target_pairs={{0,8},{2,10},{4,12},{6,14},{8,0},{10,2},{12,4},{14,6},{1,9},{3,11}... | collective-permute-start | bytes 1204232 | tf_op jit(solution)/shard_map/ppermute | solution.py:21
  87.1 19.6 %copy-start.5 = (bf16[64,896]{1,0:T(8,128)(2,1)}, bf16[64,896]{1,0:T(8,128)(2,1)S(1)}, u32[]{:S(2)}) copy-start(bf16[64,896]{1,0:T(8,128)(2,1)S(1)} %reduce_sum.12) | copy-start | bytes 344068
  87.1 14.7 %collective-permute-start.1 = (bf16[64,896]{1,0:T(8,128)(2,1)S(1)}, bf16[64,896]{1,0:T(8,128)(2,1)S(1)}, u32[]{:S(2)}, u32[]{:S(2)}) collective-permute-start(bf16[64,896]{1,0:T(8,128)(2,1)S(1)} %reduce_sum.12), channel_id=1, source_target_pairs={{0,256},{16,272},{32,288},{48,304},{64,320},{80,336},{96,352},{112... | collective-permute-start | bytes 344072 | tf_op jit(solution)/shard_map/ppermute | solution.py:21
  101.9 14.6 %collective-permute-start.2 = (bf16[64,896]{1,0:T(8,128)(2,1)S(1)}, bf16[64,896]{1,0:T(8,128)(2,1)S(1)}, u32[]{:S(2)}, u32[]{:S(2)}) collective-permute-start(bf16[64,896]{1,0:T(8,128)(2,1)S(1)} %fusion.12), channel_id=1, source_target_pairs={{0,128},{16,144},{32,160},{48,176},{64,192},{80,208},{96,224},{112... | collective-permute-start | bytes 344072 | tf_op jit(solution)/shard_map/ppermute | solution.py:21
  106.7 9.7 %copy-start.9 = (bf16[64,896]{1,0:T(8,128)(2,1)S(1)}, bf16[64,896]{1,0:T(8,128)(2,1)}, u32[]{:S(2)}) copy-start(bf16[64,896]{1,0:T(8,128)(2,1)} %copy-done.8) | copy-start | bytes 344068
  107.9 37.6 %collective-permute-start.9 = (bf16[8,56,896]{2,1,0:T(8,128)(2,1)S(1)}, bf16[8,56,896]{2,1,0:T(8,128)(2,1)S(1)}, u32[]{:S(2)}, u32[]{:S(2)}) collective-permute-start(bf16[8,56,896]{2,1,0:T(8,128)(2,1)S(1)} %pad_maximum_fusion.mine), channel_id=1, source_target_pairs={{0,16},{16,0},{32,48},{48,32},{64,80},{80,64},{96,112},{112,96},{1... | collective-permute-start | bytes 2408456 | tf_op jit(solution)/shard_map/ppermute | solution.py:21
  118.1 9.6 %collective-permute-start.3 = (bf16[64,896]{1,0:T(8,128)(2,1)}, bf16[64,896]{1,0:T(8,128)(2,1)}, u32[]{:S(2)}, u32[]{:S(2)}) collective-permute-start(bf16[64,896]{1,0:T(8,128)(2,1)} %fusion.13), channel_id=1, source_target_pairs={{0,64},{16,80},{32,96},{48,112},{64,0},{80,16},{96,32},{112,48},{1... | collective-permute-start | bytes 344072 | tf_op jit(solution)/shard_map/ppermute | solution.py:21
  122.7 8.7 %copy-start.7 = (bf16[256,512]{0,1:T(8,128)(2,1)S(1)}, bf16[256,512]{0,1:T(8,128)(2,1)}, u32[]{:S(2)}) copy-start(bf16[256,512]{0,1:T(8,128)(2,1)} %get-tuple-element.10) | copy-start | bytes 786436
  124.2 22.0 %collective-permute-start.10 = (bf16[256,896]{1,0:T(8,128)(2,1)S(1)}, bf16[256,896]{1,0:T(8,128)(2,1)S(1)}, u32[]{:S(2)}, u32[]{:S(2)}) collective-permute-start(bf16[256,896]{1,0:T(8,128)(2,1)S(1)} %convolution_convert_fusion), channel_id=1, source_target_pairs={{0,1},{1,0},{2,3},{3,2},{4,5},{5,4},{6,7},{7,6},{8,9},{9,8},{10,11... | collective-permute-start | bytes 1376264 | tf_op jit(solution)/shard_map/ppermute | solution.py:21
  128.8 7.1 %collective-permute-start.4 = (f32[64,896]{1,0:T(8,128)S(1)}, f32[64,896]{1,0:T(8,128)S(1)}, u32[]{:S(2)}, u32[]{:S(2)}) collective-permute-start(f32[64,896]{1,0:T(8,128)S(1)} %multiply_add_fusion.2), channel_id=1, source_target_pairs={{0,32},{16,48},{32,0},{48,16},{64,96},{80,112},{96,64},{112,80},{1... | collective-permute-start | bytes 688136 | tf_op jit(solution)/shard_map/ppermute | solution.py:21
  135.9 10.4 %copy-start.2 = (s32[256,896]{1,0:T(8,128)S(1)}, s32[256,896]{1,0:T(8,128)}, u32[]{:S(2)}) copy-start(s32[256,896]{1,0:T(8,128)} %codes.1) | copy-start | bytes 2752516
  135.9 10.4 %copy-start.15 = (bf16[256,896]{1,0:T(8,128)(2,1)S(1)}, bf16[256,896]{1,0:T(8,128)(2,1)}, u32[]{:S(2)}) copy-start(bf16[256,896]{1,0:T(8,128)(2,1)} %param.14) | copy-start | bytes 1376260
  135.9 10.4 %copy-start.16 = (bf16[256,896]{1,0:T(8,128)(2,1)S(1)}, bf16[256,896]{1,0:T(8,128)(2,1)}, u32[]{:S(2)}) copy-start(bf16[256,896]{1,0:T(8,128)(2,1)} %param.13) | copy-start | bytes 1376260
  135.9 12.7 %collective-permute-start.5 = (f32[64,896]{1,0:T(8,128)S(1)}, f32[64,896]{1,0:T(8,128)S(1)}, u32[]{:S(2)}, u32[]{:S(2)}) collective-permute-start(f32[64,896]{1,0:T(8,128)S(1)} %multiply_add_fusion.1), channel_id=1, source_target_pairs={{0,16},{16,0},{32,48},{48,32},{64,80},{80,64},{96,112},{112,96},{1... | collective-permute-start | bytes 688136 | tf_op jit(solution)/shard_map/ppermute | solution.py:21
  (8 other events, 25.1 us)

commit v7 on v5

--- a/solution.py
+++ b/solution.py
@@ -12,13 +12,19 @@
 GROUP = 128
 
 
-def trade(block, axis):
-    return lax.all_to_all(block, axis, split_axis=0, concat_axis=0, tiled=True)
+def trade(block, axis, order=None):
+    groups = None if order is None else [order]
+    return lax.all_to_all(
+        block, axis, split_axis=0, concat_axis=0, tiled=True, axis_index_groups=groups
+    )
 
 
 def partner(block, axis, bit):
     count = lax.axis_size(axis)
     return lax.ppermute(block, axis, [(s, s ^ bit) for s in range(count)])
+
+
+KERNEL_VMEM = pltpu.CompilerParams(vmem_limit_bytes=8 * 1024 * 1024)
 
 
 def order_kernel(place, mine, other, out):
@@ -45,28 +51,28 @@
         out_shape=jax.ShapeDtypeStruct((count, 2, rows, width), mine.dtype),
         in_specs=[pl.BlockSpec(memory_space=pltpu.SMEM), whole, whole],
         out_specs=whole,
+        compiler_params=KERNEL_VMEM,
         cost_estimate=pl.CostEstimate(
             flops=0, bytes_accessed=8 * count * rows * width, transcendentals=0
         ),
     )(jnp.stack([spot, core]), mine, other)
 
 
-def sign_rows(count, inner):
-    index = np.arange(count * inner)
-    upper, lower = index // inner, index % inner
+def sign_rows(order, inner):
+    upper = np.repeat(np.array(order), inner)
+    lower = np.arange(upper.size) % inner
     both = upper[:, None] & upper[None, :]
     parity = np.zeros_like(both)
-    for bit in range(count.bit_length()):
+    for bit in range(len(order).bit_length()):
         parity ^= both >> bit & 1
     same = lower[:, None] == lower[None, :]
     return ((1 - 2 * parity) * same).astype(np.float32)
 
 
-def gather_factor(local_factor):
+def gather_factor(local_factor, other):
     core, spot = lax.axis_index("hid") % 2, lax.axis_index("out")
     _, width = local_factor.shape
     bits = lax.axis_size("out").bit_length() - 1
-    other = partner(local_factor, "rep", 1)
     block = jnp.where(core == lax.axis_index("rep"), local_factor, other)[None]
     for bit in range(bits):
         other = partner(block, "out", 1 << bit)
@@ -79,7 +85,9 @@
     where = lax.axis_index("hid")
     count = lax.axis_size("hid")
     total = block
-    for bit in reversed(range(count.bit_length() - 1)):
+    bits = count.bit_length() - 1
+    turns = [*range(bits - 2, 1, -1), bits - 1, *range(min(bits - 1, 2) - 1, -1, -1)]
+    for bit in turns:
         sent = total if bit < 2 else total.astype(jnp.bfloat16)
         other = partner(sent, "hid", 1 << bit).astype(jnp.float32)
         sign = 1.0 - 2.0 * (where >> bit & 1).astype(jnp.float32)
@@ -95,18 +103,21 @@
     few = mine // hid_count
     code_rows = weight_codes.shape[0]
     grads_out = out_grad[0]
-    signs = sign_rows(hid_count, few)
+    order = [index ^ hid_count // 2 for index in range(hid_count)]
+    signs = sign_rows(order, few)
     root = math.sqrt(hid_count)
 
     tokens = lax.dynamic_slice_in_dim(x_act[0], out_index * mine, mine, axis=0)
-    rows = trade(tokens.reshape(hid_count, few, width), "hid").reshape(mine, width)
+    rows = trade(tokens.reshape(hid_count, few, width), "hid", order).reshape(mine, width)
 
     scales = jnp.exp2(group_exps.astype(jnp.float32)).astype(jnp.bfloat16)
     lanes = np.repeat(np.eye(width // GROUP, dtype=np.float32), GROUP, axis=1)
     scales = jnp.dot(scales, lanes.astype(jnp.bfloat16), preferred_element_type=jnp.float32)
     w_deq = (weight_codes.astype(jnp.float32) * scales).astype(jnp.bfloat16)
-    w_other = partner(w_deq, "rep", 1)
-    factor = gather_factor(local_factor)
+    sent = jnp.concatenate([w_deq, local_factor], axis=0)
+    arrived = partner(sent, "rep", 1)
+    w_other = arrived[:code_rows]
+    factor = gather_factor(local_factor, arrived[code_rows:])
 
     grads_t = grads_out.T
     g_own = lax.dynamic_slice_in_dim(grads_out, rep_index * code_rows, code_rows, axis=1)
@@ -125,7 +136,7 @@
 
     mixed = jnp.dot(signs.astype(jnp.bfloat16), rows, preferred_element_type=jnp.float32)
     mixed = (mixed / root).astype(jnp.bfloat16).reshape(hid_count, few, width)
-    mixed = trade(mixed, "hid").reshape(mine, width)
+    mixed = trade(mixed, "hid", order).reshape(mine, width)
     mixed = jnp.broadcast_to(mixed[None], (out_count, mine, width))
     mixed = trade(mixed, "out").reshape(token_count, width)
 

time: 162 us -> 151 us (0.932)
  waiting for transfers between devices: 58.6 us -> 40 us
  starting transfers between devices: 81.4 us -> 88.3 us
  Pallas kernels: 2.81 us -> 0.72 us
    ppermute x12 -> x11, waiting for transfers between devices: 46.9 us -> 35.5 us  [partner(): return lax.ppermute(block, axis, [(s, s ^ bit) for s in range(count)])]
    all_to_all x4, waiting for transfers between devices: 11.6 us -> 4.5 us  [trade(): lax.all_to_all(block, axis, split_axis=0, concat_axis=0, tiled=True, axis...]
    all_to_all x4, starting transfers between devices: 34 us -> 40.9 us  [trade(): lax.all_to_all(block, axis, split_axis=0, concat_axis=0, tiled=True, axis...]
    pallas_call x1, Pallas kernels: 2.81 us -> 0.72 us  [in_order(): pl.pallas_call(order_kernel, out_shape=jax.ShapeDtypeStruct((count, 2, ro...]
    concatenate x3, other arithmetic: 0.18 us -> 1.96 us  [gather_factor(): block = jnp.concatenate([block, other], axis=0)]
    ppermute x12 -> x11, starting transfers between devices: 47.5 us -> 47.3 us  [partner(): return lax.ppermute(block, axis, [(s, s ^ bit) for s in range(count)])]
  transfers between devices with their start and end apart: 16 -> 15, of which waited for: 9 -> 6; matrix products, arithmetic and copies ran while one was open for 9% -> 11% of each run, Pallas kernels for 2% -> 0%
where the time goes in v7:
time: 151 us; the launch traced here: 150 us
  starting transfers between devices  88.3 us (58%)
  waiting for transfers between devices  40 us (26%)
  matrix products  9.72 us (6%)
  local copies, waits for them, and re-layouts  5.67 us (4%)
  other arithmetic  4.93 us (3%)
    ppermute x11, starting transfers between devices, partner(): return lax.ppermute(block, axis, [(s, s ^ bit) for s in range(count)])  47.3 us
    all_to_all x4, starting transfers between devices, trade(): lax.all_to_all(block, axis, split_axis=0, concat_axis=0, tiled=True, axis...  40.9 us
    ppermute x11, waiting for transfers between devices, partner(): return lax.ppermute(block, axis, [(s, s ^ bit) for s in range(count)])  35.5 us
    all_to_all x4, waiting for transfers between devices, trade(): lax.all_to_all(block, axis, split_axis=0, concat_axis=0, tiled=True, axis...  4.5 us
  transfers between devices with their start and end apart: 15, of which 6 were waited for; matrix products, arithmetic and copies ran while one was open for 11% of the time, Pallas kernels for 0%

profile of v7, /device:TPU:1, one launch (start us, length us, event | category | flops | bytes accessed | tf_op | source)
XLA Modules:
  0.0 150.4 jit_solution(8903761109899670928)
XLA Ops:
  2.5 20.1 %all-to-all-start.1 = ((bf16[32,2,896]{2,1,0:T(2,128)(2,1)}), bf16[32,2,896]{2,1,0:T(2,128)(2,1)S(1)}, u32[]{:S(2)}, u32[]{:S(2)}) async-start(bf16[32,2,896]{2,1,0:T(2,128)(2,1)} %reshape.35), calls=%async_computation.1 | async-start | bytes 229376 | tf_op jit(solution)/shard_map/all_to_all | solution.py:17
  24.3 4.7 %collective-permute-start = (bf16[312,896]{1,0:T(8,128)(2,1)S(1)}, bf16[312,896]{1,0:T(8,128)(2,1)S(1)}, u32[]{:S(2)}, u32[]{:S(2)}) collective-permute-start(bf16[312,896]{1,0:T(8,128)(2,1)S(1)} %pad_maximum_fusion.1), channel_id=1, source_target_pairs={{0,1},{1,0},{2,3},{3,2},{4,5},{5,4},{6,7},{7,6},{8,9},{9,8},{10,11... | collective-permute-start | bytes 1677320 | tf_op jit(solution)/shard_map/ppermute | solution.py:24
  28.9 1.9 %dynamic-slice_bitcast_fusion = (bf16[256,512]{0,1:T(8,128)(2,1)}, bf16[256,512]{0,1:T(8,128)(2,1)}, bf16[512,256]{1,0:T(8,128)(2,1)S(1)}, bf16[512,256]{1,0:T(8,128)(2,1)S(1)}) fusion(bf16[1,512,512]{2,1,0:T(8,128)(2,1)} %param.10, s32[]{:T(128)S(6)} %select_n.31, s32[]{:T(128)S(6)} %select_n.30), kind=kLoop, calls=%fused_computation.26 | loop fusion | bytes 1572872 | tf_op jit(solution)/shard_map/dynamic_slice | solution.py:126
  31.8 12.5 %all-to-all-start.2 = ((bf16[32,2,896]{2,1,0:T(2,128)(2,1)}), bf16[32,2,896]{2,1,0:T(2,128)(2,1)S(1)}, u32[]{:S(2)}, u32[]{:S(2)}) async-start(bf16[32,2,896]{2,1,0:T(2,128)(2,1)} %reshape.37), calls=%async_computation.2 | async-start | bytes 229376 | tf_op jit(solution)/shard_map/all_to_all | solution.py:17
  46.0 4.5 %all-to-all-done.2 = bf16[32,2,896]{2,1,0:T(2,128)(2,1)S(1)} async-done(((bf16[32,2,896]{2,1,0:T(2,128)(2,1)}), bf16[32,2,896]{2,1,0:T(2,128)(2,1)S(1)}, u32[]{:S(2)}, u32[]{:S(2)}) %all-to-all-start.2) | async-done | bytes 114720 | tf_op jit(solution)/shard_map/all_to_all | solution.py:17
  50.5 4.7 %all-to-all-start = ((bf16[8,64,896]{2,1,0:T(8,128)(2,1)}), bf16[8,64,896]{2,1,0:T(8,128)(2,1)S(1)}, u32[]{:S(2)}, u32[]{:S(2)}) async-start(bf16[8,64,896]{2,1,0:T(8,128)(2,1)} %bitcast.4), calls=%async_computation | async-start | bytes 1835008 | tf_op jit(solution)/shard_map/all_to_all | solution.py:17
  55.3 3.4 %collective-permute-start.6 = (bf16[1,56,896]{2,1,0:T(8,128)(2,1)S(1)}, bf16[1,56,896]{2,1,0:T(8,128)(2,1)S(1)}, u32[]{:S(2)}, u32[]{:S(2)}) collective-permute-start(bf16[1,56,896]{2,1,0:T(8,128)(2,1)S(1)} %fusion.15), channel_id=1, source_target_pairs={{0,2},{2,0},{4,6},{6,4},{8,10},{10,8},{12,14},{14,12},{1,3},{3,1},... | collective-permute-start | bytes 301064 | tf_op jit(solution)/shard_map/ppermute | solution.py:24
  58.6 10.4 %collective-permute-done.6 = bf16[1,56,896]{2,1,0:T(8,128)(2,1)S(1)} collective-permute-done((bf16[1,56,896]{2,1,0:T(8,128)(2,1)S(1)}, bf16[1,56,896]{2,1,0:T(8,128)(2,1)S(1)}, u32[]{:S(2)}, u32[]{:S(2)}) %collective-permute-start.6) | collective-permute-done | bytes 100384 | tf_op jit(solution)/shard_map/ppermute | solution.py:24
  69.0 3.1 %collective-permute-start.7 = (bf16[2,56,896]{2,1,0:T(8,128)(2,1)S(1)}, bf16[2,56,896]{2,1,0:T(8,128)(2,1)S(1)}, u32[]{:S(2)}, u32[]{:S(2)}) collective-permute-start(bf16[2,56,896]{2,1,0:T(8,128)(2,1)S(1)} %pad_maximum_fusion.3), channel_id=1, source_target_pairs={{0,4},{2,6},{4,0},{6,2},{8,12},{10,14},{12,8},{14,10},{1,5},{3,7},... | collective-permute-start | bytes 602120 | tf_op jit(solution)/shard_map/ppermute | solution.py:24
  73.3 3.7 %all-to-all-start.3 = ((bf16[8,64,896]{2,1,0:T(8,128)(2,1)}), bf16[8,64,896]{2,1,0:T(8,128)(2,1)S(1)}, u32[]{:S(2)}, u32[]{:S(2)}) async-start(bf16[8,64,896]{2,1,0:T(8,128)(2,1)} %broadcast_in_dim.20), calls=%async_computation.3 | async-start | bytes 1835008 | tf_op jit(solution)/shard_map/all_to_all | solution.py:17
  77.8 4.9 %collective-permute-start.8 = (bf16[4,56,896]{2,1,0:T(8,128)(2,1)}, bf16[4,56,896]{2,1,0:T(8,128)(2,1)}, u32[]{:S(2)}, u32[]{:S(2)}) collective-permute-start(bf16[4,56,896]{2,1,0:T(8,128)(2,1)} %pad_maximum_fusion.2), channel_id=1, source_target_pairs={{0,8},{2,10},{4,12},{6,14},{8,0},{10,2},{12,4},{14,6},{1,9},{3,11}... | collective-permute-start | bytes 1204232 | tf_op jit(solution)/shard_map/ppermute | solution.py:24
  82.8 6.7 %collective-permute-start.1 = (bf16[64,896]{1,0:T(8,128)(2,1)S(1)}, bf16[64,896]{1,0:T(8,128)(2,1)S(1)}, u32[]{:S(2)}, u32[]{:S(2)}) collective-permute-start(bf16[64,896]{1,0:T(8,128)(2,1)S(1)} %reduce_sum.12), channel_id=1, source_target_pairs={{0,128},{16,144},{32,160},{48,176},{64,192},{80,208},{96,224},{112... | collective-permute-start | bytes 344072 | tf_op jit(solution)/shard_map/ppermute | solution.py:24
  89.6 10.5 %collective-permute-done.1 = bf16[64,896]{1,0:T(8,128)(2,1)S(1)} collective-permute-done((bf16[64,896]{1,0:T(8,128)(2,1)S(1)}, bf16[64,896]{1,0:T(8,128)(2,1)S(1)}, u32[]{:S(2)}, u32[]{:S(2)}) %collective-permute-start.1) | collective-permute-done | bytes 114720 | tf_op jit(solution)/shard_map/ppermute | solution.py:24
  100.1 1.9 %collective-permute-start.2 = (bf16[64,896]{1,0:T(8,128)(2,1)S(1)}, bf16[64,896]{1,0:T(8,128)(2,1)S(1)}, u32[]{:S(2)}, u32[]{:S(2)}) collective-permute-start(bf16[64,896]{1,0:T(8,128)(2,1)S(1)} %fusion.11), channel_id=1, source_target_pairs={{0,64},{16,80},{32,96},{48,112},{64,0},{80,16},{96,32},{112,48},{1... | collective-permute-start | bytes 344072 | tf_op jit(solution)/shard_map/ppermute | solution.py:24
  103.2 3.4 %collective-permute-start.9 = (bf16[8,56,896]{2,1,0:T(8,128)(2,1)S(1)}, bf16[8,56,896]{2,1,0:T(8,128)(2,1)S(1)}, u32[]{:S(2)}, u32[]{:S(2)}) collective-permute-start(bf16[8,56,896]{2,1,0:T(8,128)(2,1)S(1)} %pad_maximum_fusion.mine), channel_id=1, source_target_pairs={{0,16},{16,0},{32,48},{48,32},{64,80},{80,64},{96,112},{112,96},{1... | collective-permute-start | bytes 2408456 | tf_op jit(solution)/shard_map/ppermute | solution.py:24
  106.6 2.4 %collective-permute-done.2 = bf16[64,896]{1,0:T(8,128)(2,1)S(1)} collective-permute-done((bf16[64,896]{1,0:T(8,128)(2,1)S(1)}, bf16[64,896]{1,0:T(8,128)(2,1)S(1)}, u32[]{:S(2)}, u32[]{:S(2)}) %collective-permute-start.2) | collective-permute-done | bytes 114720 | tf_op jit(solution)/shard_map/ppermute | solution.py:24
  109.0 1.6 %fusion.12 = bf16[64,896]{1,0:T(8,128)(2,1)} fusion(bf16[64,896]{1,0:T(8,128)(2,1)} %copy-done.1, bf16[64,896]{1,0:T(8,128)(2,1)S(1)} %copy-done.5, bf16[64,896]{1,0:T(8,128)(2,1)S(1)} %collective-permute-done.2, f32[]{:T(128)S(6)} %sub.24, f32[]{:T(128)S(6)} %sub.23), kind=kLoop, calls=%fused_computation.38 | loop fusion | flops 458752 | bytes 458760 | tf_op jit(solution)/shard_map/convert_element_type | solution.py:91
  110.6 9.6 %collective-permute-start.3 = (bf16[64,896]{1,0:T(8,128)(2,1)}, bf16[64,896]{1,0:T(8,128)(2,1)}, u32[]{:S(2)}, u32[]{:S(2)}) collective-permute-start(bf16[64,896]{1,0:T(8,128)(2,1)} %fusion.12), channel_id=1, source_target_pairs={{0,256},{16,272},{32,288},{48,304},{64,320},{80,336},{96,352},{112... | collective-permute-start | bytes 344072 | tf_op jit(solution)/shard_map/ppermute | solution.py:24
  121.8 4.4 %collective-permute-start.10 = (bf16[256,896]{1,0:T(8,128)(2,1)S(1)}, bf16[256,896]{1,0:T(8,128)(2,1)S(1)}, u32[]{:S(2)}, u32[]{:S(2)}) collective-permute-start(bf16[256,896]{1,0:T(8,128)(2,1)S(1)} %convolution_convert_fusion), channel_id=1, source_target_pairs={{0,1},{1,0},{2,3},{3,2},{4,5},{5,4},{6,7},{7,6},{8,9},{9,8},{10,11... | collective-permute-start | bytes 1376264 | tf_op jit(solution)/shard_map/ppermute | solution.py:24
  126.2 6.2 %collective-permute-done.3 = bf16[64,896]{1,0:T(8,128)(2,1)} collective-permute-done((bf16[64,896]{1,0:T(8,128)(2,1)}, bf16[64,896]{1,0:T(8,128)(2,1)}, u32[]{:S(2)}, u32[]{:S(2)}) %collective-permute-start.3) | collective-permute-done | bytes 114720 | tf_op jit(solution)/shard_map/ppermute | solution.py:24
  133.4 1.9 %collective-permute-start.4 = (f32[64,896]{1,0:T(8,128)S(1)}, f32[64,896]{1,0:T(8,128)S(1)}, u32[]{:S(2)}, u32[]{:S(2)}) collective-permute-start(f32[64,896]{1,0:T(8,128)S(1)} %multiply_add_fusion.2), channel_id=1, source_target_pairs={{0,32},{16,48},{32,0},{48,16},{64,96},{80,112},{96,64},{112,80},{1... | collective-permute-start | bytes 688136 | tf_op jit(solution)/shard_map/ppermute | solution.py:24
  135.8 6.1 %collective-permute-done.4 = f32[64,896]{1,0:T(8,128)S(1)} collective-permute-done((f32[64,896]{1,0:T(8,128)S(1)}, f32[64,896]{1,0:T(8,128)S(1)}, u32[]{:S(2)}, u32[]{:S(2)}) %collective-permute-start.4) | collective-permute-done | bytes 229408 | tf_op jit(solution)/shard_map/ppermute | solution.py:24
  141.9 3.5 %collective-permute-start.5 = (f32[64,896]{1,0:T(8,128)S(1)}, f32[64,896]{1,0:T(8,128)S(1)}, u32[]{:S(2)}, u32[]{:S(2)}) collective-permute-start(f32[64,896]{1,0:T(8,128)S(1)} %multiply_add_fusion.1), channel_id=1, source_target_pairs={{0,16},{16,0},{32,48},{48,32},{64,80},{80,64},{96,112},{112,96},{1... | collective-permute-start | bytes 688136 | tf_op jit(solution)/shard_map/ppermute | solution.py:24
  146.2 2.4 %fusion.8 = (bf16[256,896]{1,0:T(8,128)(2,1)}, bf16[256,896]{1,0:T(8,128)(2,1)}, bf16[256,896]{1,0:T(8,128)(2,1)}) fusion(bf16[256,896]{1,0:T(8,128)(2,1)S(1)} %copy-done.13, bf16[256,896]{1,0:T(8,128)(2,1)S(1)} %copy-done.14, bf16[896,896]{1,0:T(8,128)(2,1)S(1)} %bitcast.34, f32[256,896]{1,0:T(8,128)S(1)} %fusion.21, ...), kind=kOutput, calls=%fused_computation.21 | convolution fusion | flops 416317440 | bytes 6193152 | tf_op jit(solution)/shard_map/dot_general | solution.py:157
  (64 shorter events, 15.2 us)
Async XLA Ops:
  0.6 23.5 %copy-start.10 = (bf16[56,896]{1,0:T(8,128)(2,1)S(1)}, bf16[56,896]{1,0:T(8,128)(2,1)}, u32[]{:S(2)}) copy-start(bf16[56,896]{1,0:T(8,128)(2,1)} %param.13) | copy-start | bytes 301060
  2.5 28.3 %all-to-all-start.1 = ((bf16[32,2,896]{2,1,0:T(2,128)(2,1)}), bf16[32,2,896]{2,1,0:T(2,128)(2,1)S(1)}, u32[]{:S(2)}, u32[]{:S(2)}) async-start(bf16[32,2,896]{2,1,0:T(2,128)(2,1)} %reshape.35), calls=%async_computation.1 | async-start | bytes 229376 | tf_op jit(solution)/shard_map/all_to_all | solution.py:17
  24.2 6.7 %copy-start.12 = (bf16[64,64]{1,0:T(8,128)(2,1)S(1)}, bf16[64,64]{1,0:T(8,128)(2,1)}, u32[]{:S(2)}) copy-start(bf16[64,64]{1,0:T(8,128)(2,1)} %constant.84.clone) | copy-start | bytes 24580
  24.3 20.4 %collective-permute-start = (bf16[312,896]{1,0:T(8,128)(2,1)S(1)}, bf16[312,896]{1,0:T(8,128)(2,1)S(1)}, u32[]{:S(2)}, u32[]{:S(2)}) collective-permute-start(bf16[312,896]{1,0:T(8,128)(2,1)S(1)} %pad_maximum_fusion.1), channel_id=1, source_target_pairs={{0,1},{1,0},{2,3},{3,2},{4,5},{5,4},{6,7},{7,6},{8,9},{9,8},{10,11... | collective-permute-start | bytes 1677320 | tf_op jit(solution)/shard_map/ppermute | solution.py:24
  31.8 18.8 %all-to-all-start.2 = ((bf16[32,2,896]{2,1,0:T(2,128)(2,1)}), bf16[32,2,896]{2,1,0:T(2,128)(2,1)S(1)}, u32[]{:S(2)}, u32[]{:S(2)}) async-start(bf16[32,2,896]{2,1,0:T(2,128)(2,1)} %reshape.37), calls=%async_computation.2 | async-start | bytes 229376 | tf_op jit(solution)/shard_map/all_to_all | solution.py:17
  46.0 9.2 %copy-start.11 = (bf16[56,896]{1,0:T(8,128)(2,1)S(1)}, bf16[56,896]{1,0:T(8,128)(2,1)}, u32[]{:S(2)}) copy-start(bf16[56,896]{1,0:T(8,128)(2,1)} %param.13) | copy-start | bytes 301060
  50.5 21.7 %all-to-all-start = ((bf16[8,64,896]{2,1,0:T(8,128)(2,1)}), bf16[8,64,896]{2,1,0:T(8,128)(2,1)S(1)}, u32[]{:S(2)}, u32[]{:S(2)}) async-start(bf16[8,64,896]{2,1,0:T(8,128)(2,1)} %bitcast.4), calls=%async_computation | async-start | bytes 1835008 | tf_op jit(solution)/shard_map/all_to_all | solution.py:17
  55.3 13.7 %collective-permute-start.6 = (bf16[1,56,896]{2,1,0:T(8,128)(2,1)S(1)}, bf16[1,56,896]{2,1,0:T(8,128)(2,1)S(1)}, u32[]{:S(2)}, u32[]{:S(2)}) collective-permute-start(bf16[1,56,896]{2,1,0:T(8,128)(2,1)S(1)} %fusion.15), channel_id=1, source_target_pairs={{0,2},{2,0},{4,6},{6,4},{8,10},{10,8},{12,14},{14,12},{1,3},{3,1},... | collective-permute-start | bytes 301064 | tf_op jit(solution)/shard_map/ppermute | solution.py:24
  69.0 7.9 %collective-permute-start.7 = (bf16[2,56,896]{2,1,0:T(8,128)(2,1)S(1)}, bf16[2,56,896]{2,1,0:T(8,128)(2,1)S(1)}, u32[]{:S(2)}, u32[]{:S(2)}) collective-permute-start(bf16[2,56,896]{2,1,0:T(8,128)(2,1)S(1)} %pad_maximum_fusion.3), channel_id=1, source_target_pairs={{0,4},{2,6},{4,0},{6,2},{8,12},{10,14},{12,8},{14,10},{1,5},{3,7},... | collective-permute-start | bytes 602120 | tf_op jit(solution)/shard_map/ppermute | solution.py:24
  73.3 47.0 %all-to-all-start.3 = ((bf16[8,64,896]{2,1,0:T(8,128)(2,1)}), bf16[8,64,896]{2,1,0:T(8,128)(2,1)S(1)}, u32[]{:S(2)}, u32[]{:S(2)}) async-start(bf16[8,64,896]{2,1,0:T(8,128)(2,1)} %broadcast_in_dim.20), calls=%async_computation.3 | async-start | bytes 1835008 | tf_op jit(solution)/shard_map/all_to_all | solution.py:17
  77.8 24.3 %collective-permute-start.8 = (bf16[4,56,896]{2,1,0:T(8,128)(2,1)}, bf16[4,56,896]{2,1,0:T(8,128)(2,1)}, u32[]{:S(2)}, u32[]{:S(2)}) collective-permute-start(bf16[4,56,896]{2,1,0:T(8,128)(2,1)} %pad_maximum_fusion.2), channel_id=1, source_target_pairs={{0,8},{2,10},{4,12},{6,14},{8,0},{10,2},{12,4},{14,6},{1,9},{3,11}... | collective-permute-start | bytes 1204232 | tf_op jit(solution)/shard_map/ppermute | solution.py:24
  82.8 19.3 %copy-start.1 = (bf16[64,896]{1,0:T(8,128)(2,1)}, bf16[64,896]{1,0:T(8,128)(2,1)S(1)}, u32[]{:S(2)}) copy-start(bf16[64,896]{1,0:T(8,128)(2,1)S(1)} %reduce_sum.12) | copy-start | bytes 344068
  82.8 17.3 %collective-permute-start.1 = (bf16[64,896]{1,0:T(8,128)(2,1)S(1)}, bf16[64,896]{1,0:T(8,128)(2,1)S(1)}, u32[]{:S(2)}, u32[]{:S(2)}) collective-permute-start(bf16[64,896]{1,0:T(8,128)(2,1)S(1)} %reduce_sum.12), channel_id=1, source_target_pairs={{0,128},{16,144},{32,160},{48,176},{64,192},{80,208},{96,224},{112... | collective-permute-start | bytes 344072 | tf_op jit(solution)/shard_map/ppermute | solution.py:24
  100.1 8.9 %collective-permute-start.2 = (bf16[64,896]{1,0:T(8,128)(2,1)S(1)}, bf16[64,896]{1,0:T(8,128)(2,1)S(1)}, u32[]{:S(2)}, u32[]{:S(2)}) collective-permute-start(bf16[64,896]{1,0:T(8,128)(2,1)S(1)} %fusion.11), channel_id=1, source_target_pairs={{0,64},{16,80},{32,96},{48,112},{64,0},{80,16},{96,32},{112,48},{1... | collective-permute-start | bytes 344072 | tf_op jit(solution)/shard_map/ppermute | solution.py:24
  102.1 6.9 %copy-start.5 = (bf16[64,896]{1,0:T(8,128)(2,1)S(1)}, bf16[64,896]{1,0:T(8,128)(2,1)}, u32[]{:S(2)}) copy-start(bf16[64,896]{1,0:T(8,128)(2,1)} %copy-done.4) | copy-start | bytes 344068
  103.2 42.2 %collective-permute-start.9 = (bf16[8,56,896]{2,1,0:T(8,128)(2,1)S(1)}, bf16[8,56,896]{2,1,0:T(8,128)(2,1)S(1)}, u32[]{:S(2)}, u32[]{:S(2)}) collective-permute-start(bf16[8,56,896]{2,1,0:T(8,128)(2,1)S(1)} %pad_maximum_fusion.mine), channel_id=1, source_target_pairs={{0,16},{16,0},{32,48},{48,32},{64,80},{80,64},{96,112},{112,96},{1... | collective-permute-start | bytes 2408456 | tf_op jit(solution)/shard_map/ppermute | solution.py:24
  110.6 21.7 %collective-permute-start.3 = (bf16[64,896]{1,0:T(8,128)(2,1)}, bf16[64,896]{1,0:T(8,128)(2,1)}, u32[]{:S(2)}, u32[]{:S(2)}) collective-permute-start(bf16[64,896]{1,0:T(8,128)(2,1)} %fusion.12), channel_id=1, source_target_pairs={{0,256},{16,272},{32,288},{48,304},{64,320},{80,336},{96,352},{112... | collective-permute-start | bytes 344072 | tf_op jit(solution)/shard_map/ppermute | solution.py:24
  120.3 12.1 %copy-start.2 = (bf16[64,896]{1,0:T(8,128)(2,1)S(1)}, bf16[64,896]{1,0:T(8,128)(2,1)}, u32[]{:S(2)}) copy-start(bf16[64,896]{1,0:T(8,128)(2,1)} %copy-done.1) | copy-start | bytes 344068
  120.3 12.1 %copy-start.6 = (bf16[64,896]{1,0:T(8,128)(2,1)S(1)}, bf16[64,896]{1,0:T(8,128)(2,1)}, u32[]{:S(2)}) copy-start(bf16[64,896]{1,0:T(8,128)(2,1)} %copy-done.4) | copy-start | bytes 344068
  120.3 12.1 %copy-start.9 = (bf16[64,896]{1,0:T(8,128)(2,1)S(1)}, bf16[64,896]{1,0:T(8,128)(2,1)}, u32[]{:S(2)}) copy-start(bf16[64,896]{1,0:T(8,128)(2,1)} %copy-done.8) | copy-start | bytes 344068
  120.3 15.0 %copy-start.3 = (bf16[256,512]{0,1:T(8,128)(2,1)S(1)}, bf16[256,512]{0,1:T(8,128)(2,1)}, u32[]{:S(2)}) copy-start(bf16[256,512]{0,1:T(8,128)(2,1)} %get-tuple-element.10) | copy-start | bytes 786436
  121.8 24.3 %collective-permute-start.10 = (bf16[256,896]{1,0:T(8,128)(2,1)S(1)}, bf16[256,896]{1,0:T(8,128)(2,1)S(1)}, u32[]{:S(2)}, u32[]{:S(2)}) collective-permute-start(bf16[256,896]{1,0:T(8,128)(2,1)S(1)} %convolution_convert_fusion), channel_id=1, source_target_pairs={{0,1},{1,0},{2,3},{3,2},{4,5},{5,4},{6,7},{7,6},{8,9},{9,8},{10,11... | collective-permute-start | bytes 1376264 | tf_op jit(solution)/shard_map/ppermute | solution.py:24
  133.4 8.5 %collective-permute-start.4 = (f32[64,896]{1,0:T(8,128)S(1)}, f32[64,896]{1,0:T(8,128)S(1)}, u32[]{:S(2)}, u32[]{:S(2)}) collective-permute-start(f32[64,896]{1,0:T(8,128)S(1)} %multiply_add_fusion.2), channel_id=1, source_target_pairs={{0,32},{16,48},{32,0},{48,16},{64,96},{80,112},{96,64},{112,80},{1... | collective-permute-start | bytes 688136 | tf_op jit(solution)/shard_map/ppermute | solution.py:24
  141.9 6.6 %collective-permute-start.5 = (f32[64,896]{1,0:T(8,128)S(1)}, f32[64,896]{1,0:T(8,128)S(1)}, u32[]{:S(2)}, u32[]{:S(2)}) collective-permute-start(f32[64,896]{1,0:T(8,128)S(1)} %multiply_add_fusion.1), channel_id=1, source_target_pairs={{0,16},{16,0},{32,48},{48,32},{64,80},{80,64},{96,112},{112,96},{1... | collective-permute-start | bytes 688136 | tf_op jit(solution)/shard_map/ppermute | solution.py:24
  (6 other events, 17.6 us)
